TPU v7x, 128 devices: a whole 4x4x4 slice. The times are simulated.
128 devices in a mesh: grp: 2 (over core), blk: 64 (over x, y, z).
Axes of the slice: x: 4, y: 4, z: 4, core: 2. Of those that a mesh axis runs over, the one named last changes fastest.
Arguments:
- columns: float32 [2, 64, 1048576], P('grp', None, 'blk'), may hold values from -6 to 6
- operators: float32 [2, 64, 64], P('grp'), may hold values from -1 to 1, as said below
- normal_weights: float32 [2, 64], replicated, may hold values from -0.75 to 0.75
- face_patch: int32 [1048576, 1], P('blk'), may hold values from 0 to 63; in each aligned block of 16384 rows (0 to 16383, 16384 to 32767, ...) at most 512 rows name the same one
- face_point: int32 [1048576], P('blk'), may hold values from 0 to 16383
- live_count: int32 [64], P('blk'), may hold values from 1 to 16384, 917504 in all
- impinged: int32 [1048576], P('blk'), may hold values 0 or 1
- crystal_load: float32 [1048576], P('blk'), may hold values from 0.2 to 2
- film: float32 [1048576], P('blk'), may hold values from 0.05 to 1
Outputs:
- new_columns: float32 [2, 64, 1048576], P('grp', None, 'blk')
- surface: float32 [2, 2, 1048576], P('grp', None, 'blk')
Inputs may be any that keep to these rules, and one draw needn't show every extreme that they name: `face_patch`: among the faces of one gas block (aligned blocks of 16384 rows) no patch is named more than 512 times. `operators`: diagonal entries lie in 0.5 to 1.
All inputs are finite; a program needn't handle non-finite values. No bound on the sum of `live_count` or of `impinged` on one device may be relied on, other than what follows from the above.
Results may differ from a plain program's by a relative error of at most 0.0001.
Values sent between devices are 32-bit elements; how exact they have to be, the bound alone decides.
No kernel may reach another device: no remote copies, remote signals or barrier semaphores. Data moves between devices by JAX's collectives and lax.ppermute only.
A program may use at most 128 MiB of HBM per device.

v0:
```python
import jax
import jax.numpy as jnp
from jax import lax
from jax.sharding import PartitionSpec as P

ITERS = 4


def extended(x, sides, width):
    for axis, dim in sides:
        size, length = (lax.axis_size(axis), x.shape[dim])
        up = [(i, (i + 1) % size) for i in range(size - 1)]
        down = [(j, i) for i, j in up]
        last = lax.slice_in_dim(x, length - width, length, axis=dim)
        first = lax.slice_in_dim(x, 0, width, axis=dim)
        before = lax.ppermute(last, axis, up)
        after = lax.ppermute(first, axis, down)
        x = jnp.concatenate([before, x, after], axis=dim)
    return x


def lateral_of(padded, row):
    return padded[:-2] + padded[2:] - 2.0 * row


def build_slots(face_patch, face_point, live_count):
    patch = face_patch[:, 0]
    width = patch.shape[0]
    blocks = lax.axis_size("blk")
    capacity = 2 * width // blocks
    live = lax.iota(jnp.int32, width) < live_count[0]
    onehot = (patch[None, :] == lax.iota(jnp.int32, blocks)[:, None]).astype(jnp.int32)
    ranks = jnp.sum(jnp.cumsum(onehot, axis=1) * onehot, axis=0) - 1
    slots = patch * capacity + ranks
    targets = jnp.where(live, face_point, width)
    marker = jnp.full((blocks * capacity,), width, jnp.int32).at[slots].set(targets)
    return (live, slots, marker.reshape(1, blocks, capacity), capacity)


def local(
    columns,
    operators,
    normal_weights,
    face_patch,
    face_point,
    live_count,
    impinged,
    crystal_load,
    film,
):
    highest = lax.Precision.HIGHEST
    width = columns.shape[2]
    blocks = lax.axis_size("blk")
    gas_flag = lax.axis_index("grp") == 0
    side = columns[0]
    matrix = operators[0]
    live, slots, marker, capacity = build_slots(face_patch, face_point, live_count)
    live_float = live.astype(jnp.float32)
    gas_rim = extended(side[0:1], (("blk", 1),), 1)[0]

    def gas_payload():
        flux = (
            jnp.dot(normal_weights[0], side, precision=highest, preferred_element_type=jnp.float32)
            + 0.25 * lateral_of(gas_rim, side[0])
        ) * live_float
        crystal = impinged.astype(jnp.float32) * crystal_load * live_float
        filled = (
            jnp.zeros((2, blocks * capacity), jnp.float32)
            .at[:, slots]
            .set(jnp.stack([flux, crystal]))
        )
        return filled.reshape(2, blocks, capacity)

    def wall_payload():
        return jnp.zeros((2, blocks, capacity), jnp.float32)

    payload = lax.cond(gas_flag, gas_payload, wall_payload)
    sent_marker = jnp.where(gas_flag, marker, width)
    outgoing = jnp.concatenate([jnp.zeros_like(payload), payload], axis=1)
    out_marker = jnp.concatenate([jnp.full_like(sent_marker, width), sent_marker], axis=1)
    arrived, arrived_marker = (
        lax.all_to_all(outgoing, ("grp", "blk"), split_axis=1, concat_axis=1, tiled=True),
        lax.all_to_all(out_marker, ("grp", "blk"), split_axis=1, concat_axis=1, tiled=True),
    )
    arrived = arrived[:, :blocks]
    arrived_marker = arrived_marker[:, :blocks]
    rows = arrived.reshape(2, blocks * capacity)
    points = arrived_marker.reshape(blocks * capacity)

    def wall_sums():
        heat_sum = jnp.zeros((width,), jnp.float32).at[points].add(rows[0], mode="drop")
        mass_sum = jnp.zeros((width,), jnp.float32).at[points].add(rows[1], mode="drop")
        return (heat_sum, mass_sum)

    def gas_sums():
        return (jnp.zeros((width,), jnp.float32), jnp.zeros((width,), jnp.float32))

    heat, mass = lax.cond(gas_flag, gas_sums, wall_sums)

    def substep(current, rim_row, heat_part, mass_part):
        source = 0.2 * (heat_part - 0.5 * mass_part + 0.5 * lateral_of(rim_row, current[0]))
        return jnp.dot(
            matrix, current.at[0].add(source), precision=highest, preferred_element_type=jnp.float32
        )

    wall = side
    for step in range(ITERS):
        wall_rim = extended(wall[0:1], (("blk", 1),), 1)[0]
        wall = lax.cond(
            gas_flag,
            lambda current, rim_row: current,
            lambda current, rim_row: substep(current, rim_row, heat, mass),
            wall,
            wall_rim,
        )

    def wall_lookup():
        film_new = jnp.maximum(film + 0.5 * (wall[0] - 0.3) - 0.1 * mass, 0.0)
        surface_rows = jnp.stack([wall[0], film_new])
        valid = (points < width).astype(jnp.float32)
        found = surface_rows[:, jnp.minimum(points, width - 1)] * valid[None, :]
        return (surface_rows, found.reshape(2, blocks, capacity))

    def gas_lookup():
        return (jnp.zeros((2, width), jnp.float32), jnp.zeros((2, blocks, capacity), jnp.float32))

    wall_surface, looked = lax.cond(gas_flag, gas_lookup, wall_lookup)
    replies = jnp.concatenate([looked, jnp.zeros_like(looked)], axis=1)
    returned = lax.all_to_all(replies, ("grp", "blk"), split_axis=1, concat_axis=1, tiled=True)[
        :, blocks:
    ]

    def gas_finish():
        face_values = returned.reshape(2, blocks * capacity)[:, slots] * live_float[None, :]
        gas_new = (
            jnp.dot(matrix, side, precision=highest, preferred_element_type=jnp.float32)
            + normal_weights[1][:, None] * face_values[0][None, :]
        )
        return (gas_new, face_values)

    def wall_finish():
        return (wall, wall_surface)

    new_columns, surface = lax.cond(gas_flag, gas_finish, wall_finish)
    return (new_columns[None], surface[None])


def solution(mesh):
    return jax.shard_map(
        local,
        mesh=mesh,
        in_specs=(
            P("grp", None, "blk"),
            P("grp", None, None),
            P(),
            P("blk", None),
            P("blk"),
            P("blk"),
            P("blk"),
            P("blk"),
            P("blk"),
        ),
        out_specs=(P("grp", None, "blk"), P("grp", None, "blk")),
        check_vma=False,
    )
```

profile of v0, /device:TPU:0, one launch (start us, length us, event | category | flops | bytes accessed | tf_op | source)
XLA Modules:
  0.0 899.7 jit_solution(3093149880959852161)
XLA Ops:
  16.4 60.4 %scatter_custom_fusion.3 = s32[32768]{0:T(1024)S(1)} fusion(s32[16384]{0:T(1024)S(1)} %bitcast.112, s32[16384]{0:T(1024)S(1)} %fusion.16, s32[]{:T(128)} %constant.202.clone.1), kind=kCustom, calls=%fused_computation.65 | custom fusion | bytes 131076 | tf_op jit(solution)/shard_map/scatter | solution.py:36
  77.6 11.4 %all-to-all-start = ((s32[1,128,512]{2,0,1:T(1,128)}), s32[1,128,512]{2,0,1:T(1,128)S(1)}, u32[]{:S(2)}, u32[]{:S(2)}) async-start(s32[1,128,512]{2,0,1:T(1,128)} %concatenate.30), calls=%async_computation | async-start | bytes 524288 | tf_op jit(solution)/shard_map/all_to_all | solution.py:83
  90.9 58.1 %conditional.8 = (f32[2,64,512]{0,2,1:T(8,128)}) conditional(s32[]{:T(128)} %convert_element_type.10, () %tuple.81, (s32[16384]{0:T(1024)S(1)}, f32[2,64]{1,0:T(2,128)S(1)}, f32[64,16384]{1,0:T(8,128)}, f32[16386]{0:T(1024)S(1)}, f32[16384]{0:T(1024)S(1)}, /*index=5*/s32[16384]{0:T(1024)S(1)}, f32[16384]{0:T(1024)S(1)}) %tuple.147), branch_computations={%region_3.4_spmd, %region_4.6_spmd} | conditional | flops 12812288 | bytes 5899272 | solution.py:77
  96.5 5.0 copy.34
  101.4 47.4 %scatter_custom_fusion = f32[2,32768]{0,1:T(8,128)} fusion(s32[16384]{0:T(1024)S(1)} %compare_select_fusion.1, f32[16384,2]{1,0:T(8,128)} %copy.34, f32[]{:T(128)} %constant.161.clone), kind=kCustom, calls=%fused_computation.29 | custom fusion | bytes 262656 | tf_op jit(solution)/shard_map/cond/branch_1_fun/scatter | solution.py:70
  149.0 9.2 %copy.38 = f32[2,64,512]{2,0,1:T(2,128)S(1)} copy(f32[2,64,512]{0,2,1:T(8,128)} %get-tuple-element.283) | data formatting | bytes 524288 | tf_op jit(solution)/shard_map/cond | solution.py:77
  159.1 9.8 %all-to-all-start.1 = ((f32[2,128,512]{2,0,1:T(2,128)}), f32[2,128,512]{2,0,1:T(2,128)S(1)}, u32[]{:S(2)}, u32[]{:S(2)}) async-start(f32[2,128,512]{2,0,1:T(2,128)} %concatenate.32), calls=%async_computation.1 | async-start | bytes 1048576 | tf_op jit(solution)/shard_map/all_to_all | solution.py:82
  168.9 12.8 %all-to-all-done.1 = f32[2,128,512]{2,0,1:T(2,128)S(1)} async-done(((f32[2,128,512]{2,0,1:T(2,128)}), f32[2,128,512]{2,0,1:T(2,128)S(1)}, u32[]{:S(2)}, u32[]{:S(2)}) %all-to-all-start.1) | async-done | bytes 524320 | tf_op jit(solution)/shard_map/all_to_all | solution.py:82
  199.0 4.7 conditional.11
  222.8 5.2 collective-permute-start.6
  235.2 4.8 conditional.13
  240.0 7.8 conditional.14
  240.0 7.8 broadcast.248
  247.9 9.2 %copy.40 = f32[2,64,512]{2,0,1:T(2,128)S(1)} copy(f32[2,64,512]{0,2,1:T(8,128)} %get-tuple-element.207) | data formatting | bytes 524288 | tf_op jit(solution)/shard_map/cond | solution.py:127
  258.0 514.0 %all-to-all-start.2 = ((f32[2,128,512]{2,0,1:T(2,128)}), f32[2,128,512]{2,0,1:T(2,128)S(1)}, u32[]{:S(2)}, u32[]{:S(2)}) async-start(f32[2,128,512]{2,0,1:T(2,128)} %concatenate.36), calls=%async_computation.2 | async-start | bytes 1048576 | tf_op jit(solution)/shard_map/all_to_all | solution.py:129
  772.0 12.8 %all-to-all-done.2 = f32[2,128,512]{2,0,1:T(2,128)S(1)} async-done(((f32[2,128,512]{2,0,1:T(2,128)}), f32[2,128,512]{2,0,1:T(2,128)S(1)}, u32[]{:S(2)}, u32[]{:S(2)}) %all-to-all-start.2) | async-done | bytes 524320 | tf_op jit(solution)/shard_map/all_to_all | solution.py:129
  784.8 113.8 %conditional.15 = (f32[64,16384]{1,0:T(8,128)}, f32[1,2,16384]{2,1,0:T(2,128)S(1)}) conditional(s32[]{:T(128)} %convert_element_type.10, (f32[64,16384]{1,0:T(8,128)}, f32[2,16384]{1,0:T(2,128)S(1)}) %tuple.91, (f32[64,64]{1,0:T(8,128)S(1)}, f32[64,16384]{1,0:T(8,128)}, f32[2,64]{1,0:T(2,128)S(1)}, f32[2,128,512]{2,0,1:T(2,128)S(1)}, ...), branch_computations={%region_21.22_spmd, %region_22.23_spmd} | conditional | flops 807518208 | bytes 28066604 | solution.py:144
  785.1 16.0 %copy.42 = f32[2,128,512]{0,2,1:T(8,128)} copy(f32[2,128,512]{2,0,1:T(2,128)S(1)} %get-tuple-element.249) | data formatting | bytes 1048576 | tf_op jit(solution)/shard_map
  801.0 11.5 %slice.219 = f32[2,64,512]{0,2,1:T(8,128)} slice(f32[2,128,512]{0,2,1:T(8,128)} %copy.42), slice={[0:2], [64:128], [0:512]} | slice | bytes 524288 | tf_op jit(solution)/shard_map/slice | solution.py:129
  812.5 60.5 %gather_fusion.1 = f32[16384,2]{1,0:T(8,128)} fusion(f32[2,32768]{0,1:T(8,128)} %bitcast.82, s32[16384]{0:T(1024)S(1)} %fusion.11), kind=kCustom, calls=%fused_computation.1 | custom fusion | bytes 327680 | tf_op jit(solution)/shard_map/cond/branch_1_fun/gather | solution.py:134
  873.0 7.9 bitcast_multiply_fusion
  880.9 5.3 copy.45
  886.2 7.0 fusion.10
  893.2 5.3 convolution_add_fusion
  (83 shorter events, 87.4 us)
Async XLA Ops:
  2.4 86.7 %collective-permute-start = (f32[1,1]{1,0:T(1,128)}, f32[1,1]{1,0:T(1,128)}, u32[]{:S(2)}, u32[]{:S(2)}) collective-permute-start(f32[1,1]{1,0:T(1,128)} %get-tuple-element.268), channel_id=1, source_target_pairs={{0,1},{1,2},{2,3},{3,4},{4,5},{5,6},{6,7},{7,8},{8,9},{9,10},{10,1... | collective-permute-start | bytes 20 | tf_op jit(solution)/shard_map/ppermute | solution.py:16
  6.8 82.3 %collective-permute-start.1 = (f32[1,1]{1,0:T(1,128)}, f32[1,1]{1,0:T(1,128)}, u32[]{:S(2)}, u32[]{:S(2)}) collective-permute-start(f32[1,1]{1,0:T(1,128)} %get-tuple-element.267), channel_id=1, source_target_pairs={{1,0},{2,1},{3,2},{4,3},{5,4},{6,5},{7,6},{8,7},{9,8},{10,9},{11,1... | collective-permute-start | bytes 20 | tf_op jit(solution)/shard_map/ppermute | solution.py:17
  9.0 6.5 copy-start.3
  9.1 7.3 copy-start.7
  9.6 2.0 copy-start.1
  11.6 79.2 %copy-start.5 = (s32[16384]{0:T(1024)S(1)}, s32[16384]{0:T(1024)}, u32[]{:S(2)}) copy-start(s32[16384]{0:T(1024)} %param.39) | copy-start | bytes 196612
  11.6 79.2 %copy-start.6 = (f32[16384]{0:T(1024)S(1)}, f32[16384]{0:T(1024)}, u32[]{:S(2)}) copy-start(f32[16384]{0:T(1024)} %param.40) | copy-start | bytes 196612
  11.6 79.2 %copy-start.9 = (f32[2,64]{1,0:T(2,128)S(1)}, f32[2,64]{1,0:T(2,128)}, u32[]{:S(2)}) copy-start(f32[2,64]{1,0:T(2,128)} %param.35) | copy-start | bytes 1540
  77.6 81.5 %all-to-all-start = ((s32[1,128,512]{2,0,1:T(1,128)}), s32[1,128,512]{2,0,1:T(1,128)S(1)}, u32[]{:S(2)}, u32[]{:S(2)}) async-start(s32[1,128,512]{2,0,1:T(1,128)} %concatenate.30), calls=%async_computation | async-start | bytes 524288 | tf_op jit(solution)/shard_map/all_to_all | solution.py:83
  158.2 23.5 %copy-start.2 = (f32[1,64,64]{2,1,0:T(8,128)S(1)}, f32[1,64,64]{2,1,0:T(8,128)}, u32[]{:S(2)}) copy-start(f32[1,64,64]{2,1,0:T(8,128)} %param.34) | copy-start | bytes 49156
  159.1 22.5 %all-to-all-start.1 = ((f32[2,128,512]{2,0,1:T(2,128)}), f32[2,128,512]{2,0,1:T(2,128)S(1)}, u32[]{:S(2)}, u32[]{:S(2)}) async-start(f32[2,128,512]{2,0,1:T(2,128)} %concatenate.32), calls=%async_computation.1 | async-start | bytes 1048576 | tf_op jit(solution)/shard_map/all_to_all | solution.py:82
  188.7 4.5 collective-permute-start.2
  191.9 5.6 collective-permute-start.3
  206.1 4.0 collective-permute-start.4
  208.8 5.5 collective-permute-start.5
  222.8 6.5 collective-permute-start.6
  228.0 5.7 collective-permute-start.7
  235.2 4.8 copy-start.8
  258.0 526.8 %all-to-all-start.2 = ((f32[2,128,512]{2,0,1:T(2,128)}), f32[2,128,512]{2,0,1:T(2,128)S(1)}, u32[]{:S(2)}, u32[]{:S(2)}) async-start(f32[2,128,512]{2,0,1:T(2,128)} %concatenate.36), calls=%async_computation.2 | async-start | bytes 1048576 | tf_op jit(solution)/shard_map/all_to_all | solution.py:129
  886.2 7.0 copy-start
  898.6 0.7 copy-start.4
where the time goes:
time: 910 us; the launch traced here: 900 us
  starting transfers between devices  556 us (61%)
  local copies, waits for them, and re-layouts  272 us (30%)
  waiting for transfers between devices  38.5 us (4%)
  other arithmetic  20.9 us (2%)
  matrix products  9.58 us (1%)
    all_to_all x1, starting transfers between devices, local(): lax.all_to_all(replies, ('grp', 'blk'), split_axis=1, concat_axis=1, tile...  514 us
    gather x1, local copies, waits for them, and re-layouts, gas_finish(): returned.reshape(2, blocks * capacity)[:, slots] * live_float[None, :]  60.5 us
    scatter x1, local copies, waits for them, and re-layouts, build_slots(): jnp.full((blocks * capacity,), width, jnp.int32).at[slots].set(targets)  60.4 us
    scatter x1, local copies, waits for them, and re-layouts, gas_payload(): filled = jnp.zeros((2, blocks * capacity), jnp.float32).at[:, slots].set(...  47.4 us
    another operation x7, local copies, waits for them, and re-layouts  23.8 us
    cond x7, local copies, waits for them, and re-layouts  23.3 us
  transfers between devices with their start and end apart: 11, of which 5 were waited for; matrix products, arithmetic and copies ran while one was open for 15% of the time, Pallas kernels for 0%

commit v1 on v0

v1 whole, which is shorter than its diff:
```python
import jax
import jax.numpy as jnp
from jax import lax
from jax.experimental import pallas as pl
from jax.experimental.pallas import tpu as pltpu
from jax.sharding import PartitionSpec as P

ITERS = 4
L = 128
HALO = ITERS
ROWS = 12
FACE_CHUNK = 2048
SLOT_STEP = 8

f32 = jnp.float32
bf16 = jnp.bfloat16
i32 = jnp.int32
HIGHEST = lax.Precision.HIGHEST
NT = (((1,), (1,)), ((), ()))
NN = (((1,), (0,)), ((), ()))


def iota(shape, dim):
    return lax.broadcasted_iota(i32, shape, dim)


def split(x):
    high = x.astype(bf16).astype(f32)
    return high, x - high


def dot(a, b, dims=NN, precision=None):
    return lax.dot_general(a, b, dims, precision=precision, preferred_element_type=f32)


def onehot(mask):
    return jnp.where(mask, 1.0, 0.0).astype(bf16)


def masked(mask, x):
    return jnp.where(mask, x, 0.0).astype(bf16)


def route(width, blocks, capacity):
    c = FACE_CHUNK
    steps = width // c
    per = capacity // L
    highs = blocks * per
    sub = 256

    def kernel(live_ref, patch_ref, point_ref, v0_ref, side_ref, weight_ref, out_ref, slot_ref, carry, acc, eacc):
        i = pl.program_id(0)

        @pl.when(i == 0)
        def _():
            carry[...] = jnp.zeros_like(carry)
            acc[...] = jnp.zeros_like(acc)
            eacc[...] = jnp.zeros_like(eacc)

        patch, point = patch_ref[...], point_ref[...]
        named = iota((blocks, c), 0) == patch
        hot = onehot(named)
        upto = onehot(iota((sub, sub), 0) <= iota((sub, sub), 1))
        before = carry[...]
        ranks = []
        for j in range(c // sub):
            cut = slice(j * sub, (j + 1) * sub)
            count = dot(hot[:, cut], upto)
            ranks.append(jnp.sum(jnp.where(named[:, cut], count + before, 0.0), axis=0, keepdims=True))
            before = before + count[:, sub - 1 : sub]
        carry[...] = before
        rank = jnp.concatenate(ranks, axis=1).astype(i32) - 1
        slot = patch * capacity + rank
        slot_ref[...] = slot

        live = (iota((1, c), 1) + i * c) < live_ref[0]
        value = v0_ref[...] + jnp.sum(weight_ref[...] * side_ref[...], axis=0, keepdims=True)
        value = jnp.where(live, value, 0.0)
        v_high, v_low = split(value)
        t_high, t_low = ((point >> 7).astype(f32), (point & (L - 1)).astype(f32))
        high = onehot(iota((highs, c), 0) == (slot >> 7))
        low = iota((L, c), 0) == (slot & (L - 1))
        laid = jnp.concatenate([masked(low, x) for x in (v_high, v_low, t_high, t_low)], axis=0)
        placed = dot(high, laid, NT)
        for q in range(4):
            acc[pl.ds(q * highs, highs), :] += placed[:, q * L : (q + 1) * L]

        last = point >= width - 3
        edge_patch = jnp.where(last, patch + 1, jnp.where(point < 3, patch - 1, -1))
        edge_point = jnp.where(last, point - (width - 8), point)
        edge_hot = onehot(iota((blocks, c), 0) == edge_patch)
        edge_low = iota((8, c), 0) == edge_point
        zeros = jnp.zeros((L - 16, c), bf16)
        edges = jnp.concatenate([masked(edge_low, v_high), masked(edge_low, v_low)], axis=0)
        eacc[...] += dot(edge_hot, jnp.concatenate([edges, zeros], axis=0), NT)

        @pl.when(i == steps - 1)
        def _():
            for r in range(per):
                part = [acc[pl.ds(q * highs + r, blocks, stride=per), :] for q in range(4)]
                out_ref[pl.ds(r, blocks, stride=ROWS), :] = part[0] + part[1]
                out_ref[pl.ds(per + r, blocks, stride=ROWS), :] = part[2] * float(L) + part[3]
            edge = eacc[...]
            lane = iota(edge.shape, 1)
            both = edge + pltpu.roll(edge, L - 8, 1)
            out_ref[pl.ds(2 * per, blocks, stride=ROWS), :] = jnp.where(lane < 8, both, 0.0)
            for r in range(2 * per + 1, ROWS):
                out_ref[pl.ds(r, blocks, stride=ROWS), :] = jnp.zeros((blocks, L), f32)

    def call(live_count, patch, point, v0, side, weight):
        row = pl.BlockSpec((1, c), lambda i: (0, i))
        return pl.pallas_call(
            kernel,
            grid=(steps,),
            in_specs=[
                pl.BlockSpec(memory_space=pltpu.SMEM),
                row,
                row,
                row,
                pl.BlockSpec((side.shape[0], c), lambda i: (0, i)),
                pl.BlockSpec(weight.shape, lambda i: (0, 0)),
            ],
            out_specs=[pl.BlockSpec((blocks * ROWS, L), lambda i: (0, 0)), row],
            out_shape=[
                jax.ShapeDtypeStruct((blocks * ROWS, L), f32),
                jax.ShapeDtypeStruct((1, width), i32),
            ],
            scratch_shapes=[
                pltpu.VMEM((blocks, 1), f32),
                pltpu.VMEM((4 * highs, L), f32),
                pltpu.VMEM((blocks, L), f32),
            ],
            name="route",
        )(live_count, patch, point, v0, side, weight)

    return call


def matrices(nl, width):
    c = FACE_CHUNK
    steps = width // c
    out_rows = nl + 8
    tail = (ITERS + 1) * width // L

    def kernel(flag_ref, op_ref, weight_ref, halo_ref, side_ref, y_ref, rows_ref, coef_ref, lhs):
        i = pl.program_id(0)

        @pl.when(i == 0)
        def _():
            gas = flag_ref[0] == 1
            one = op_ref[...]
            two = dot(one, one, precision=HIGHEST)
            three = dot(two, one, precision=HIGHEST)
            four = dot(two, two, precision=HIGHEST)
            main = jnp.where(gas, one, four)
            unit = jnp.where(iota((1, nl), 1) == 0, 1.0, 0.0)
            full = jnp.concatenate([main, unit, one[0:1], two[0:1], three[0:1], four[0:1], jnp.zeros((3, nl), f32)], axis=0)
            high, low = split(full)
            lhs[...] = jnp.concatenate([high, low, high, low], axis=1).astype(bf16)
            rows_ref[pl.ds(tail, 8), :] = dot(full[nl:], halo_ref[...], precision=HIGHEST)
            lead = [jnp.broadcast_to(m[0:1, 0:1], (1, L)) for m in (one, two, three, four)]
            rows_ref[pl.ds(tail + 8, 8), :] = jnp.concatenate(lead + [jnp.zeros((4, L), f32)], axis=0)
            lane = iota((nl, L), 1)
            coef = jnp.where(lane == 0, jnp.where(gas, weight_ref[...], four[:, 0:1]), 0.0)
            for k, m in ((1, three), (2, two), (3, one)):
                coef = jnp.where(lane == k, jnp.where(gas, 0.0, m[:, 0:1]), coef)
            coef_ref[...] = coef

        high, low = split(side_ref[...])
        high, low = high.astype(bf16), low.astype(bf16)
        out = dot(lhs[...], jnp.concatenate([high, high, low, low], axis=0))
        y_ref[...] = out[:nl]
        for n in range(ITERS + 1):
            part = [out[nl + n : nl + n + 1, k * L : (k + 1) * L] for k in range(c // L)]
            start = pl.multiple_of(n * (width // L) + i * (c // L), 8)
            rows_ref[pl.ds(start, c // L), :] = jnp.concatenate(part, axis=0)

    def call(flag, op, weight, halo, side):
        return pl.pallas_call(
            kernel,
            grid=(steps,),
            in_specs=[
                pl.BlockSpec(memory_space=pltpu.SMEM),
                pl.BlockSpec((nl, nl), lambda i: (0, 0)),
                pl.BlockSpec((nl, 1), lambda i: (0, 0)),
                pl.BlockSpec((nl, L), lambda i: (0, 0)),
                pl.BlockSpec((nl, c), lambda i: (0, i)),
            ],
            out_specs=[
                pl.BlockSpec((nl, c), lambda i: (0, i)),
                pl.BlockSpec((tail + 16, L), lambda i: (0, 0)),
                pl.BlockSpec((nl, L), lambda i: (0, 0)),
            ],
            out_shape=[
                jax.ShapeDtypeStruct((nl, width), f32),
                jax.ShapeDtypeStruct((tail + 16, L), f32),
                jax.ShapeDtypeStruct((nl, L), f32),
            ],
            scratch_shapes=[pltpu.VMEM((out_rows, 4 * nl), bf16)],
            name="matrices",
        )(flag, op, weight, halo, side)

    return call


def gather_sum(width, blocks, capacity):
    per = capacity // L
    tall = width // L

    def kernel(x_ref, out_ref, acc):
        acc[...] = jnp.zeros_like(acc)

        def step(s, edge):
            start = pl.multiple_of(s * SLOT_STEP * ROWS, 8)
            x = x_ref[pl.ds(start, SLOT_STEP * ROWS), :]
            v_high, v_low = split(x)
            t = x.astype(i32)
            t_high, t_low = t >> 7, t & (L - 1)
            highs, lows = [], []
            for m in range(SLOT_STEP):
                edge = edge + x[m * ROWS + 2 * per : m * ROWS + 2 * per + 1]
                for r in range(per):
                    a, b = m * ROWS + r, m * ROWS + per + r
                    highs.append(onehot(iota((tall, L), 0) == t_high[b : b + 1]))
                    low = iota((L, L), 0) == t_low[b : b + 1]
                    lows.append(jnp.concatenate([masked(low, v_high[a : a + 1]), masked(low, v_low[a : a + 1])], axis=0))
            acc[...] += dot(jnp.concatenate(highs, axis=1), jnp.concatenate(lows, axis=1), NT)
            return edge

        edge = lax.fori_loop(0, blocks // SLOT_STEP, step, jnp.zeros((1, L), f32))
        out_ref[pl.ds(0, tall), :] = acc[:, :L] + acc[:, L:]
        out_ref[pl.ds(tall, 8), :] = jnp.broadcast_to(edge, (8, L))

    def call(x):
        return pl.pallas_call(
            kernel,
            out_shape=jax.ShapeDtypeStruct((tall + 8, L), f32),
            scratch_shapes=[pltpu.VMEM((tall, 2 * L), f32)],
            name="gather_sum",
        )(x)

    return call


def surface_lookup(width, blocks, capacity):
    per = capacity // L
    tall = width // L
    ext = tall + 16

    def kernel(flag_ref, mine_ref, other_ref, rows_ref, film_ref, x_ref, out_ref, source_ref, surface_ref):
        gas = flag_ref[0] == 1
        lane, line = iota((ext, L), 1), iota((ext, L), 0)
        inside = (line >= 8) & (line < tall + 8)
        left = (line == 7) & (lane >= L - HALO)
        right = (line == tall + 8) & (lane < HALO)
        valid = inside | (left & (flag_ref[1] == 1)) | (right & (flag_ref[2] == 1))

        def extend(body, edge_left, edge_right):
            zeros = jnp.zeros((7, L), f32)
            full = jnp.concatenate([zeros, edge_left, body, edge_right, zeros], axis=0)
            return jnp.where(valid, full, 0.0)

        def lateral(x):
            ahead = pltpu.roll(x, L - 1, 1)
            ahead = jnp.where(lane == L - 1, pltpu.roll(ahead, ext - 1, 0), ahead)
            behind = pltpu.roll(x, 1, 1)
            behind = jnp.where(lane == 0, pltpu.roll(behind, 1, 0), behind)
            return behind + ahead - 2.0 * x

        mine, other = mine_ref[...], other_ref[...]
        heat, mass = jnp.where(gas, mine, other), jnp.where(gas, other, mine)
        q = heat - 0.5 * mass
        q_edge = q[tall : tall + 1]
        q = extend(q[:tall], pltpu.roll(q_edge, L - 8, 1), q_edge)
        tail = (ITERS + 1) * tall
        lead = rows_ref[pl.ds(tail + 8, 8), :]

        def base(n):
            edge = rows_ref[pl.ds(tail + n, 1), :]
            return extend(rows_ref[pl.ds(n * tall, tall), :], edge, edge)

        sources = []
        row = base(0)
        for n in range(1, ITERS + 1):
            sources.append(0.2 * (q + 0.5 * lateral(row)))
            row = base(n)
            for j, source in enumerate(sources):
                row = row + lead[n - 1 - j : n - j] * source
            row = jnp.where(valid, row, 0.0)
        for n in range(ITERS):
            source_ref[pl.ds(n * tall, tall), :] = sources[n][8 : tall + 8]
        wall_row = row[8 : tall + 8]
        film_new = jnp.maximum(film_ref[...] + 0.5 * (wall_row - 0.3) - 0.1 * mass[:tall], 0.0)
        surface_ref[pl.ds(0, tall), :] = wall_row
        surface_ref[pl.ds(tall, tall), :] = film_new

        high, low = split(jnp.where(gas, film_new, wall_row).T)
        table = jnp.concatenate([high, low], axis=1).astype(bf16)

        def step(s, carry):
            start = pl.multiple_of(s * SLOT_STEP * ROWS, 8)
            t = x_ref[pl.ds(start, SLOT_STEP * ROWS), :].astype(i32)
            t_high, t_low = t >> 7, t & (L - 1)
            rows = [m * ROWS + per + r for m in range(SLOT_STEP) for r in range(per)]
            highs = jnp.concatenate([onehot(iota((tall, L), 0) == t_high[b : b + 1]) for b in rows], axis=1)
            found = dot(table, jnp.concatenate([highs, highs], axis=0))
            picked = []
            for k, b in enumerate(rows):
                low = iota((L, L), 0) == t_low[b : b + 1]
                picked.append(jnp.sum(jnp.where(low, found[:, k * L : (k + 1) * L], 0.0), axis=0, keepdims=True))
            size = SLOT_STEP * per
            out_ref[pl.ds(pl.multiple_of(s * size, 8), size), :] = jnp.concatenate(picked, axis=0)
            return carry

        lax.fori_loop(0, blocks // SLOT_STEP, step, 0)

    def call(flags, mine, other, rows, film, x):
        vmem = pl.BlockSpec(memory_space=pltpu.VMEM)
        return pl.pallas_call(
            kernel,
            in_specs=[pl.BlockSpec(memory_space=pltpu.SMEM)] + [vmem] * 5,
            out_shape=[
                jax.ShapeDtypeStruct((blocks * per, L), f32),
                jax.ShapeDtypeStruct((ITERS * tall, L), f32),
                jax.ShapeDtypeStruct((2 * tall, L), f32),
            ],
            name="surface_lookup",
        )(flags, mine, other, rows, film, x)

    return call


def face_lookup(width, blocks, capacity):
    c = FACE_CHUNK
    steps = width // c
    highs = blocks * capacity // L

    def kernel(live_ref, reply_ref, slot_ref, out_ref, table):
        i = pl.program_id(0)

        @pl.when(i == 0)
        def _():
            high, low = split(reply_ref[...].T)
            table[...] = jnp.concatenate([high, low], axis=1).astype(bf16)

        slot = slot_ref[...]
        hot = onehot(iota((highs, c), 0) == (slot >> 7))
        found = dot(table[...], jnp.concatenate([hot, hot], axis=0))
        low = iota((L, c), 0) == (slot & (L - 1))
        live = (iota((1, c), 1) + i * c) < live_ref[0]
        picked = jnp.where(live, jnp.sum(jnp.where(low, found, 0.0), axis=0, keepdims=True), 0.0)
        out_ref[...] = jnp.concatenate([picked[:, k * L : (k + 1) * L] for k in range(c // L)], axis=0)

    def call(live_count, reply, slot):
        return pl.pallas_call(
            kernel,
            grid=(steps,),
            in_specs=[
                pl.BlockSpec(memory_space=pltpu.SMEM),
                pl.BlockSpec((highs, L), lambda i: (0, 0)),
                pl.BlockSpec((1, c), lambda i: (0, i)),
            ],
            out_specs=pl.BlockSpec((c // L, L), lambda i: (i, 0)),
            out_shape=jax.ShapeDtypeStruct((width // L, L), f32),
            scratch_shapes=[pltpu.VMEM((L, 2 * highs), bf16)],
            name="face_lookup",
        )(live_count, reply, slot)

    return call


def finish(nl, width):
    c = FACE_CHUNK
    steps = width // c
    tall = width // L
    part = c // L

    def kernel(flag_ref, y_ref, coef_ref, source_ref, surface_ref, mine_ref, other_ref, out_ref, rows_ref):
        gas = flag_ref[0] == 1
        film, first = mine_ref[...], other_ref[...]
        coef = coef_ref[...]
        sources = [jnp.where(gas, first, source_ref[0])] + [source_ref[n] for n in range(1, ITERS)]
        spread = [jnp.broadcast_to(coef[:, n : n + 1], (nl, L)) for n in range(ITERS)]
        for k in range(part):
            cut = slice(k * L, (k + 1) * L)
            total = y_ref[:, cut]
            for n in range(ITERS):
                total = total + spread[n] * sources[n][k : k + 1]
            out_ref[:, cut] = total
        top = jnp.where(gas, first, surface_ref[0])
        bottom = jnp.where(gas, film, surface_ref[1])
        for n, x in enumerate((top, bottom)):
            rows_ref[n : n + 1, :] = jnp.concatenate([x[k : k + 1] for k in range(part)], axis=1)

    def call(flag, y, coef, source, surface, mine, other):
        tile = pl.BlockSpec((part, L), lambda i: (i, 0))
        return pl.pallas_call(
            kernel,
            grid=(steps,),
            in_specs=[
                pl.BlockSpec(memory_space=pltpu.SMEM),
                pl.BlockSpec((nl, c), lambda i: (0, i)),
                pl.BlockSpec((nl, L), lambda i: (0, 0)),
                pl.BlockSpec((ITERS, part, L), lambda i: (0, i, 0)),
                pl.BlockSpec((2, part, L), lambda i: (0, i, 0)),
                tile,
                tile,
            ],
            out_specs=[pl.BlockSpec((nl, c), lambda i: (0, i)), pl.BlockSpec((2, c), lambda i: (0, i))],
            out_shape=[jax.ShapeDtypeStruct((nl, width), f32), jax.ShapeDtypeStruct((2, width), f32)],
            name="finish",
        )(flag, y, coef, source.reshape(ITERS, tall, L), surface.reshape(2, tall, L), mine, other)

    return call


def local(columns, operators, normal_weights, face_patch, face_point, live_count, impinged, crystal_load, film):
    nl, width = columns.shape[1:]
    blocks = lax.axis_size("blk")
    capacity = 2 * width // blocks
    per = capacity // L
    tall = width // L
    block = lax.axis_index("blk")
    gas = lax.axis_index("grp") == 0
    side, matrix = columns[0], operators[0]
    flags = jnp.stack([gas, block > 0, block < blocks - 1]).astype(i32)

    up = [(i, i + 1) for i in range(blocks - 1)]
    down = [(i + 1, i) for i in range(blocks - 1)]
    swap = [(i, blocks + i) for i in range(blocks)] + [(blocks + i, i) for i in range(blocks)]
    left = lax.ppermute(side[:, width - HALO :], "blk", up)
    right = lax.ppermute(side[:, :HALO], "blk", down)
    halo = jnp.concatenate([right, jnp.zeros((nl, L - 2 * HALO), f32), left], axis=1)

    row = side[0]
    before = jnp.concatenate([jnp.zeros((1,), f32), row[:-1]])
    after = jnp.concatenate([row[1:], jnp.zeros((1,), f32)])
    v0 = jnp.where(gas, 0.25 * (before + after - 2.0 * row), impinged.astype(f32) * crystal_load)
    weight = jnp.where(gas, normal_weights[0], 0.0)[:, None]
    patch, point = face_patch.reshape(1, width), face_point.reshape(1, width)
    message, slot = route(width, blocks, capacity)(live_count, patch, point, v0.reshape(1, width), side, weight)

    lines, lanes = lax.broadcasted_iota(i32, message.shape, 0), lax.broadcasted_iota(i32, message.shape, 1)
    for f, amount in ((0, left[0, HALO - 1]), (width - 1, right[0, 0])):
        amount = jnp.where(gas & (live_count[0] > f), 0.25 * amount, 0.0)
        where, name, spot = slot[0, f], patch[0, f], point[0, f]
        line = (where // capacity) * ROWS + (where // L) % per
        message = message + jnp.where((lines == line) & (lanes == where % L), amount, 0.0)
        last = spot >= width - 3
        edge = jnp.where(last, name + 1, jnp.where(spot < 3, name - 1, -1))
        at = jnp.where(last, spot - (width - 8), spot)
        line = jnp.where(edge < 0, -1, edge * ROWS + 2 * per)
        message = message + jnp.where((lines == line) & (lanes == at), amount, 0.0)

    arrived = lax.all_to_all(message.reshape(-1), "blk", split_axis=0, concat_axis=0, tiled=True)
    arrived = arrived.reshape(blocks * ROWS, L)
    y, rows, coef = matrices(nl, width)(flags, matrix, normal_weights[1][:, None], halo, side)
    swapped = lax.ppermute(rows, ("grp", "blk"), swap)
    rows = jnp.where(gas, swapped, rows)

    mine = gather_sum(width, blocks, capacity)(arrived)
    other = lax.ppermute(mine, ("grp", "blk"), swap)
    replies, source, surface = surface_lookup(width, blocks, capacity)(flags, mine, other, rows, film.reshape(tall, L), arrived)
    returned = lax.all_to_all(replies.reshape(-1), "blk", split_axis=0, concat_axis=0, tiled=True)
    found = face_lookup(width, blocks, capacity)(live_count, returned.reshape(blocks * per, L), slot)
    paired = lax.ppermute(found, ("grp", "blk"), swap)
    new_columns, surface = finish(nl, width)(flags, y, coef, source, surface, found, paired)
    return new_columns[None], surface[None]


def solution(mesh):
    return jax.shard_map(
        local,
        mesh=mesh,
        in_specs=(
            P("grp", None, "blk"),
            P("grp", None, None),
            P(),
            P("blk", None),
            P("blk"),
            P("blk"),
            P("blk"),
            P("blk"),
            P("blk"),
        ),
        out_specs=(P("grp", None, "blk"), P("grp", None, "blk")),
        check_vma=False,
    )
```

time: 910 us -> 132 us (0.15)
  the two profiles are of different devices: /device:TPU:0 before, /device:TPU:1 now
where the time goes in v1:
time: 132 us; the launch traced here: 131 us
  Pallas kernels  51.9 us (39%)
  starting transfers between devices  26.5 us (20%)
  blocking collectives  16.5 us (12%)
  between operations  15.2 us (12%)
  local copies, waits for them, and re-layouts  10.7 us (8%)
  other arithmetic  8.87 us (7%)
    pallas_call x4, Pallas kernels, call(): pl.pallas_call(kernel, grid=(steps,), in_specs=[pl.BlockSpec(memory_space...  34.8 us
    all_to_all x1, blocking collectives, local(): lax.all_to_all(replies.reshape(-1), 'blk', split_axis=0, concat_axis=0, t...  16.5 us
    all_to_all x1, starting transfers between devices, local(): lax.all_to_all(message.reshape(-1), 'blk', split_axis=0, concat_axis=0, t...  15 us
    pallas_call x1, Pallas kernels, call(): pl.pallas_call(kernel, out_shape=jax.ShapeDtypeStruct((tall + 8, L), f32)...  8.79 us
    pallas_call x1, Pallas kernels, call(): pl.pallas_call(kernel, in_specs=[pl.BlockSpec(memory_space=pltpu.SMEM)] +...  8.36 us
    ppermute x1, starting transfers between devices, local(): left = lax.ppermute(side[:, width - HALO:], 'blk', up)  4.99 us
    slice x3, local copies, waits for them, and re-layouts, local(): where, name, spot = (slot[0, f], patch[0, f], point[0, f])  3.78 us
  transfers between devices with their start and end apart: 6, of which 1 were waited for; matrix products, arithmetic and copies ran while one was open for 11% of the time, Pallas kernels for 22%

profile of v1, /device:TPU:1, one launch (start us, length us, event | category | flops | bytes accessed | tf_op | source)
XLA Modules:
  0.0 130.9 jit_solution(1863533807877129683)
XLA Ops:
  0.6 0.9 fusion.5
  1.5 1.3 collective-permute-start
  2.8 5.0 %collective-permute-start.1 = (f32[64,4]{1,0:T(8,128)S(1)}, f32[64,4]{1,0:T(8,128)S(1)}, u32[]{:S(2)}, u32[]{:S(2)}) collective-permute-start(f32[64,4]{1,0:T(8,128)S(1)} %get-tuple-element.25), channel_id=1, source_target_pairs={{0,1},{1,2},{2,3},{3,4},{4,5},{5,6},{6,7},{7,8},{8,9},{9,10},{10,1... | collective-permute-start | bytes 3080 | tf_op jit(solution)/shard_map/ppermute | solution.py:431
  7.8 1.3 fusion.6
  11.6 1.3 fusion.8
  16.5 1.1 slice_multiply_fusion
  17.5 1.4 %fusion.4 = (f32[1,1,16383]{2,1,0:T(1,128)S(1)}, f32[1,1,16383]{2,1,0:T(1,128)S(1)}) fusion(f32[1,64,16384]{2,1,0:T(8,128)} %param.9), kind=kLoop, calls=%fused_computation.20 | loop fusion | bytes 262128 | tf_op jit(solution)/shard_map/slice | solution.py:437
  19.6 0.8 fusion.3
  21.1 1.6 %fusion.2 = f32[16384]{0:T(1024)} fusion(f32[16384]{0:T(1024)S(1)} %bitcast.44, f32[16383]{0:T(1024)S(1)} %bitcast.46, f32[1]{0:T(128)} %constant.99.clone.1, f32[16383]{0:T(1024)S(1)} %bitcast.45, f32[16384]{0:T(1024)} %param.16, s32[16384]{0:T(1024)} %param.15, pred[]{:T(512)} %eq.64), kind=kLoop, calls=%fused_computation.5 | loop fusion | flops 131072 | bytes 393213 | tf_op jit(solution)/shard_map/jit(_where)/select_n | solution.py:438
  22.7 12.3 %route.1 = (f32[768,128]{1,0:T(8,128)}, s32[1,16384]{1,0:T(1,128)}) custom-call(s32[1]{0:T(128)S(6)} %copy.17.live_ref, s32[1,16384]{1,0:T(1,128)} %bitcast.50, s32[1,16384]{1,0:T(1,128)} %bitcast.52, f32[1,16384]{1,0:T(1,128)} %bitcast.42, f32[64,16384]{1,0:T(8,128)} %bitcast.37, f32[64,1]{1,0:T(8,128)} %copy.14.weight_ref), custom_call_target="tpu_custom_call" | custom-call | tf_op jit(solution)/shard_map/route/pallas_call | solution.py:112
  35.0 1.2 fusion.7
  46.6 2.3 %select_add_fusion = f32[768,128]{1,0:T(8,128)} fusion(f32[768,128]{1,0:T(8,128)} %get-tuple-element.14, f32[]{:T(128)S(6)} %select_n.132, f32[]{:T(128)S(6)} %select_n.121, pred[128]{0:T(512)(128)(4,1)S(1)} %get-tuple-element.38, pred[128]{0:T(512)(128)(4,1)S(1)} %get-tuple-element.39, pred[128]{0:T(512)(128)(4,1)S(1)} %get-tuple-element.40, ...), kind=kLoop, calls=%fused_computation | loop fusion | flops 1179648 | bytes 790024 | tf_op jit(solution)/shard_map/add | solution.py:453
  49.0 15.0 %all-to-all-start = ((f32[64,1536,1]{1,2,0:T(1,128)}), f32[64,1536,1]{1,2,0:T(1,128)S(1)}, u32[]{:S(2)}, u32[]{:S(2)}) async-start(f32[64,1536,1]{1,2,0:T(1,128)} %bitcast.25), calls=%async_computation | async-start | bytes 786432 | tf_op jit(solution)/shard_map/all_to_all | solution.py:455
  64.7 8.1 %matrices.1 = (f32[64,16384]{1,0:T(8,128)}, f32[656,128]{1,0:T(8,128)}, f32[64,128]{1,0:T(8,128)}) custom-call(s32[3]{0:T(128)} %add_convert_fusion.flag_ref, f32[64,64]{1,0:T(8,128)} %bitcast.54, f32[64,1]{1,0:T(8,128)} %copy.13.weight_ref, f32[64,128]{1,0:T(8,128)} %pad_maximum_fusion.halo_ref, f32[64,16384]{1,0:T(8,128)} %bitcast.38), custom_call_target="tpu_custom_call" | custom-call | tf_op jit(solution)/shard_map/matrices/pallas_call | solution.py:179
  72.8 1.5 %collective-permute-start.3 = (f32[656,128]{1,0:T(8,128)}, f32[656,128]{1,0:T(8,128)S(1)}, u32[]{:S(2)}, u32[]{:S(2)}) collective-permute-start(f32[656,128]{1,0:T(8,128)} %get-tuple-element.16), channel_id=1, source_target_pairs={{0,64},{1,65},{2,66},{3,67},{4,68},{5,69},{6,70},{7,71},{8,72},{9,... | collective-permute-start | bytes 1007624 | tf_op jit(solution)/shard_map/ppermute | solution.py:458
  75.1 8.8 %gather_sum.1.mine_ref = f32[136,128]{1,0:T(8,128)} custom-call(f32[768,128]{1,0:T(8,128)} %bitcast.39), custom_call_target="tpu_custom_call" | custom-call | tf_op jit(solution)/shard_map/gather_sum/pallas_call | solution.py:235
  83.9 2.4 %collective-permute-start.2 = (f32[136,128]{1,0:T(8,128)}, f32[136,128]{1,0:T(8,128)S(1)}, u32[]{:S(2)}, u32[]{:S(2)}) collective-permute-start(f32[136,128]{1,0:T(8,128)} %gather_sum.1.mine_ref), channel_id=1, source_target_pairs={{0,64},{1,65},{2,66},{3,67},{4,68},{5,69},{6,70},{7,71},{8,72},{9,... | collective-permute-start | bytes 208904 | tf_op jit(solution)/shard_map/ppermute | solution.py:462
  86.2 1.8 %broadcast_select_fusion.rows_ref = f32[656,128]{1,0:T(8,128)} fusion(f32[656,128]{1,0:T(8,128)S(1)} %collective-permute-done.3, f32[656,128]{1,0:T(8,128)} %get-tuple-element.16, pred[]{:T(512)} %eq.64), kind=kLoop, calls=%fused_computation.1 | loop fusion | flops 83968 | bytes 1007617 | tf_op jit(solution)/shard_map/jit(_where)/select_n | solution.py:459
  88.6 8.4 %surface_lookup.1 = (f32[256,128]{1,0:T(8,128)}, f32[512,128]{1,0:T(8,128)}, f32[256,128]{1,0:T(8,128)}) custom-call(s32[3]{0:T(128)} %add_convert_fusion.flag_ref, f32[136,128]{1,0:T(8,128)} %gather_sum.1.mine_ref, f32[136,128]{1,0:T(8,128)} %copy-done.1, f32[656,128]{1,0:T(8,128)} %broadcast_select_fusion.rows_ref, f32[128,128]{1,0:T(8,128)} %bitcast.53, ...), custom_call_target="tpu_custom_call" | custom-call | tf_op jit(solution)/shard_map/surface_lookup/pallas_call | solution.py:319
  97.0 16.5 %all_to_all.18 = f32[64,512,1]{1,2,0:T(1,128)} all-to-all(f32[64,512,1]{1,2,0:T(1,128)} %bitcast.48), channel_id=1, replica_groups=mesh['grp'=2,'blk'=64] {'blk'}, dimensions={0} | all-to-all | bytes 262144 | tf_op jit(solution)/shard_map/all_to_all | solution.py:464
  113.5 6.9 %face_lookup.1.mine_ref = f32[128,128]{1,0:T(8,128)} custom-call(s32[1]{0:T(128)S(6)} %copy.17.live_ref, f32[256,128]{1,0:T(8,128)} %bitcast.41, s32[1,16384]{1,0:T(1,128)} %get-tuple-element.15.slot_ref), custom_call_target="tpu_custom_call" | custom-call | tf_op jit(solution)/shard_map/face_lookup/pallas_call | solution.py:355
  120.4 1.4 %collective-permute-start.4 = (f32[128,128]{1,0:T(8,128)}, f32[128,128]{1,0:T(8,128)S(1)}, u32[]{:S(2)}, u32[]{:S(2)}) collective-permute-start(f32[128,128]{1,0:T(8,128)} %face_lookup.1.mine_ref), channel_id=1, source_target_pairs={{0,64},{1,65},{2,66},{3,67},{4,68},{5,69},{6,70},{7,71},{8,72},{9,... | collective-permute-start | bytes 196616 | tf_op jit(solution)/shard_map/ppermute | solution.py:466
  121.8 1.1 collective-permute-done.4.other_ref
  123.5 7.4 %finish.1 = (f32[64,16384]{1,0:T(8,128)}, f32[2,16384]{1,0:T(2,128)}) custom-call(s32[3]{0:T(128)} %add_convert_fusion.flag_ref, f32[64,16384]{1,0:T(8,128)} %get-tuple-element.12.y_ref, f32[64,128]{1,0:T(8,128)} %get-tuple-element.13.coef_ref, f32[4,128,128]{2,1,0:T(8,128)} %bitcast.43, f32[2,128,128]{2,1,0:T(8,128)} %bitcast.47, ...), custom_call_target="tpu_custom_call" | custom-call | tf_op jit(solution)/shard_map/finish/pallas_call | solution.py:397
  (23 shorter events, 6.0 us)
Async XLA Ops:
  1.5 42.6 %collective-permute-start = (f32[64,4]{1,0:T(8,128)S(1)}, f32[64,4]{1,0:T(8,128)S(1)}, u32[]{:S(2)}, u32[]{:S(2)}) collective-permute-start(f32[64,4]{1,0:T(8,128)S(1)} %get-tuple-element.24), channel_id=1, source_target_pairs={{1,0},{2,1},{3,2},{4,3},{5,4},{6,5},{7,6},{8,7},{9,8},{10,9},{11,1... | collective-permute-start | bytes 3080 | tf_op jit(solution)/shard_map/ppermute | solution.py:432
  2.8 42.5 %collective-permute-start.1 = (f32[64,4]{1,0:T(8,128)S(1)}, f32[64,4]{1,0:T(8,128)S(1)}, u32[]{:S(2)}, u32[]{:S(2)}) collective-permute-start(f32[64,4]{1,0:T(8,128)S(1)} %get-tuple-element.25), channel_id=1, source_target_pairs={{0,1},{1,2},{2,3},{3,4},{4,5},{5,6},{6,7},{7,8},{8,9},{9,10},{10,1... | collective-permute-start | bytes 3080 | tf_op jit(solution)/shard_map/ppermute | solution.py:431
  49.0 25.4 %all-to-all-start = ((f32[64,1536,1]{1,2,0:T(1,128)}), f32[64,1536,1]{1,2,0:T(1,128)S(1)}, u32[]{:S(2)}, u32[]{:S(2)}) async-start(f32[64,1536,1]{1,2,0:T(1,128)} %bitcast.25), calls=%async_computation | async-start | bytes 786432 | tf_op jit(solution)/shard_map/all_to_all | solution.py:455
  72.8 13.4 %collective-permute-start.3 = (f32[656,128]{1,0:T(8,128)}, f32[656,128]{1,0:T(8,128)S(1)}, u32[]{:S(2)}, u32[]{:S(2)}) collective-permute-start(f32[656,128]{1,0:T(8,128)} %get-tuple-element.16), channel_id=1, source_target_pairs={{0,64},{1,65},{2,66},{3,67},{4,68},{5,69},{6,70},{7,71},{8,72},{9,... | collective-permute-start | bytes 1007624 | tf_op jit(solution)/shard_map/ppermute | solution.py:458
  74.3 0.7 copy-start
  83.9 4.1 %collective-permute-start.2 = (f32[136,128]{1,0:T(8,128)}, f32[136,128]{1,0:T(8,128)S(1)}, u32[]{:S(2)}, u32[]{:S(2)}) collective-permute-start(f32[136,128]{1,0:T(8,128)} %gather_sum.1.mine_ref), channel_id=1, source_target_pairs={{0,64},{1,65},{2,66},{3,67},{4,68},{5,69},{6,70},{7,71},{8,72},{9,... | collective-permute-start | bytes 208904 | tf_op jit(solution)/shard_map/ppermute | solution.py:462
  88.0 0.6 copy-start.1
  120.4 2.5 %collective-permute-start.4 = (f32[128,128]{1,0:T(8,128)}, f32[128,128]{1,0:T(8,128)S(1)}, u32[]{:S(2)}, u32[]{:S(2)}) collective-permute-start(f32[128,128]{1,0:T(8,128)} %face_lookup.1.mine_ref), channel_id=1, source_target_pairs={{0,64},{1,65},{2,66},{3,67},{4,68},{5,69},{6,70},{7,71},{8,72},{9,... | collective-permute-start | bytes 196616 | tf_op jit(solution)/shard_map/ppermute | solution.py:466
  122.9 0.6 copy-start.2

commit v2 on v1

v2 whole, which is shorter than its diff:
```python
import jax
import jax.numpy as jnp
from jax import lax
from jax.experimental import pallas as pl
from jax.experimental.pallas import tpu as pltpu
from jax.sharding import PartitionSpec as P

ITERS = 4
L = 128
HALO = ITERS
ROWS = 12
FACE_CHUNK = 2048
SLOT_STEP = 8

f32 = jnp.float32
bf16 = jnp.bfloat16
i32 = jnp.int32
HIGHEST = lax.Precision.HIGHEST
NT = (((1,), (1,)), ((), ()))
NN = (((1,), (0,)), ((), ()))


def iota(shape, dim):
    return lax.broadcasted_iota(i32, shape, dim)


def split(x):
    high = x.astype(bf16).astype(f32)
    return high, x - high


def dot(a, b, dims=NN, precision=None):
    return lax.dot_general(a, b, dims, precision=precision, preferred_element_type=f32)


def onehot(mask):
    return jnp.where(mask, 1.0, 0.0).astype(bf16)


def masked(mask, x):
    return jnp.where(mask, x, 0.0).astype(bf16)


def transposed(x):
    m, n = x.shape
    if n < L:
        x = jnp.concatenate([x, jnp.zeros((m, L - n), f32)], axis=1)
    if m < L:
        x = jnp.concatenate([x, jnp.zeros((L - m, L), f32)], axis=0)
    return x.T


def edge_of(patch, point, width):
    last = point >= width - 3
    return (
        jnp.where(last, patch + 1, jnp.where(point < 3, patch - 1, -1)),
        jnp.where(last, point - (width - 8), point),
    )


def route(width, blocks, capacity):
    c = FACE_CHUNK
    steps = width // c
    per = capacity // L
    highs = blocks * per
    sub = 256

    def kernel(
        live_ref,
        patch_ref,
        point_ref,
        impinged_ref,
        load_ref,
        side_ref,
        before_ref,
        after_ref,
        weight_ref,
        out_ref,
        slot_ref,
        carry,
        acc,
        eacc,
        weight,
        first_face,
        first_side,
    ):
        i = pl.program_id(0)
        gas = lax.axis_index("grp") == 0
        patch, point, side = patch_ref[...], point_ref[...], side_ref[...]

        @pl.when(i == 0)
        def _():
            carry[...] = jnp.zeros_like(carry)
            acc[...] = jnp.zeros_like(acc)
            eacc[...] = jnp.zeros_like(eacc)
            nl = side.shape[0]
            weight[...] = transposed(weight_ref[...])[:nl]
            first_face[0:1, :] = patch[:, :L]
            first_face[1:2, :] = point[:, :L]
            first_side[...] = side[:, :L]

        named = iota((blocks, c), 0) == patch
        hot = onehot(named)
        upto = onehot(iota((sub, sub), 0) <= iota((sub, sub), 1))
        before = carry[...]
        ranks = []
        for j in range(c // sub):
            cut = slice(j * sub, (j + 1) * sub)
            count = dot(hot[:, cut], upto)
            ranks.append(jnp.sum(jnp.where(named[:, cut], count + before, 0.0), axis=0, keepdims=True))
            before = before + count[:, sub - 1 : sub]
        carry[...] = before
        rank = jnp.concatenate(ranks, axis=1).astype(i32) - 1
        slot = patch * capacity + rank
        slot_ref[...] = slot

        lane = iota((1, c), 1)
        live = (lane + i * c) < live_ref[0]
        row = side[0:1]
        ahead = jnp.where(lane == c - 1, jnp.where(i == steps - 1, 0.0, after_ref[0:1, 0:1]), pltpu.roll(row, c - 1, 1))
        behind = jnp.where(lane == 0, jnp.where(i == 0, 0.0, before_ref[0:1, L - 1 : L]), pltpu.roll(row, 1, 1))
        flux = jnp.sum(weight[:, 0:1] * side, axis=0, keepdims=True) + 0.25 * (behind + ahead - 2.0 * row)
        crystal = impinged_ref[...].astype(f32) * load_ref[...]
        value = jnp.where(live, jnp.where(gas, flux, crystal), 0.0)
        v_high, v_low = split(value)
        t_high, t_low = ((point >> 7).astype(f32), (point & (L - 1)).astype(f32))
        high = onehot(iota((highs, c), 0) == (slot >> 7))
        low = iota((L, c), 0) == (slot & (L - 1))
        laid = jnp.concatenate([masked(low, x) for x in (v_high, v_low, t_high, t_low)], axis=0)
        placed = dot(high, laid, NT)
        for q in range(4):
            acc[pl.ds(q * highs, highs), :] += placed[:, q * L : (q + 1) * L]

        edge_patch, edge_point = edge_of(patch, point, width)
        edge_hot = onehot(iota((blocks, c), 0) == edge_patch)
        edge_low = iota((8, c), 0) == edge_point
        zeros = jnp.zeros((L - 16, c), bf16)
        edges = jnp.concatenate([masked(edge_low, v_high), masked(edge_low, v_low)], axis=0)
        eacc[...] += dot(edge_hot, jnp.concatenate([edges, zeros], axis=0), NT)

        @pl.when(i == steps - 1)
        def _():
            for r in range(per):
                part = [acc[pl.ds(q * highs + r, blocks, stride=per), :] for q in range(4)]
                out_ref[pl.ds(r, blocks, stride=ROWS), :] = part[0] + part[1]
                out_ref[pl.ds(per + r, blocks, stride=ROWS), :] = part[2] * float(L) + part[3]
            edge = eacc[...]
            spot, to = iota(edge.shape, 1), iota(edge.shape, 0)
            info = jnp.where(spot < 8, edge + pltpu.roll(edge, L - 8, 1), 0.0)
            info = jnp.where((spot == 8) & gas, first_side[0:1, 0:1], info)
            info = jnp.where((spot == 9) & gas, row[:, c - 1 :], info)
            ends = (
                (10, first_face[0:1, 0:1], first_face[1:2, 0:1], live_ref[0] > 0),
                (11, patch[:, c - 1 :], point[:, c - 1 :], live_ref[0] >= width),
            )
            for at, name, target, alive in ends:
                info = jnp.where(spot == at, jnp.where((to == name) & alive, target.astype(f32), -1.0), info)
                name, target = edge_of(name, target, width)
                info = jnp.where(spot == at + 2, jnp.where((to == name) & alive, target.astype(f32), -1.0), info)
            out_ref[pl.ds(2 * per, blocks, stride=ROWS), :] = info
            block = lax.axis_index("blk")
            half = spot[:1] < L // 2
            left, right = transposed(first_side[...]), transposed(side[:, c - L :])
            for r in range(2):
                rows = []
                for ends, base in ((left, 0), (right, L - HALO)):
                    j = base + 2 * r
                    rows.append(jnp.where(half, ends[j : j + 1], pltpu.roll(ends[j + 1 : j + 2], L // 2, 1)))
                sent = jnp.where(to == block - 1, rows[0], jnp.where(to == block + 1, rows[1], 0.0))
                out_ref[pl.ds(2 * per + 1 + r, blocks, stride=ROWS), :] = sent
            for r in range(2 * per + 3, ROWS):
                out_ref[pl.ds(r, blocks, stride=ROWS), :] = jnp.zeros((blocks, L), f32)

    def call(live_count, patch, point, impinged, load, side, weights):
        nl = side.shape[0]
        row = pl.BlockSpec((1, c), lambda i: (0, i))
        return pl.pallas_call(
            kernel,
            grid=(steps,),
            in_specs=[
                pl.BlockSpec(memory_space=pltpu.SMEM),
                row,
                row,
                row,
                row,
                pl.BlockSpec((nl, c), lambda i: (0, i)),
                pl.BlockSpec((8, L), lambda i: (0, jnp.maximum(i * (c // L) - 1, 0))),
                pl.BlockSpec((8, L), lambda i: (0, jnp.minimum((i + 1) * (c // L), width // L - 1))),
                pl.BlockSpec(weights.shape, lambda i: (0, 0)),
            ],
            out_specs=[pl.BlockSpec((blocks * ROWS, L), lambda i: (0, 0)), row],
            out_shape=[
                jax.ShapeDtypeStruct((blocks * ROWS, L), f32),
                jax.ShapeDtypeStruct((1, width), i32),
            ],
            scratch_shapes=[
                pltpu.VMEM((blocks, 1), f32),
                pltpu.VMEM((4 * highs, L), f32),
                pltpu.VMEM((blocks, L), f32),
                pltpu.VMEM((nl, L), f32),
                pltpu.VMEM((8, L), i32),
                pltpu.VMEM((nl, L), f32),
            ],
            name="route",
        )(live_count, patch, point, impinged, load, side, side, side, weights)

    return call


def matrices(nl, width):
    c = FACE_CHUNK
    steps = width // c
    out_rows = nl + 8
    tail = (ITERS + 1) * width // L

    def kernel(op_ref, weight_ref, side_ref, y_ref, rows_ref, coef_ref, lhs):
        i = pl.program_id(0)

        @pl.when(i == 0)
        def _():
            gas = lax.axis_index("grp") == 0
            coupling = transposed(weight_ref[...])[:nl, 1:2]
            one = op_ref[...]
            two = dot(one, one, precision=HIGHEST)
            three = dot(two, one, precision=HIGHEST)
            four = dot(two, two, precision=HIGHEST)
            main = jnp.where(gas, one, four)
            unit = jnp.where(iota((1, nl), 1) == 0, 1.0, 0.0)
            full = jnp.concatenate([main, unit, one[0:1], two[0:1], three[0:1], four[0:1], jnp.zeros((3, nl), f32)], axis=0)
            high, low = split(full)
            lhs[...] = jnp.concatenate([high, low, high, low], axis=1).astype(bf16)
            rows_ref[pl.ds(tail, 8), :] = jnp.concatenate([full[nl:], jnp.zeros((8, L - nl), f32)], axis=1)
            lead = [jnp.broadcast_to(m[0:1, 0:1], (1, L)) for m in (one, two, three, four)]
            rows_ref[pl.ds(tail + 8, 8), :] = jnp.concatenate(lead + [jnp.zeros((4, L), f32)], axis=0)
            lane = iota((nl, L), 1)
            coef = jnp.where(lane == 0, jnp.where(gas, coupling, four[:, 0:1]), 0.0)
            for k, m in ((1, three), (2, two), (3, one)):
                coef = jnp.where(lane == k, jnp.where(gas, 0.0, m[:, 0:1]), coef)
            coef_ref[...] = coef

        high, low = split(side_ref[...])
        high, low = high.astype(bf16), low.astype(bf16)
        out = dot(lhs[...], jnp.concatenate([high, high, low, low], axis=0))
        y_ref[...] = out[:nl]
        for n in range(ITERS + 1):
            part = [out[nl + n : nl + n + 1, k * L : (k + 1) * L] for k in range(c // L)]
            start = pl.multiple_of(n * (width // L) + i * (c // L), 8)
            rows_ref[pl.ds(start, c // L), :] = jnp.concatenate(part, axis=0)

    def call(op, weights, side):
        return pl.pallas_call(
            kernel,
            grid=(steps,),
            in_specs=[
                pl.BlockSpec((nl, nl), lambda i: (0, 0)),
                pl.BlockSpec(weights.shape, lambda i: (0, 0)),
                pl.BlockSpec((nl, c), lambda i: (0, i)),
            ],
            out_specs=[
                pl.BlockSpec((nl, c), lambda i: (0, i)),
                pl.BlockSpec((tail + 16, L), lambda i: (0, 0)),
                pl.BlockSpec((nl, L), lambda i: (0, 0)),
            ],
            out_shape=[
                jax.ShapeDtypeStruct((nl, width), f32),
                jax.ShapeDtypeStruct((tail + 16, L), f32),
                jax.ShapeDtypeStruct((nl, L), f32),
            ],
            scratch_shapes=[pltpu.VMEM((out_rows, 4 * nl), bf16)],
            name="matrices",
        )(op, weights, side)

    return call


def gather_sum(width, blocks, capacity):
    per = capacity // L
    tall = width // L

    def kernel(x_ref, out_ref, acc):
        def step(s, nothing):
            start = pl.multiple_of(s * SLOT_STEP * ROWS, 8)
            x = x_ref[pl.ds(start, SLOT_STEP * ROWS), :]
            v_high, v_low = split(x)
            t = x.astype(i32)
            t_high, t_low = t >> 7, t & (L - 1)
            highs, lows = [], []
            for m in range(SLOT_STEP):
                for r in range(per):
                    a, b = m * ROWS + r, m * ROWS + per + r
                    highs.append(onehot(iota((tall, L), 0) == t_high[b : b + 1]))
                    low = iota((L, L), 0) == t_low[b : b + 1]
                    lows.append(jnp.concatenate([masked(low, v_high[a : a + 1]), masked(low, v_low[a : a + 1])], axis=0))
            acc[...] += dot(jnp.concatenate(highs, axis=1), jnp.concatenate(lows, axis=1), NT)
            return nothing

        info = x_ref[pl.ds(2 * per, blocks, stride=ROWS), :]
        across = transposed(info)
        lane = iota((1, L), 1)
        left = lane < blocks

        def ends(a, b):
            return jnp.where(left, a, pltpu.roll(b, blocks, 1))

        value = 0.25 * ends(pltpu.roll(across[9:10], 1, 1), pltpu.roll(across[8:9], L - 1, 1))
        target = ends(across[10:11], across[11:12]).astype(i32)
        halo = ends(across[12:13], across[13:14]).astype(i32)
        v_high, v_low = split(value)
        low = iota((L, L), 0) == (target & (L - 1))
        high = onehot(iota((tall, L), 0) == (target >> 7))
        acc[...] = dot(high, jnp.concatenate([masked(low, v_high), masked(low, v_low)], axis=0), NT)
        at = onehot(iota((L, L), 0) == halo)
        pieces = jnp.concatenate([v_high, v_low, jnp.zeros((6, L), f32)], axis=0).astype(bf16)
        edge = jnp.sum(dot(pieces, at, NT), axis=0, keepdims=True)
        edge = edge + jnp.where(lane < 8, jnp.sum(info, axis=0, keepdims=True), 0.0)

        lax.fori_loop(0, blocks // SLOT_STEP, step, 0)
        out_ref[pl.ds(0, tall), :] = acc[:, :L] + acc[:, L:]
        block, source = lax.axis_index("blk"), iota((blocks, L), 0)
        rows = [edge]
        for near in (block - 1, block + 1):
            for r in range(2):
                columns = x_ref[pl.ds(2 * per + 1 + r, blocks, stride=ROWS), :]
                rows.append(jnp.sum(jnp.where(source == near, columns, 0.0), axis=0, keepdims=True))
        out_ref[pl.ds(tall, 8), :] = jnp.concatenate(rows + [jnp.zeros((3, L), f32)], axis=0)

    def call(x):
        return pl.pallas_call(
            kernel,
            out_shape=jax.ShapeDtypeStruct((tall + 8, L), f32),
            scratch_shapes=[pltpu.VMEM((tall, 2 * L), f32)],
            name="gather_sum",
        )(x)

    return call


def surface_lookup(width, blocks, capacity):
    per = capacity // L
    tall = width // L
    ext = tall + 16

    def kernel(mine_ref, other_ref, rows_ref, film_ref, x_ref, out_ref, source_ref, surface_ref):
        gas = lax.axis_index("grp") == 0
        block = lax.axis_index("blk")
        lane, line = iota((ext, L), 1), iota((ext, L), 0)
        inside = (line >= 8) & (line < tall + 8)
        left = (line == 7) & (lane >= L - HALO)
        right = (line == tall + 8) & (lane < HALO)
        valid = inside | (left & (block > 0)) | (right & (block < blocks - 1))

        def extend(body, edge_left, edge_right):
            zeros = jnp.zeros((7, L), f32)
            full = jnp.concatenate([zeros, edge_left, body, edge_right, zeros], axis=0)
            return jnp.where(valid, full, 0.0)

        def lateral(x):
            ahead = pltpu.roll(x, L - 1, 1)
            ahead = jnp.where(lane == L - 1, pltpu.roll(ahead, ext - 1, 0), ahead)
            behind = pltpu.roll(x, 1, 1)
            behind = jnp.where(lane == 0, pltpu.roll(behind, 1, 0), behind)
            return behind + ahead - 2.0 * x

        mine, other = mine_ref[...], other_ref[...]
        heat, mass = jnp.where(gas, mine, other), jnp.where(gas, other, mine)
        q = heat - 0.5 * mass
        q_edge = q[tall : tall + 1]
        q = extend(q[:tall], pltpu.roll(q_edge, L - 8, 1), q_edge)
        tail = (ITERS + 1) * tall
        lead = rows_ref[pl.ds(tail + 8, 8), :]
        near = jnp.where(gas, other[tall:], mine[tall:])
        half = lane[:1] < L // 2

        def columns(a):
            for x in (near[a : a + 1], near[a + 1 : a + 2]):
                yield jnp.where(half, x, 0.0)
                yield jnp.where(half, pltpu.roll(x, L // 2, 1), 0.0)

        gap = jnp.zeros((L - 2 * HALO, L), f32)
        halo = jnp.concatenate([*columns(3), gap, *columns(1)], axis=0)
        halo = dot(rows_ref[pl.ds(tail, 8), :], halo, NT, precision=HIGHEST)

        def base(n):
            edge = halo[n : n + 1]
            return extend(rows_ref[pl.ds(n * tall, tall), :], edge, edge)

        sources = []
        row = base(0)
        for n in range(1, ITERS + 1):
            sources.append(0.2 * (q + 0.5 * lateral(row)))
            row = base(n)
            for j, source in enumerate(sources):
                row = row + lead[n - 1 - j : n - j] * source
            row = jnp.where(valid, row, 0.0)
        for n in range(ITERS):
            source_ref[pl.ds(n * tall, tall), :] = sources[n][8 : tall + 8]
        wall_row = row[8 : tall + 8]
        film_new = jnp.maximum(film_ref[...] + 0.5 * (wall_row - 0.3) - 0.1 * mass[:tall], 0.0)
        surface_ref[pl.ds(0, tall), :] = wall_row
        surface_ref[pl.ds(tall, tall), :] = film_new

        high, low = split(jnp.where(gas, wall_row, film_new).T)
        table = jnp.concatenate([high, low], axis=1).astype(bf16)

        def step(s, carry):
            start = pl.multiple_of(s * SLOT_STEP * ROWS, 8)
            t = x_ref[pl.ds(start, SLOT_STEP * ROWS), :].astype(i32)
            t_high, t_low = t >> 7, t & (L - 1)
            rows = [m * ROWS + per + r for m in range(SLOT_STEP) for r in range(per)]
            highs = jnp.concatenate([onehot(iota((tall, L), 0) == t_high[b : b + 1]) for b in rows], axis=1)
            found = dot(table, jnp.concatenate([highs, highs], axis=0))
            picked = []
            for k, b in enumerate(rows):
                low = iota((L, L), 0) == t_low[b : b + 1]
                picked.append(jnp.sum(jnp.where(low, found[:, k * L : (k + 1) * L], 0.0), axis=0, keepdims=True))
            size = SLOT_STEP * per
            out_ref[pl.ds(pl.multiple_of(s * size, 8), size), :] = jnp.concatenate(picked, axis=0)
            return carry

        lax.fori_loop(0, blocks // SLOT_STEP, step, 0)

    def call(mine, other, rows, film, x):
        vmem = pl.BlockSpec(memory_space=pltpu.VMEM)
        return pl.pallas_call(
            kernel,
            in_specs=[vmem] * 5,
            out_shape=[
                jax.ShapeDtypeStruct((blocks * per, L), f32),
                jax.ShapeDtypeStruct((ITERS * tall, L), f32),
                jax.ShapeDtypeStruct((2 * tall, L), f32),
            ],
            name="surface_lookup",
        )(mine, other, rows, film, x)

    return call


def face_finish(nl, width, blocks, capacity):
    c = FACE_CHUNK
    steps = width // c
    tall = width // L
    part = c // L
    highs = blocks * capacity // L

    def kernel(live_ref, reply_ref, slot_ref, y_ref, coef_ref, source_ref, surface_ref, out_ref, found_ref, rows_ref, table):
        i = pl.program_id(0)
        gas = lax.axis_index("grp") == 0

        @pl.when(i == 0)
        def _():
            high, low = split(reply_ref[...].T)
            table[...] = jnp.concatenate([high, low], axis=1).astype(bf16)

        slot = slot_ref[...]
        hot = onehot(iota((highs, c), 0) == (slot >> 7))
        found = dot(table[...], jnp.concatenate([hot, hot], axis=0))
        low = iota((L, c), 0) == (slot & (L - 1))
        live = (iota((1, c), 1) + i * c) < live_ref[0]
        picked = jnp.where(live, jnp.sum(jnp.where(low, found, 0.0), axis=0, keepdims=True), 0.0)
        found_ref[...] = picked

        coef = coef_ref[...]
        spread = [jnp.broadcast_to(coef[:, n : n + 1], (nl, L)) for n in range(ITERS)]
        first = []
        for k in range(part):
            cut = slice(k * L, (k + 1) * L)
            lead = jnp.where(gas, picked[:, cut], source_ref[0, k : k + 1])
            total = y_ref[:, cut] + spread[0] * lead
            for n in range(1, ITERS):
                total = total + spread[n] * source_ref[n, k : k + 1]
            out_ref[:, cut] = total
            rows_ref[0:1, cut] = jnp.where(gas, picked[:, cut], surface_ref[0, k : k + 1])
            rows_ref[1:2, cut] = surface_ref[1, k : k + 1]

    def call(live_count, reply, slot, y, coef, source, surface):
        row = pl.BlockSpec((1, c), lambda i: (0, i))
        wide = pl.BlockSpec((nl, c), lambda i: (0, i))
        return pl.pallas_call(
            kernel,
            grid=(steps,),
            in_specs=[
                pl.BlockSpec(memory_space=pltpu.SMEM),
                pl.BlockSpec((highs, L), lambda i: (0, 0)),
                row,
                wide,
                pl.BlockSpec((nl, L), lambda i: (0, 0)),
                pl.BlockSpec((ITERS, part, L), lambda i: (0, i, 0)),
                pl.BlockSpec((2, part, L), lambda i: (0, i, 0)),
            ],
            out_specs=[wide, row, pl.BlockSpec((2, c), lambda i: (0, i))],
            out_shape=[
                jax.ShapeDtypeStruct((nl, width), f32),
                jax.ShapeDtypeStruct((1, width), f32),
                jax.ShapeDtypeStruct((2, width), f32),
            ],
            scratch_shapes=[pltpu.VMEM((L, 2 * highs), bf16)],
            name="face_finish",
        )(live_count, reply, slot, y, coef, source.reshape(ITERS, tall, L), surface.reshape(2, tall, L))

    return call


def local(columns, operators, normal_weights, face_patch, face_point, live_count, impinged, crystal_load, film):
    nl, width = columns.shape[1:]
    blocks = lax.axis_size("blk")
    capacity = 2 * width // blocks
    per = capacity // L
    gas = lax.axis_index("grp") == 0
    side, matrix = columns[0], operators[0]
    swap = [(i, blocks + i) for i in range(blocks)] + [(blocks + i, i) for i in range(blocks)]

    def across(x):
        return lax.ppermute(x, ("grp", "blk"), swap)

    def exchange(x):
        return lax.all_to_all(x.reshape(-1), "blk", split_axis=0, concat_axis=0, tiled=True).reshape(x.shape)

    faces = [x.reshape(1, width) for x in (face_patch, face_point, impinged, crystal_load)]
    message, slot = route(width, blocks, capacity)(live_count, *faces, side, normal_weights)
    arrived = exchange(message)
    y, rows, coef = matrices(nl, width)(matrix, normal_weights, side)
    rows = jnp.where(gas, across(rows), rows)

    mine = gather_sum(width, blocks, capacity)(arrived)
    film = film.reshape(width // L, L)
    replies, source, surface = surface_lookup(width, blocks, capacity)(mine, across(mine), rows, film, arrived)
    returned = exchange(replies)
    new_columns, found, surface = face_finish(nl, width, blocks, capacity)(live_count, returned, slot, y, coef, source, surface)
    bottom = lax.broadcasted_iota(i32, surface.shape, 0) == 1
    surface = jnp.where(gas & bottom, across(found), surface)
    return new_columns[None], surface[None]


def solution(mesh):
    return jax.shard_map(
        local,
        mesh=mesh,
        in_specs=(
            P("grp", None, "blk"),
            P("grp", None, None),
            P(),
            P("blk", None),
            P("blk"),
            P("blk"),
            P("blk"),
            P("blk"),
            P("blk"),
        ),
        out_specs=(P("grp", None, "blk"), P("grp", None, "blk")),
        check_vma=False,
    )
```

time: 132 us -> 89.9 us (0.68)
  between operations: 15.2 us -> 1.3 us
  starting transfers between devices: 26.5 us -> 16.7 us
  local copies, waits for them, and re-layouts: 10.7 us -> 1.37 us
  other arithmetic: 8.87 us -> 3.47 us
  Pallas kernels: 51.9 us -> 48.8 us
    pallas_call x4 -> x2, Pallas kernels: 34.8 us -> 22.8 us  [call(): pl.pallas_call(kernel, grid=(steps,), in_specs=[pl.BlockSpec(memory_space...]
    pallas_call x1 -> x2, Pallas kernels: 8.36 us -> 16.8 us  [the longest x1 8.63 us: call(): pl.pallas_call(kernel, in_specs=[vmem] * 5, out_shape=[jax.ShapeDtypeStru...]
    slice x7 -> x0, local copies, waits for them, and re-layouts: 7.26 us -> none  [the longest x3 3.78 us: local(): where, name, spot = (slot[0, f], patch[0, f], point[0, f])]
    ppermute x5 -> x3, starting transfers between devices: 11.5 us -> 4.71 us  [across(): return lax.ppermute(x, ('grp', 'blk'), swap)]
    all_to_all x1, starting transfers between devices: 15 us -> 12 us  [exchange(): lax.all_to_all(x.reshape(-1), 'blk', split_axis=0, concat_axis=0, tiled=T...]
    add x1 -> x0, other arithmetic: 2.34 us -> none  [local(): message = message + jnp.where((lines == line) & (lanes == at), amount, 0.0)]
    select_n x3 -> x1, other arithmetic: 4.11 us -> 1.77 us  [local(): rows = jnp.where(gas, across(rows), rows)]
    broadcast_in_dim x0 -> x1, other arithmetic: none -> 1.69 us  [local(): return (new_columns[None], surface[None])]
  transfers between devices with their start and end apart: 6 -> 4, of which waited for: 1 -> 2; matrix products, arithmetic and copies ran while one was open for 11% -> 2% of each run, Pallas kernels for 22% -> 19%
where the time goes in v2:
time: 89.9 us; the launch traced here: 89.2 us
  Pallas kernels  48.8 us (54%)
  starting transfers between devices  16.7 us (19%)
  blocking collectives  15.3 us (17%)
  other arithmetic  3.47 us (4%)
  waiting for transfers between devices  2.36 us (3%)
  local copies, waits for them, and re-layouts  1.37 us (2%)
  between operations  1.3 us (1%)
    pallas_call x2, Pallas kernels, call(): pl.pallas_call(kernel, grid=(steps,), in_specs=[pl.BlockSpec(memory_space...  22.8 us
    all_to_all x1, blocking collectives, exchange(): lax.all_to_all(x.reshape(-1), 'blk', split_axis=0, concat_axis=0, tiled=T...  15.3 us
    all_to_all x1, starting transfers between devices, exchange(): lax.all_to_all(x.reshape(-1), 'blk', split_axis=0, concat_axis=0, tiled=T...  12 us
    pallas_call x1, Pallas kernels, call(): pl.pallas_call(kernel, out_shape=jax.ShapeDtypeStruct((tall + 8, L), f32)...  9.12 us
    pallas_call x1, Pallas kernels, call(): pl.pallas_call(kernel, in_specs=[vmem] * 5, out_shape=[jax.ShapeDtypeStru...  8.63 us
    pallas_call x1, Pallas kernels, call(): pl.pallas_call(kernel, grid=(steps,), in_specs=[pl.BlockSpec((nl, nl), la...  8.19 us
    ppermute x3, starting transfers between devices, across(): return lax.ppermute(x, ('grp', 'blk'), swap)  4.71 us
  transfers between devices with their start and end apart: 4, of which 2 were waited for; matrix products, arithmetic and copies ran while one was open for 2% of the time, Pallas kernels for 19%

profile of v2, /device:TPU:1, one launch (start us, length us, event | category | flops | bytes accessed | tf_op | source)
XLA Modules:
  0.0 89.2 jit_solution(14063450123613831890)
XLA Ops:
  1.3 13.0 %route.1 = (f32[768,128]{1,0:T(8,128)}, s32[1,16384]{1,0:T(1,128)}) custom-call(s32[1]{0:T(128)S(6)} %copy.13.live_ref, s32[1,16384]{1,0:T(1,128)} %bitcast.28, s32[1,16384]{1,0:T(1,128)} %bitcast.29, s32[1,16384]{1,0:T(1,128)} %bitcast.30, f32[1,16384]{1,0:T(1,128)} %bitcast.31, f32[64,16384]{1,0:T(8,128)} %bitcast.17, f32[64,16384]{1,0:T(8,128)} %bitcast.18, ...), custom_call_target="tpu_custom_call" | custom-call | tf_op jit(solution)/shard_map/route/pallas_call | solution.py:177
  14.3 12.0 %all-to-all-start = ((f32[64,1536,1]{1,2,0:T(1,128)}), f32[64,1536,1]{1,2,0:T(1,128)S(1)}, u32[]{:S(2)}, u32[]{:S(2)}) async-start(f32[64,1536,1]{1,2,0:T(1,128)} %bitcast.24), calls=%async_computation | async-start | bytes 786432 | tf_op jit(solution)/shard_map/all_to_all | solution.py:516
  26.3 8.2 %matrices.1 = (f32[64,16384]{1,0:T(8,128)}, f32[656,128]{1,0:T(8,128)}, f32[64,128]{1,0:T(8,128)}) custom-call(f32[64,64]{1,0:T(8,128)} %bitcast.34, f32[2,64]{1,0:T(2,128)} %weight_ref.3, f32[64,16384]{1,0:T(8,128)} %bitcast.20), custom_call_target="tpu_custom_call" | custom-call | tf_op jit(solution)/shard_map/matrices/pallas_call | solution.py:251
  34.5 1.0 %collective-permute-start.1 = (f32[656,128]{1,0:T(8,128)}, f32[656,128]{1,0:T(8,128)S(1)}, u32[]{:S(2)}, u32[]{:S(2)}) collective-permute-start(f32[656,128]{1,0:T(8,128)} %get-tuple-element.14), channel_id=1, source_target_pairs={{0,64},{1,65},{2,66},{3,67},{4,68},{5,69},{6,70},{7,71},{8,72},{9,... | collective-permute-start | bytes 1007624 | tf_op jit(solution)/shard_map/ppermute | solution.py:513
  35.4 1.2 %all-to-all-done = f32[64,1536,1]{1,2,0:T(1,128)S(1)} async-done(((f32[64,1536,1]{1,2,0:T(1,128)}), f32[64,1536,1]{1,2,0:T(1,128)S(1)}, u32[]{:S(2)}, u32[]{:S(2)}) %all-to-all-start) | async-done | bytes 393248 | tf_op jit(solution)/shard_map/all_to_all | solution.py:516
  36.7 0.0 copy-start
  36.7 0.7 copy-done
  37.4 9.1 %gather_sum.1.mine_ref = f32[136,128]{1,0:T(8,128)} custom-call(f32[768,128]{1,0:T(8,128)} %bitcast.21), custom_call_target="tpu_custom_call" | custom-call | tf_op jit(solution)/shard_map/gather_sum/pallas_call | solution.py:328
  46.5 2.3 %collective-permute-start = (f32[136,128]{1,0:T(8,128)}, f32[136,128]{1,0:T(8,128)S(1)}, u32[]{:S(2)}, u32[]{:S(2)}) collective-permute-start(f32[136,128]{1,0:T(8,128)} %gather_sum.1.mine_ref), channel_id=1, source_target_pairs={{0,64},{1,65},{2,66},{3,67},{4,68},{5,69},{6,70},{7,71},{8,72},{9,... | collective-permute-start | bytes 208904 | tf_op jit(solution)/shard_map/ppermute | solution.py:513
  48.9 0.0 collective-permute-done.1
  48.9 1.8 %broadcast_select_fusion.rows_ref = f32[656,128]{1,0:T(8,128)} fusion(f32[656,128]{1,0:T(8,128)S(1)} %collective-permute-done.1, f32[656,128]{1,0:T(8,128)} %get-tuple-element.14, pred[]{:T(512)S(6)} %eq.10), kind=kLoop, calls=%fused_computation | loop fusion | flops 83968 | bytes 1007617 | tf_op jit(solution)/shard_map/jit(_where)/select_n | solution.py:522
  50.6 0.0 collective-permute-done.other_ref
  50.6 0.0 copy-start.1
  50.6 0.6 copy-done.1
  51.3 8.6 %surface_lookup.1 = (f32[256,128]{1,0:T(8,128)}, f32[512,128]{1,0:T(8,128)}, f32[256,128]{1,0:T(8,128)}) custom-call(f32[136,128]{1,0:T(8,128)} %gather_sum.1.mine_ref, f32[136,128]{1,0:T(8,128)} %copy-done.1, f32[656,128]{1,0:T(8,128)} %broadcast_select_fusion.rows_ref, f32[128,128]{1,0:T(8,128)} %bitcast.32, f32[768,128]{1,0:T(8,128)} %bitcast.22), custom_call_target="tpu_custom_call" | custom-call | tf_op jit(solution)/shard_map/surface_lookup/pallas_call | solution.py:424
  59.9 15.3 %all_to_all.18 = f32[64,512,1]{1,2,0:T(1,128)} all-to-all(f32[64,512,1]{1,2,0:T(1,128)} %bitcast.27), channel_id=1, replica_groups=mesh['grp'=2,'blk'=64] {'blk'}, dimensions={0} | all-to-all | bytes 262144 | tf_op jit(solution)/shard_map/all_to_all | solution.py:516
  75.2 9.8 %face_finish.1 = (f32[64,16384]{1,0:T(8,128)}, f32[1,16384]{1,0:T(1,128)}, f32[2,16384]{1,0:T(2,128)}) custom-call(s32[1]{0:T(128)S(6)} %copy.13.live_ref, f32[256,128]{1,0:T(8,128)} %bitcast.23, s32[1,16384]{1,0:T(1,128)} %get-tuple-element.16.slot_ref, f32[64,16384]{1,0:T(8,128)} %get-tuple-element.17.y_ref, f32[64,128]{1,0:T(8,128)} %get-tuple-element.18.coef_ref, ...), custom_call_target="tpu_custom_call" | custom-call | tf_op jit(solution)/shard_map/face_finish/pallas_call | solution.py:478
  85.0 1.4 %collective-permute-start.2 = (f32[1,16384]{1,0:T(1,128)}, f32[1,16384]{1,0:T(1,128)S(1)}, u32[]{:S(2)}, u32[]{:S(2)}) collective-permute-start(f32[1,16384]{1,0:T(1,128)} %get-tuple-element.22), channel_id=1, source_target_pairs={{0,64},{1,65},{2,66},{3,67},{4,68},{5,69},{6,70},{7,71},{8,72},{9,... | collective-permute-start | bytes 196616 | tf_op jit(solution)/shard_map/ppermute | solution.py:513
  86.4 1.1 %collective-permute-done.2 = f32[1,16384]{1,0:T(1,128)S(1)} collective-permute-done((f32[1,16384]{1,0:T(1,128)}, f32[1,16384]{1,0:T(1,128)S(1)}, u32[]{:S(2)}, u32[]{:S(2)}) %collective-permute-start.2) | collective-permute-done | bytes 65568 | tf_op jit(solution)/shard_map/ppermute | solution.py:513
  87.6 1.7 %select_bitcast_fusion = f32[1,2,16384]{2,1,0:T(2,128)} fusion(f32[2,16384]{1,0:T(2,128)} %get-tuple-element.23, pred[2]{0:T(512)(128)(4,1)S(1)} %compare_and_fusion, f32[16384]{0:T(1024)S(1)} %bitcast.33), kind=kLoop, calls=%fused_computation.1 | loop fusion | flops 32768 | bytes 327682 | tf_op jit(solution)/shard_map/broadcast_in_dim | solution.py:531
  (1 shorter events, 0.0 us)
Async XLA Ops:
  14.3 22.4 %all-to-all-start = ((f32[64,1536,1]{1,2,0:T(1,128)}), f32[64,1536,1]{1,2,0:T(1,128)S(1)}, u32[]{:S(2)}, u32[]{:S(2)}) async-start(f32[64,1536,1]{1,2,0:T(1,128)} %bitcast.24), calls=%async_computation | async-start | bytes 786432 | tf_op jit(solution)/shard_map/all_to_all | solution.py:516
  34.5 14.4 %collective-permute-start.1 = (f32[656,128]{1,0:T(8,128)}, f32[656,128]{1,0:T(8,128)S(1)}, u32[]{:S(2)}, u32[]{:S(2)}) collective-permute-start(f32[656,128]{1,0:T(8,128)} %get-tuple-element.14), channel_id=1, source_target_pairs={{0,64},{1,65},{2,66},{3,67},{4,68},{5,69},{6,70},{7,71},{8,72},{9,... | collective-permute-start | bytes 1007624 | tf_op jit(solution)/shard_map/ppermute | solution.py:513
  36.7 0.7 copy-start
  46.5 4.1 %collective-permute-start = (f32[136,128]{1,0:T(8,128)}, f32[136,128]{1,0:T(8,128)S(1)}, u32[]{:S(2)}, u32[]{:S(2)}) collective-permute-start(f32[136,128]{1,0:T(8,128)} %gather_sum.1.mine_ref), channel_id=1, source_target_pairs={{0,64},{1,65},{2,66},{3,67},{4,68},{5,69},{6,70},{7,71},{8,72},{9,... | collective-permute-start | bytes 208904 | tf_op jit(solution)/shard_map/ppermute | solution.py:513
  50.6 0.6 copy-start.1
  85.0 2.5 %collective-permute-start.2 = (f32[1,16384]{1,0:T(1,128)}, f32[1,16384]{1,0:T(1,128)S(1)}, u32[]{:S(2)}, u32[]{:S(2)}) collective-permute-start(f32[1,16384]{1,0:T(1,128)} %get-tuple-element.22), channel_id=1, source_target_pairs={{0,64},{1,65},{2,66},{3,67},{4,68},{5,69},{6,70},{7,71},{8,72},{9,... | collective-permute-start | bytes 196616 | tf_op jit(solution)/shard_map/ppermute | solution.py:513

commit v3 on v2

--- a/solution.py
+++ b/solution.py
@@ -8,7 +8,7 @@
 ITERS = 4
 L = 128
 HALO = ITERS
-ROWS = 12
+ROWS = 11
 FACE_CHUNK = 2048
 SLOT_STEP = 8
 
@@ -33,12 +33,34 @@
     return lax.dot_general(a, b, dims, precision=precision, preferred_element_type=f32)
 
 
+def counter(count, n):
+    return jnp.concatenate([iota((count, L), 0).astype(f32).astype(bf16)] * (n // L), axis=1)
+
+
+def spread(x):
+    return jnp.broadcast_to(x, (16, x.shape[1])).astype(bf16)
+
+
+def halves(x):
+    rows = jnp.broadcast_to(x, (16, x.shape[1]))
+    high = rows.astype(bf16)
+    return high, (rows - high.astype(f32)).astype(bf16)
+
+
+def tiled(rows, count):
+    return jnp.concatenate([rows] * (count // 16), axis=0)
+
+
+def hits(x, count):
+    return counter(count, x.shape[1]) == tiled(spread(x), count)
+
+
 def onehot(mask):
-    return jnp.where(mask, 1.0, 0.0).astype(bf16)
-
-
-def masked(mask, x):
-    return jnp.where(mask, x, 0.0).astype(bf16)
+    return jnp.where(mask, jnp.ones(mask.shape, bf16), jnp.zeros(mask.shape, bf16))
+
+
+def masked(mask, rows):
+    return jnp.where(mask, tiled(rows, mask.shape[0]), jnp.zeros(mask.shape, bf16))
 
 
 def transposed(x):
@@ -79,6 +101,7 @@
         slot_ref,
         carry,
         acc,
+        spots,
         eacc,
         weight,
         first_face,
@@ -100,15 +123,17 @@
             first_side[...] = side[:, :L]
 
         named = iota((blocks, c), 0) == patch
-        hot = onehot(named)
-        upto = onehot(iota((sub, sub), 0) <= iota((sub, sub), 1))
+        hot = onehot(hits(patch.astype(f32), blocks))
+        wide = (sub, sub + L)
+        upto = jnp.where((iota(wide, 0) <= iota(wide, 1)) | (iota(wide, 1) >= sub), 1.0, 0.0).astype(bf16)
         before = carry[...]
         ranks = []
         for j in range(c // sub):
             cut = slice(j * sub, (j + 1) * sub)
             count = dot(hot[:, cut], upto)
-            ranks.append(jnp.sum(jnp.where(named[:, cut], count + before, 0.0), axis=0, keepdims=True))
-            before = before + count[:, sub - 1 : sub]
+            total = count[:, :sub] + jnp.concatenate([before] * (sub // L), axis=1)
+            ranks.append(jnp.sum(jnp.where(named[:, cut], total, 0.0), axis=0, keepdims=True))
+            before = before + count[:, sub:]
         carry[...] = before
         rank = jnp.concatenate(ranks, axis=1).astype(i32) - 1
         slot = patch * capacity + rank
@@ -124,29 +149,28 @@
         value = jnp.where(live, jnp.where(gas, flux, crystal), 0.0)
         v_high, v_low = split(value)
         t_high, t_low = ((point >> 7).astype(f32), (point & (L - 1)).astype(f32))
-        high = onehot(iota((highs, c), 0) == (slot >> 7))
-        low = iota((L, c), 0) == (slot & (L - 1))
-        laid = jnp.concatenate([masked(low, x) for x in (v_high, v_low, t_high, t_low)], axis=0)
-        placed = dot(high, laid, NT)
+        high = onehot(hits((slot >> 7).astype(f32), highs))
+        low = hits((slot & (L - 1)).astype(f32), L)
+        laid = jnp.concatenate([masked(low, x) for x in (*halves(value), spread(t_high), spread(t_low))], axis=0)
+        placed = dot(laid, high, NT)
         for q in range(4):
-            acc[pl.ds(q * highs, highs), :] += placed[:, q * L : (q + 1) * L]
+            acc[pl.ds(q * L, L), :] += placed[q * L : (q + 1) * L]
 
         edge_patch, edge_point = edge_of(patch, point, width)
-        edge_hot = onehot(iota((blocks, c), 0) == edge_patch)
+        edge_hot = onehot(hits(edge_patch.astype(f32), blocks))
         edge_low = iota((8, c), 0) == edge_point
-        zeros = jnp.zeros((L - 16, c), bf16)
-        edges = jnp.concatenate([masked(edge_low, v_high), masked(edge_low, v_low)], axis=0)
-        eacc[...] += dot(edge_hot, jnp.concatenate([edges, zeros], axis=0), NT)
+        edges = jnp.concatenate([jnp.where(edge_low, x, 0.0) for x in (v_high, v_low)], axis=0).astype(bf16)
+        eacc[...] += dot(edges, edge_hot, NT)
 
         @pl.when(i == steps - 1)
         def _():
+            spots[pl.ds(0, highs), :] = (acc[:L] + acc[L : 2 * L]).T
+            spots[pl.ds(highs, highs), :] = (acc[2 * L : 3 * L] * float(L) + acc[3 * L :]).T
             for r in range(per):
-                part = [acc[pl.ds(q * highs + r, blocks, stride=per), :] for q in range(4)]
-                out_ref[pl.ds(r, blocks, stride=ROWS), :] = part[0] + part[1]
-                out_ref[pl.ds(per + r, blocks, stride=ROWS), :] = part[2] * float(L) + part[3]
-            edge = eacc[...]
-            spot, to = iota(edge.shape, 1), iota(edge.shape, 0)
-            info = jnp.where(spot < 8, edge + pltpu.roll(edge, L - 8, 1), 0.0)
+                for q in range(2):
+                    out_ref[pl.ds(q * per + r, blocks, stride=ROWS), :] = spots[pl.ds(q * highs + r, blocks, stride=per), :]
+            spot, to = iota((blocks, L), 1), iota((blocks, L), 0)
+            info = transposed(eacc[0:8] + eacc[8:16])[:blocks]
             info = jnp.where((spot == 8) & gas, first_side[0:1, 0:1], info)
             info = jnp.where((spot == 9) & gas, row[:, c - 1 :], info)
             ends = (
@@ -168,8 +192,6 @@
                     rows.append(jnp.where(half, ends[j : j + 1], pltpu.roll(ends[j + 1 : j + 2], L // 2, 1)))
                 sent = jnp.where(to == block - 1, rows[0], jnp.where(to == block + 1, rows[1], 0.0))
                 out_ref[pl.ds(2 * per + 1 + r, blocks, stride=ROWS), :] = sent
-            for r in range(2 * per + 3, ROWS):
-                out_ref[pl.ds(r, blocks, stride=ROWS), :] = jnp.zeros((blocks, L), f32)
 
     def call(live_count, patch, point, impinged, load, side, weights):
         nl = side.shape[0]
@@ -194,9 +216,10 @@
                 jax.ShapeDtypeStruct((1, width), i32),
             ],
             scratch_shapes=[
-                pltpu.VMEM((blocks, 1), f32),
-                pltpu.VMEM((4 * highs, L), f32),
                 pltpu.VMEM((blocks, L), f32),
+                pltpu.VMEM((4 * L, highs), f32),
+                pltpu.VMEM((2 * highs, L), f32),
+                pltpu.VMEM((16, blocks), f32),
                 pltpu.VMEM((nl, L), f32),
                 pltpu.VMEM((8, L), i32),
                 pltpu.VMEM((nl, L), f32),
@@ -281,16 +304,15 @@
         def step(s, nothing):
             start = pl.multiple_of(s * SLOT_STEP * ROWS, 8)
             x = x_ref[pl.ds(start, SLOT_STEP * ROWS), :]
-            v_high, v_low = split(x)
             t = x.astype(i32)
-            t_high, t_low = t >> 7, t & (L - 1)
+            t_high, t_low = (t >> 7).astype(f32), (t & (L - 1)).astype(f32)
             highs, lows = [], []
             for m in range(SLOT_STEP):
                 for r in range(per):
                     a, b = m * ROWS + r, m * ROWS + per + r
-                    highs.append(onehot(iota((tall, L), 0) == t_high[b : b + 1]))
-                    low = iota((L, L), 0) == t_low[b : b + 1]
-                    lows.append(jnp.concatenate([masked(low, v_high[a : a + 1]), masked(low, v_low[a : a + 1])], axis=0))
+                    highs.append(onehot(hits(t_high[b : b + 1], tall)))
+                    low = hits(t_low[b : b + 1], L)
+                    lows.append(jnp.concatenate([masked(low, part) for part in halves(x[a : a + 1])], axis=0))
             acc[...] += dot(jnp.concatenate(highs, axis=1), jnp.concatenate(lows, axis=1), NT)
             return nothing
 
@@ -306,10 +328,10 @@
         target = ends(across[10:11], across[11:12]).astype(i32)
         halo = ends(across[12:13], across[13:14]).astype(i32)
         v_high, v_low = split(value)
-        low = iota((L, L), 0) == (target & (L - 1))
-        high = onehot(iota((tall, L), 0) == (target >> 7))
-        acc[...] = dot(high, jnp.concatenate([masked(low, v_high), masked(low, v_low)], axis=0), NT)
-        at = onehot(iota((L, L), 0) == halo)
+        low = hits((target & (L - 1)).astype(f32), L)
+        high = onehot(hits((target >> 7).astype(f32), tall))
+        acc[...] = dot(high, jnp.concatenate([masked(low, x) for x in halves(value)], axis=0), NT)
+        at = onehot(hits(halo.astype(f32), L))
         pieces = jnp.concatenate([v_high, v_low, jnp.zeros((6, L), f32)], axis=0).astype(bf16)
         edge = jnp.sum(dot(pieces, at, NT), axis=0, keepdims=True)
         edge = edge + jnp.where(lane < 8, jnp.sum(info, axis=0, keepdims=True), 0.0)
@@ -340,7 +362,7 @@
     tall = width // L
     ext = tall + 16
 
-    def kernel(mine_ref, other_ref, rows_ref, film_ref, x_ref, out_ref, source_ref, surface_ref):
+    def kernel(mine_ref, other_ref, rows_mine, rows_other, film_ref, x_ref, out_ref, source_ref, surface_ref):
         gas = lax.axis_index("grp") == 0
         block = lax.axis_index("blk")
         lane, line = iota((ext, L), 1), iota((ext, L), 0)
@@ -367,7 +389,12 @@
         q_edge = q[tall : tall + 1]
         q = extend(q[:tall], pltpu.roll(q_edge, L - 8, 1), q_edge)
         tail = (ITERS + 1) * tall
-        lead = rows_ref[pl.ds(tail + 8, 8), :]
+
+        def rows(start, size):
+            cut = pl.ds(start, size)
+            return jnp.where(gas, rows_other[cut, :], rows_mine[cut, :])
+
+        lead = rows(tail + 8, 8)
         near = jnp.where(gas, other[tall:], mine[tall:])
         half = lane[:1] < L // 2
 
@@ -378,11 +405,11 @@
 
         gap = jnp.zeros((L - 2 * HALO, L), f32)
         halo = jnp.concatenate([*columns(3), gap, *columns(1)], axis=0)
-        halo = dot(rows_ref[pl.ds(tail, 8), :], halo, NT, precision=HIGHEST)
+        halo = dot(rows(tail, 8), halo, NT, precision=HIGHEST)
 
         def base(n):
             edge = halo[n : n + 1]
-            return extend(rows_ref[pl.ds(n * tall, tall), :], edge, edge)
+            return extend(rows(n * tall, tall), edge, edge)
 
         sources = []
         row = base(0)
@@ -405,9 +432,9 @@
         def step(s, carry):
             start = pl.multiple_of(s * SLOT_STEP * ROWS, 8)
             t = x_ref[pl.ds(start, SLOT_STEP * ROWS), :].astype(i32)
-            t_high, t_low = t >> 7, t & (L - 1)
+            t_high, t_low = (t >> 7).astype(f32), t & (L - 1)
             rows = [m * ROWS + per + r for m in range(SLOT_STEP) for r in range(per)]
-            highs = jnp.concatenate([onehot(iota((tall, L), 0) == t_high[b : b + 1]) for b in rows], axis=1)
+            highs = jnp.concatenate([onehot(hits(t_high[b : b + 1], tall)) for b in rows], axis=1)
             found = dot(table, jnp.concatenate([highs, highs], axis=0))
             picked = []
             for k, b in enumerate(rows):
@@ -419,18 +446,59 @@
 
         lax.fori_loop(0, blocks // SLOT_STEP, step, 0)
 
-    def call(mine, other, rows, film, x):
+    def call(*args):
         vmem = pl.BlockSpec(memory_space=pltpu.VMEM)
         return pl.pallas_call(
             kernel,
-            in_specs=[vmem] * 5,
+            in_specs=[vmem] * 6,
             out_shape=[
                 jax.ShapeDtypeStruct((blocks * per, L), f32),
                 jax.ShapeDtypeStruct((ITERS * tall, L), f32),
                 jax.ShapeDtypeStruct((2 * tall, L), f32),
             ],
             name="surface_lookup",
-        )(mine, other, rows, film, x)
+        )(*args)
+
+    return call
+
+
+def add_sources(nl, width):
+    c = FACE_CHUNK
+    tall = width // L
+    part = c // L
+
+    def kernel(y_ref, coef_ref, source_ref, out_ref):
+        gas = lax.axis_index("grp") == 0
+
+        @pl.when(gas)
+        def _():
+            out_ref[...] = y_ref[...]
+
+        @pl.when(jnp.logical_not(gas))
+        def _():
+            coef = coef_ref[...]
+            spread = [jnp.broadcast_to(coef[:, n : n + 1], (nl, L)) for n in range(ITERS)]
+            for k in range(part):
+                cut = slice(k * L, (k + 1) * L)
+                total = y_ref[:, cut]
+                for n in range(ITERS):
+                    total = total + spread[n] * source_ref[n, k : k + 1]
+                out_ref[:, cut] = total
+
+    def call(y, coef, source):
+        wide = pl.BlockSpec((nl, c), lambda i: (0, i))
+        return pl.pallas_call(
+            kernel,
+            grid=(width // c,),
+            in_specs=[
+                wide,
+                pl.BlockSpec((nl, L), lambda i: (0, 0)),
+                pl.BlockSpec((ITERS, part, L), lambda i: (0, i, 0)),
+            ],
+            out_specs=wide,
+            out_shape=jax.ShapeDtypeStruct((nl, width), f32),
+            name="add_sources",
+        )(y, coef, source.reshape(ITERS, tall, L))
 
     return call
 
@@ -442,7 +510,7 @@
     part = c // L
     highs = blocks * capacity // L
 
-    def kernel(live_ref, reply_ref, slot_ref, y_ref, coef_ref, source_ref, surface_ref, out_ref, found_ref, rows_ref, table):
+    def kernel(live_ref, reply_ref, slot_ref, y_ref, coef_ref, surface_ref, out_ref, found_ref, rows_ref, table):
         i = pl.program_id(0)
         gas = lax.axis_index("grp") == 0
 
@@ -452,27 +520,21 @@
             table[...] = jnp.concatenate([high, low], axis=1).astype(bf16)
 
         slot = slot_ref[...]
-        hot = onehot(iota((highs, c), 0) == (slot >> 7))
+        hot = onehot(hits((slot >> 7).astype(f32), highs))
         found = dot(table[...], jnp.concatenate([hot, hot], axis=0))
         low = iota((L, c), 0) == (slot & (L - 1))
         live = (iota((1, c), 1) + i * c) < live_ref[0]
         picked = jnp.where(live, jnp.sum(jnp.where(low, found, 0.0), axis=0, keepdims=True), 0.0)
         found_ref[...] = picked
 
-        coef = coef_ref[...]
-        spread = [jnp.broadcast_to(coef[:, n : n + 1], (nl, L)) for n in range(ITERS)]
-        first = []
+        coupling = jnp.broadcast_to(jnp.where(gas, coef_ref[:, 0:1], 0.0), (nl, L))
         for k in range(part):
             cut = slice(k * L, (k + 1) * L)
-            lead = jnp.where(gas, picked[:, cut], source_ref[0, k : k + 1])
-            total = y_ref[:, cut] + spread[0] * lead
-            for n in range(1, ITERS):
-                total = total + spread[n] * source_ref[n, k : k + 1]
-            out_ref[:, cut] = total
+            out_ref[:, cut] = y_ref[:, cut] + coupling * picked[:, cut]
             rows_ref[0:1, cut] = jnp.where(gas, picked[:, cut], surface_ref[0, k : k + 1])
             rows_ref[1:2, cut] = surface_ref[1, k : k + 1]
 
-    def call(live_count, reply, slot, y, coef, source, surface):
+    def call(live_count, reply, slot, y, coef, surface):
         row = pl.BlockSpec((1, c), lambda i: (0, i))
         wide = pl.BlockSpec((nl, c), lambda i: (0, i))
         return pl.pallas_call(
@@ -484,7 +546,6 @@
                 row,
                 wide,
                 pl.BlockSpec((nl, L), lambda i: (0, 0)),
-                pl.BlockSpec((ITERS, part, L), lambda i: (0, i, 0)),
                 pl.BlockSpec((2, part, L), lambda i: (0, i, 0)),
             ],
             out_specs=[wide, row, pl.BlockSpec((2, c), lambda i: (0, i))],
@@ -495,7 +556,7 @@
             ],
             scratch_shapes=[pltpu.VMEM((L, 2 * highs), bf16)],
             name="face_finish",
-        )(live_count, reply, slot, y, coef, source.reshape(ITERS, tall, L), surface.reshape(2, tall, L))
+        )(live_count, reply, slot, y, coef, surface.reshape(2, tall, L))
 
     return call
 
@@ -519,13 +580,14 @@
     message, slot = route(width, blocks, capacity)(live_count, *faces, side, normal_weights)
     arrived = exchange(message)
     y, rows, coef = matrices(nl, width)(matrix, normal_weights, side)
-    rows = jnp.where(gas, across(rows), rows)
+    rows_other = across(rows)
 
     mine = gather_sum(width, blocks, capacity)(arrived)
     film = film.reshape(width // L, L)
-    replies, source, surface = surface_lookup(width, blocks, capacity)(mine, across(mine), rows, film, arrived)
+    replies, source, surface = surface_lookup(width, blocks, capacity)(mine, across(mine), rows, rows_other, film, arrived)
     returned = exchange(replies)
-    new_columns, found, surface = face_finish(nl, width, blocks, capacity)(live_count, returned, slot, y, coef, source, surface)
+    y = add_sources(nl, width)(y, coef, source)
+    new_columns, found, surface = face_finish(nl, width, blocks, capacity)(live_count, returned, slot, y, coef, surface)
     bottom = lax.broadcasted_iota(i32, surface.shape, 0) == 1
     surface = jnp.where(gas & bottom, across(found), surface)
     return new_columns[None], surface[None]

time: 89.9 us -> 86 us (0.957)
  blocking collectives: 15.3 us -> 0 us
  starting transfers between devices: 16.7 us -> 23.8 us
  Pallas kernels: 48.8 us -> 51.7 us
  waiting for transfers between devices: 2.36 us -> 4.62 us
  other arithmetic: 3.47 us -> 1.7 us
    all_to_all x1 -> x0, blocking collectives: 15.3 us -> none  [exchange(): lax.all_to_all(x.reshape(-1), 'blk', split_axis=0, concat_axis=0, tiled=T...]
    all_to_all x1 -> x2, starting transfers between devices: 12 us -> 19.1 us  [exchange(): lax.all_to_all(x.reshape(-1), 'blk', split_axis=0, concat_axis=0, tiled=T...]
    pallas_call x1 -> x2, Pallas kernels: 8.63 us -> 14.4 us  [the longest x1 7.43 us: call(): pl.pallas_call(kernel, grid=(width // c,), in_specs=[wide, pl.BlockSpec((...]
    pallas_call x2, Pallas kernels: 22.8 us -> 20.6 us  [call(): pl.pallas_call(kernel, grid=(steps,), in_specs=[pl.BlockSpec(memory_space...]
    select_n x1 -> x0, other arithmetic: 1.77 us -> none  [local(): rows = jnp.where(gas, across(rows), rows)]
    all_to_all x1 -> x2, waiting for transfers between devices: 1.25 us -> 2.4 us  [exchange(): lax.all_to_all(x.reshape(-1), 'blk', split_axis=0, concat_axis=0, tiled=T...]
    ppermute x3, waiting for transfers between devices: 1.11 us -> 2.22 us  [across(): return lax.ppermute(x, ('grp', 'blk'), swap)]
    unnamed x4 -> x8, local copies, waits for them, and re-layouts: 1.37 us -> 2.01 us
  transfers between devices with their start and end apart: 4 -> 5, of which waited for: 2 -> 4; matrix products, arithmetic and copies ran while one was open for 2% -> 0% of each run, Pallas kernels for 19% -> 28%
where the time goes in v3:
time: 86 us; the launch traced here: 85.1 us
  Pallas kernels  51.7 us (60%)
  starting transfers between devices  23.8 us (28%)
  waiting for transfers between devices  4.62 us (5%)
  local copies, waits for them, and re-layouts  2.01 us (2%)
  other arithmetic  1.7 us (2%)
  between operations  1.31 us (2%)
    pallas_call x2, Pallas kernels, call(): pl.pallas_call(kernel, grid=(steps,), in_specs=[pl.BlockSpec(memory_space...  20.6 us
    all_to_all x2, starting transfers between devices, exchange(): lax.all_to_all(x.reshape(-1), 'blk', split_axis=0, concat_axis=0, tiled=T...  19.1 us
    pallas_call x1, Pallas kernels, call(): pl.pallas_call(kernel, out_shape=jax.ShapeDtypeStruct((tall + 8, L), f32)...  8.59 us
    pallas_call x1, Pallas kernels, call(): pl.pallas_call(kernel, grid=(steps,), in_specs=[pl.BlockSpec((nl, nl), la...  8.11 us
    pallas_call x1, Pallas kernels, call(): pl.pallas_call(kernel, grid=(width // c,), in_specs=[wide, pl.BlockSpec((...  7.43 us
    pallas_call x1, Pallas kernels, call(): pl.pallas_call(kernel, in_specs=[vmem] * 6, out_shape=[jax.ShapeDtypeStru...  6.98 us
    ppermute x3, starting transfers between devices, across(): return lax.ppermute(x, ('grp', 'blk'), swap)  4.64 us
    all_to_all x2, waiting for transfers between devices, exchange(): lax.all_to_all(x.reshape(-1), 'blk', split_axis=0, concat_axis=0, tiled=T...  2.4 us
  transfers between devices with their start and end apart: 5, of which 4 were waited for; matrix products, arithmetic and copies ran while one was open for 0% of the time, Pallas kernels for 28%

profile of v3, /device:TPU:1, one launch (start us, length us, event | category | flops | bytes accessed | tf_op | source)
XLA Modules:
  0.0 85.1 jit_solution(1112819077045522922)
XLA Ops:
  1.3 12.1 %route.1 = (f32[704,128]{1,0:T(8,128)}, s32[1,16384]{1,0:T(1,128)}) custom-call(s32[1]{0:T(128)S(6)} %copy.13.live_ref, s32[1,16384]{1,0:T(1,128)} %bitcast.28, s32[1,16384]{1,0:T(1,128)} %bitcast.29, s32[1,16384]{1,0:T(1,128)} %bitcast.30, f32[1,16384]{1,0:T(1,128)} %bitcast.31, f32[64,16384]{1,0:T(8,128)} %bitcast.17, f32[64,16384]{1,0:T(8,128)} %bitcast.18, ...), custom_call_target="tpu_custom_call" | custom-call | tf_op jit(solution)/shard_map/route/pallas_call | solution.py:199
  13.4 12.0 %all-to-all-start = ((f32[64,1408,1]{1,2,0:T(1,128)}), f32[64,1408,1]{1,2,0:T(1,128)S(1)}, u32[]{:S(2)}, u32[]{:S(2)}) async-start(f32[64,1408,1]{1,2,0:T(1,128)} %bitcast.24), calls=%async_computation | async-start | bytes 720896 | tf_op jit(solution)/shard_map/all_to_all | solution.py:577
  25.4 8.1 %matrices.1 = (f32[64,16384]{1,0:T(8,128)}, f32[656,128]{1,0:T(8,128)}, f32[64,128]{1,0:T(8,128)}) custom-call(f32[64,64]{1,0:T(8,128)} %bitcast.34, f32[2,64]{1,0:T(2,128)} %weight_ref.3, f32[64,16384]{1,0:T(8,128)} %bitcast.20), custom_call_target="tpu_custom_call" | custom-call | tf_op jit(solution)/shard_map/matrices/pallas_call | solution.py:274
  33.5 1.0 %collective-permute-start.1 = (f32[656,128]{1,0:T(8,128)}, f32[656,128]{1,0:T(8,128)S(1)}, u32[]{:S(2)}, u32[]{:S(2)}) collective-permute-start(f32[656,128]{1,0:T(8,128)} %get-tuple-element.14.rows_mine), channel_id=1, source_target_pairs={{0,64},{1,65},{2,66},{3,67},{4,68},{5,69},{6,70},{7,71},{8,72},{9,... | collective-permute-start | bytes 1007624 | tf_op jit(solution)/shard_map/ppermute | solution.py:574
  34.5 1.2 %all-to-all-done = f32[64,1408,1]{1,2,0:T(1,128)S(1)} async-done(((f32[64,1408,1]{1,2,0:T(1,128)}), f32[64,1408,1]{1,2,0:T(1,128)S(1)}, u32[]{:S(2)}, u32[]{:S(2)}) %all-to-all-start) | async-done | bytes 360480 | tf_op jit(solution)/shard_map/all_to_all | solution.py:577
  35.7 0.0 copy-start
  35.7 0.7 copy-done
  36.4 8.6 %gather_sum.1.mine_ref = f32[136,128]{1,0:T(8,128)} custom-call(f32[704,128]{1,0:T(8,128)} %bitcast.21), custom_call_target="tpu_custom_call" | custom-call | tf_op jit(solution)/shard_map/gather_sum/pallas_call | solution.py:350
  45.0 2.1 %collective-permute-start = (f32[136,128]{1,0:T(8,128)}, f32[136,128]{1,0:T(8,128)S(1)}, u32[]{:S(2)}, u32[]{:S(2)}) collective-permute-start(f32[136,128]{1,0:T(8,128)} %gather_sum.1.mine_ref), channel_id=1, source_target_pairs={{0,64},{1,65},{2,66},{3,67},{4,68},{5,69},{6,70},{7,71},{8,72},{9,... | collective-permute-start | bytes 208904 | tf_op jit(solution)/shard_map/ppermute | solution.py:574
  47.1 0.0 collective-permute-done.1.rows_other
  47.1 0.0 copy-start.2
  47.1 1.1 %collective-permute-done.other_ref = f32[136,128]{1,0:T(8,128)S(1)} collective-permute-done((f32[136,128]{1,0:T(8,128)}, f32[136,128]{1,0:T(8,128)S(1)}, u32[]{:S(2)}, u32[]{:S(2)}) %collective-permute-start) | collective-permute-done | bytes 69664 | tf_op jit(solution)/shard_map/ppermute | solution.py:574
  48.2 0.0 copy-start.3
  48.2 0.0 copy-done.2
  48.2 0.6 copy-done.3
  48.8 7.0 %surface_lookup.1 = (f32[256,128]{1,0:T(8,128)}, f32[512,128]{1,0:T(8,128)}, f32[256,128]{1,0:T(8,128)}) custom-call(f32[136,128]{1,0:T(8,128)} %gather_sum.1.mine_ref, f32[136,128]{1,0:T(8,128)} %copy-done.3, f32[656,128]{1,0:T(8,128)} %get-tuple-element.14.rows_mine, f32[656,128]{1,0:T(8,128)} %copy-done.2, f32[128,128]{1,0:T(8,128)} %bitcast.32, ...), custom_call_target="tpu_custom_call" | custom-call | tf_op jit(solution)/shard_map/surface_lookup/pallas_call | solution.py:451
  55.8 7.1 %all-to-all-start.1 = ((f32[64,512,1]{1,2,0:T(1,128)}), f32[64,512,1]{1,2,0:T(1,128)S(1)}, u32[]{:S(2)}, u32[]{:S(2)}) async-start(f32[64,512,1]{1,2,0:T(1,128)} %bitcast.27), calls=%async_computation.1 | async-start | bytes 262144 | tf_op jit(solution)/shard_map/all_to_all | solution.py:577
  62.9 7.4 %add_sources.1.y_ref = f32[64,16384]{1,0:T(8,128)} custom-call(f32[64,16384]{1,0:T(8,128)} %get-tuple-element.17.y_ref, f32[64,128]{1,0:T(8,128)} %get-tuple-element.18.coef_ref, f32[4,128,128]{2,1,0:T(8,128)} %bitcast.25), custom_call_target="tpu_custom_call" | custom-call | tf_op jit(solution)/shard_map/add_sources/pallas_call | solution.py:490
  70.4 1.2 %all-to-all-done.1 = f32[64,512,1]{1,2,0:T(1,128)S(1)} async-done(((f32[64,512,1]{1,2,0:T(1,128)}), f32[64,512,1]{1,2,0:T(1,128)S(1)}, u32[]{:S(2)}, u32[]{:S(2)}) %all-to-all-start.1) | async-done | bytes 131104 | tf_op jit(solution)/shard_map/all_to_all | solution.py:577
  71.6 0.7 copy-done.1
  72.2 8.5 %face_finish.1 = (f32[64,16384]{1,0:T(8,128)}, f32[1,16384]{1,0:T(1,128)}, f32[2,16384]{1,0:T(2,128)}) custom-call(s32[1]{0:T(128)S(6)} %copy.13.live_ref, f32[256,128]{1,0:T(8,128)} %bitcast.23, s32[1,16384]{1,0:T(1,128)} %get-tuple-element.16.slot_ref, f32[64,16384]{1,0:T(8,128)} %add_sources.1.y_ref, f32[64,128]{1,0:T(8,128)} %get-tuple-element.18.coef_ref, ...), custom_call_target="tpu_custom_call" | custom-call | tf_op jit(solution)/shard_map/face_finish/pallas_call | solution.py:540
  80.8 1.6 %collective-permute-start.2 = (f32[1,16384]{1,0:T(1,128)}, f32[1,16384]{1,0:T(1,128)S(1)}, u32[]{:S(2)}, u32[]{:S(2)}) collective-permute-start(f32[1,16384]{1,0:T(1,128)} %get-tuple-element.22), channel_id=1, source_target_pairs={{0,64},{1,65},{2,66},{3,67},{4,68},{5,69},{6,70},{7,71},{8,72},{9,... | collective-permute-start | bytes 196616 | tf_op jit(solution)/shard_map/ppermute | solution.py:574
  82.3 1.1 %collective-permute-done.2 = f32[1,16384]{1,0:T(1,128)S(1)} collective-permute-done((f32[1,16384]{1,0:T(1,128)}, f32[1,16384]{1,0:T(1,128)S(1)}, u32[]{:S(2)}, u32[]{:S(2)}) %collective-permute-start.2) | collective-permute-done | bytes 65568 | tf_op jit(solution)/shard_map/ppermute | solution.py:574
  83.4 1.7 %select_bitcast_fusion = f32[1,2,16384]{2,1,0:T(2,128)} fusion(f32[2,16384]{1,0:T(2,128)} %get-tuple-element.23, pred[2]{0:T(512)(128)(4,1)S(1)} %compare_and_fusion, f32[16384]{0:T(1024)S(1)} %bitcast.33), kind=kLoop, calls=%fused_computation | loop fusion | flops 32768 | bytes 327682 | tf_op jit(solution)/shard_map/broadcast_in_dim | solution.py:593
  (2 shorter events, 0.0 us)
Async XLA Ops:
  13.4 22.3 %all-to-all-start = ((f32[64,1408,1]{1,2,0:T(1,128)}), f32[64,1408,1]{1,2,0:T(1,128)S(1)}, u32[]{:S(2)}, u32[]{:S(2)}) async-start(f32[64,1408,1]{1,2,0:T(1,128)} %bitcast.24), calls=%async_computation | async-start | bytes 720896 | tf_op jit(solution)/shard_map/all_to_all | solution.py:577
  33.5 13.6 %collective-permute-start.1 = (f32[656,128]{1,0:T(8,128)}, f32[656,128]{1,0:T(8,128)S(1)}, u32[]{:S(2)}, u32[]{:S(2)}) collective-permute-start(f32[656,128]{1,0:T(8,128)} %get-tuple-element.14.rows_mine), channel_id=1, source_target_pairs={{0,64},{1,65},{2,66},{3,67},{4,68},{5,69},{6,70},{7,71},{8,72},{9,... | collective-permute-start | bytes 1007624 | tf_op jit(solution)/shard_map/ppermute | solution.py:574
  35.7 0.7 copy-start
  45.0 3.2 %collective-permute-start = (f32[136,128]{1,0:T(8,128)}, f32[136,128]{1,0:T(8,128)S(1)}, u32[]{:S(2)}, u32[]{:S(2)}) collective-permute-start(f32[136,128]{1,0:T(8,128)} %gather_sum.1.mine_ref), channel_id=1, source_target_pairs={{0,64},{1,65},{2,66},{3,67},{4,68},{5,69},{6,70},{7,71},{8,72},{9,... | collective-permute-start | bytes 208904 | tf_op jit(solution)/shard_map/ppermute | solution.py:574
  47.1 1.1 %copy-start.2 = (f32[656,128]{1,0:T(8,128)}, f32[656,128]{1,0:T(8,128)S(1)}, u32[]{:S(2)}) copy-start(f32[656,128]{1,0:T(8,128)S(1)} %collective-permute-done.1.rows_other) | copy-start | bytes 1007620
  48.2 0.6 copy-start.3
  55.8 15.7 %all-to-all-start.1 = ((f32[64,512,1]{1,2,0:T(1,128)}), f32[64,512,1]{1,2,0:T(1,128)S(1)}, u32[]{:S(2)}, u32[]{:S(2)}) async-start(f32[64,512,1]{1,2,0:T(1,128)} %bitcast.27), calls=%async_computation.1 | async-start | bytes 262144 | tf_op jit(solution)/shard_map/all_to_all | solution.py:577
  71.6 0.7 copy-start.1
  80.8 2.7 %collective-permute-start.2 = (f32[1,16384]{1,0:T(1,128)}, f32[1,16384]{1,0:T(1,128)S(1)}, u32[]{:S(2)}, u32[]{:S(2)}) collective-permute-start(f32[1,16384]{1,0:T(1,128)} %get-tuple-element.22), channel_id=1, source_target_pairs={{0,64},{1,65},{2,66},{3,67},{4,68},{5,69},{6,70},{7,71},{8,72},{9,... | collective-permute-start | bytes 196616 | tf_op jit(solution)/shard_map/ppermute | solution.py:574

commit v4 on v3

--- a/solution.py
+++ b/solution.py
@@ -8,8 +8,12 @@
 ITERS = 4
 L = 128
 HALO = ITERS
+PARAMS = pltpu.CompilerParams(vmem_limit_bytes=24 << 20)
+MIDDLE = pltpu.CompilerParams(vmem_limit_bytes=52 << 20)
+LARGE = pltpu.CompilerParams(vmem_limit_bytes=60 << 20)
 ROWS = 11
 FACE_CHUNK = 2048
+PIECE = 256
 SLOT_STEP = 8
 
 f32 = jnp.float32
@@ -126,11 +130,12 @@
         hot = onehot(hits(patch.astype(f32), blocks))
         wide = (sub, sub + L)
         upto = jnp.where((iota(wide, 0) <= iota(wide, 1)) | (iota(wide, 1) >= sub), 1.0, 0.0).astype(bf16)
+        cuts = [slice(j * sub, (j + 1) * sub) for j in range(c // sub)]
+        counts = dot(jnp.concatenate([hot[:, cut] for cut in cuts], axis=0), upto)
         before = carry[...]
         ranks = []
-        for j in range(c // sub):
-            cut = slice(j * sub, (j + 1) * sub)
-            count = dot(hot[:, cut], upto)
+        for j, cut in enumerate(cuts):
+            count = counts[j * blocks : (j + 1) * blocks]
             total = count[:, :sub] + jnp.concatenate([before] * (sub // L), axis=1)
             ranks.append(jnp.sum(jnp.where(named[:, cut], total, 0.0), axis=0, keepdims=True))
             before = before + count[:, sub:]
@@ -224,6 +229,7 @@
                 pltpu.VMEM((8, L), i32),
                 pltpu.VMEM((nl, L), f32),
             ],
+            compiler_params=LARGE,
             name="route",
         )(live_count, patch, point, impinged, load, side, side, side, weights)
 
@@ -290,6 +296,7 @@
                 jax.ShapeDtypeStruct((nl, L), f32),
             ],
             scratch_shapes=[pltpu.VMEM((out_rows, 4 * nl), bf16)],
+            compiler_params=MIDDLE,
             name="matrices",
         )(op, weights, side)
 
@@ -313,7 +320,9 @@
                     highs.append(onehot(hits(t_high[b : b + 1], tall)))
                     low = hits(t_low[b : b + 1], L)
                     lows.append(jnp.concatenate([masked(low, part) for part in halves(x[a : a + 1])], axis=0))
-            acc[...] += dot(jnp.concatenate(highs, axis=1), jnp.concatenate(lows, axis=1), NT)
+            placed = dot(jnp.concatenate(lows, axis=1), jnp.concatenate(highs, axis=1), NT)
+            for q in range(2):
+                acc[pl.ds(q * L, L), :] += placed[q * L : (q + 1) * L]
             return nothing
 
         info = x_ref[pl.ds(2 * per, blocks, stride=ROWS), :]
@@ -330,14 +339,14 @@
         v_high, v_low = split(value)
         low = hits((target & (L - 1)).astype(f32), L)
         high = onehot(hits((target >> 7).astype(f32), tall))
-        acc[...] = dot(high, jnp.concatenate([masked(low, x) for x in halves(value)], axis=0), NT)
+        acc[...] = dot(jnp.concatenate([masked(low, x) for x in halves(value)], axis=0), high, NT)
         at = onehot(hits(halo.astype(f32), L))
         pieces = jnp.concatenate([v_high, v_low, jnp.zeros((6, L), f32)], axis=0).astype(bf16)
         edge = jnp.sum(dot(pieces, at, NT), axis=0, keepdims=True)
         edge = edge + jnp.where(lane < 8, jnp.sum(info, axis=0, keepdims=True), 0.0)
 
         lax.fori_loop(0, blocks // SLOT_STEP, step, 0)
-        out_ref[pl.ds(0, tall), :] = acc[:, :L] + acc[:, L:]
+        out_ref[pl.ds(0, tall), :] = (acc[:L] + acc[L:]).T
         block, source = lax.axis_index("blk"), iota((blocks, L), 0)
         rows = [edge]
         for near in (block - 1, block + 1):
@@ -350,7 +359,8 @@
         return pl.pallas_call(
             kernel,
             out_shape=jax.ShapeDtypeStruct((tall + 8, L), f32),
-            scratch_shapes=[pltpu.VMEM((tall, 2 * L), f32)],
+            scratch_shapes=[pltpu.VMEM((2 * L, tall), f32)],
+            compiler_params=PARAMS,
             name="gather_sum",
         )(x)
 
@@ -434,12 +444,14 @@
             t = x_ref[pl.ds(start, SLOT_STEP * ROWS), :].astype(i32)
             t_high, t_low = (t >> 7).astype(f32), t & (L - 1)
             rows = [m * ROWS + per + r for m in range(SLOT_STEP) for r in range(per)]
-            highs = jnp.concatenate([onehot(hits(t_high[b : b + 1], tall)) for b in rows], axis=1)
-            found = dot(table, jnp.concatenate([highs, highs], axis=0))
             picked = []
-            for k, b in enumerate(rows):
-                low = iota((L, L), 0) == t_low[b : b + 1]
-                picked.append(jnp.sum(jnp.where(low, found[:, k * L : (k + 1) * L], 0.0), axis=0, keepdims=True))
+            for g in range(0, len(rows), PIECE // L):
+                group = rows[g : g + PIECE // L]
+                highs = jnp.concatenate([onehot(hits(t_high[b : b + 1], tall)) for b in group], axis=1)
+                found = dot(table, jnp.concatenate([highs, highs], axis=0))
+                for k, b in enumerate(group):
+                    low = iota((L, L), 0) == t_low[b : b + 1]
+                    picked.append(jnp.sum(jnp.where(low, found[:, k * L : (k + 1) * L], 0.0), axis=0, keepdims=True))
             size = SLOT_STEP * per
             out_ref[pl.ds(pl.multiple_of(s * size, 8), size), :] = jnp.concatenate(picked, axis=0)
             return carry
@@ -456,6 +468,7 @@
                 jax.ShapeDtypeStruct((ITERS * tall, L), f32),
                 jax.ShapeDtypeStruct((2 * tall, L), f32),
             ],
+            compiler_params=PARAMS,
             name="surface_lookup",
         )(*args)
 
@@ -497,6 +510,7 @@
             ],
             out_specs=wide,
             out_shape=jax.ShapeDtypeStruct((nl, width), f32),
+            compiler_params=MIDDLE,
             name="add_sources",
         )(y, coef, source.reshape(ITERS, tall, L))
 
@@ -517,22 +531,26 @@
         @pl.when(i == 0)
         def _():
             high, low = split(reply_ref[...].T)
-            table[...] = jnp.concatenate([high, low], axis=1).astype(bf16)
-
-        slot = slot_ref[...]
-        hot = onehot(hits((slot >> 7).astype(f32), highs))
-        found = dot(table[...], jnp.concatenate([hot, hot], axis=0))
-        low = iota((L, c), 0) == (slot & (L - 1))
-        live = (iota((1, c), 1) + i * c) < live_ref[0]
-        picked = jnp.where(live, jnp.sum(jnp.where(low, found, 0.0), axis=0, keepdims=True), 0.0)
-        found_ref[...] = picked
+            table[...] = jnp.concatenate([high, low], axis=0).astype(bf16)
 
         coupling = jnp.broadcast_to(jnp.where(gas, coef_ref[:, 0:1], 0.0), (nl, L))
-        for k in range(part):
-            cut = slice(k * L, (k + 1) * L)
-            out_ref[:, cut] = y_ref[:, cut] + coupling * picked[:, cut]
-            rows_ref[0:1, cut] = jnp.where(gas, picked[:, cut], surface_ref[0, k : k + 1])
-            rows_ref[1:2, cut] = surface_ref[1, k : k + 1]
+        for j in range(c // PIECE):
+            piece = slice(j * PIECE, (j + 1) * PIECE)
+            slot = slot_ref[:, piece]
+            hot = onehot(hits((slot >> 7).astype(f32), highs))
+            found = dot(table[...], hot)
+            found = found[:L] + found[L:]
+            low = iota((L, PIECE), 0) == (slot & (L - 1))
+            live = (iota((1, PIECE), 1) + (i * c + j * PIECE)) < live_ref[0]
+            picked = jnp.where(live, jnp.sum(jnp.where(low, found, 0.0), axis=0, keepdims=True), 0.0)
+            found_ref[:, piece] = picked
+            for k in range(PIECE // L):
+                m = j * (PIECE // L) + k
+                cut = slice(m * L, (m + 1) * L)
+                one = picked[:, k * L : (k + 1) * L]
+                out_ref[:, cut] = y_ref[:, cut] + coupling * one
+                rows_ref[0:1, cut] = jnp.where(gas, one, surface_ref[0, m : m + 1])
+                rows_ref[1:2, cut] = surface_ref[1, m : m + 1]
 
     def call(live_count, reply, slot, y, coef, surface):
         row = pl.BlockSpec((1, c), lambda i: (0, i))
@@ -554,7 +572,8 @@
                 jax.ShapeDtypeStruct((1, width), f32),
                 jax.ShapeDtypeStruct((2, width), f32),
             ],
-            scratch_shapes=[pltpu.VMEM((L, 2 * highs), bf16)],
+            scratch_shapes=[pltpu.VMEM((2 * L, highs), bf16)],
+            compiler_params=MIDDLE,
             name="face_finish",
         )(live_count, reply, slot, y, coef, surface.reshape(2, tall, L))
 

time: 86 us -> 78.5 us (0.913)
  Pallas kernels: 51.7 us -> 47.5 us
  local copies, waits for them, and re-layouts: 2.01 us -> 0.02 us
  other arithmetic: 1.7 us -> 0.79 us
    pallas_call x1, Pallas kernels: 8.59 us -> 6.21 us  [call(): pl.pallas_call(kernel, out_shape=jax.ShapeDtypeStruct((tall + 8, L), f32)...]
    unnamed x8, local copies, waits for them, and re-layouts: 2.01 us -> 0.02 us
    pallas_call x1, Pallas kernels: 6.98 us -> 5.67 us  [call(): pl.pallas_call(kernel, in_specs=[vmem] * 6, out_shape=[jax.ShapeDtypeStru...]
    broadcast_in_dim x1, other arithmetic: 1.69 us -> 0.78 us  [local(): return (new_columns[None], surface[None])]
where the time goes in v4:
time: 78.5 us; the launch traced here: 77.7 us
  Pallas kernels  47.5 us (61%)
  starting transfers between devices  23.8 us (30%)
  waiting for transfers between devices  4.28 us (5%)
  between operations  1.35 us (2%)
  other arithmetic  0.79 us (1%)
    pallas_call x2, Pallas kernels, call(): pl.pallas_call(kernel, grid=(steps,), in_specs=[pl.BlockSpec(memory_space...  20.1 us
    all_to_all x2, starting transfers between devices, exchange(): lax.all_to_all(x.reshape(-1), 'blk', split_axis=0, concat_axis=0, tiled=T...  19.1 us
    pallas_call x1, Pallas kernels, call(): pl.pallas_call(kernel, grid=(steps,), in_specs=[pl.BlockSpec((nl, nl), la...  8.01 us
    pallas_call x1, Pallas kernels, call(): pl.pallas_call(kernel, grid=(width // c,), in_specs=[wide, pl.BlockSpec((...  7.43 us
    pallas_call x1, Pallas kernels, call(): pl.pallas_call(kernel, out_shape=jax.ShapeDtypeStruct((tall + 8, L), f32)...  6.21 us
    pallas_call x1, Pallas kernels, call(): pl.pallas_call(kernel, in_specs=[vmem] * 6, out_shape=[jax.ShapeDtypeStru...  5.67 us
    ppermute x3, starting transfers between devices, across(): return lax.ppermute(x, ('grp', 'blk'), swap)  4.71 us
    all_to_all x2, waiting for transfers between devices, exchange(): lax.all_to_all(x.reshape(-1), 'blk', split_axis=0, concat_axis=0, tiled=T...  2.48 us
  transfers between devices with their start and end apart: 5, of which 4 were waited for; matrix products, arithmetic and copies ran while one was open for 0% of the time, Pallas kernels for 28%

profile of v4, /device:TPU:1, one launch (start us, length us, event | category | flops | bytes accessed | tf_op | source)
XLA Modules:
  0.0 77.7 jit_solution(14467362496239845277)
XLA Ops:
  1.3 0.0 copy-start.2
  1.3 0.0 copy-start.3
  1.3 11.9 %route.1 = (f32[704,128]{1,0:T(8,128)}, s32[1,16384]{1,0:T(1,128)}) custom-call(s32[1]{0:T(128)S(6)} %copy.13.live_ref, s32[1,16384]{1,0:T(1,128)} %bitcast.29, s32[1,16384]{1,0:T(1,128)} %bitcast.30, s32[1,16384]{1,0:T(1,128)} %bitcast.31, f32[1,16384]{1,0:T(1,128)} %bitcast.32, f32[64,16384]{1,0:T(8,128)} %bitcast.24, f32[64,16384]{1,0:T(8,128)} %bitcast.25, ...), custom_call_target="tpu_custom_call" | custom-call | tf_op jit(solution)/shard_map/route/pallas_call | solution.py:204
  13.2 12.1 %all-to-all-start = ((f32[64,1408,1]{1,2,0:T(1,128)}), f32[64,1408,1]{1,2,0:T(1,128)S(1)}, u32[]{:S(2)}, u32[]{:S(2)}) async-start(f32[64,1408,1]{1,2,0:T(1,128)} %bitcast.28), calls=%async_computation | async-start | bytes 720896 | tf_op jit(solution)/shard_map/all_to_all | solution.py:596
  25.3 0.0 copy-done.2
  25.3 0.0 copy-done.3
  25.3 8.0 %matrices.1 = (f32[64,16384]{1,0:T(8,128)}, f32[656,128]{1,0:T(8,128)S(1)}, f32[64,128]{1,0:T(8,128)S(1)}) custom-call(f32[64,64]{1,0:T(8,128)S(1)} %bitcast.23, f32[2,64]{1,0:T(2,128)S(1)} %copy-done.3, f32[64,16384]{1,0:T(8,128)} %bitcast.27), custom_call_target="tpu_custom_call" | custom-call | tf_op jit(solution)/shard_map/matrices/pallas_call | solution.py:280
  33.3 1.0 %collective-permute-start.1 = (f32[656,128]{1,0:T(8,128)S(1)}, f32[656,128]{1,0:T(8,128)S(1)}, u32[]{:S(2)}, u32[]{:S(2)}) collective-permute-start(f32[656,128]{1,0:T(8,128)S(1)} %get-tuple-element.14.rows_mine), channel_id=1, source_target_pairs={{0,64},{1,65},{2,66},{3,67},{4,68},{5,69},{6,70},{7,71},{8,72},{9,... | collective-permute-start | bytes 1007624 | tf_op jit(solution)/shard_map/ppermute | solution.py:593
  34.3 1.3 %all-to-all-done = f32[64,1408,1]{1,2,0:T(1,128)S(1)} async-done(((f32[64,1408,1]{1,2,0:T(1,128)}), f32[64,1408,1]{1,2,0:T(1,128)S(1)}, u32[]{:S(2)}, u32[]{:S(2)}) %all-to-all-start) | async-done | bytes 360480 | tf_op jit(solution)/shard_map/all_to_all | solution.py:596
  35.6 6.2 %gather_sum.1.mine_ref = f32[136,128]{1,0:T(8,128)S(1)} custom-call(f32[704,128]{1,0:T(8,128)S(1)} %bitcast.17), custom_call_target="tpu_custom_call" | custom-call | tf_op jit(solution)/shard_map/gather_sum/pallas_call | solution.py:359
  41.8 2.2 %collective-permute-start = (f32[136,128]{1,0:T(8,128)S(1)}, f32[136,128]{1,0:T(8,128)S(1)}, u32[]{:S(2)}, u32[]{:S(2)}) collective-permute-start(f32[136,128]{1,0:T(8,128)S(1)} %gather_sum.1.mine_ref), channel_id=1, source_target_pairs={{0,64},{1,65},{2,66},{3,67},{4,68},{5,69},{6,70},{7,71},{8,72},{9,... | collective-permute-start | bytes 208904 | tf_op jit(solution)/shard_map/ppermute | solution.py:593
  44.0 0.0 collective-permute-done.1.rows_other
  44.0 0.9 %collective-permute-done.other_ref = f32[136,128]{1,0:T(8,128)S(1)} collective-permute-done((f32[136,128]{1,0:T(8,128)S(1)}, f32[136,128]{1,0:T(8,128)S(1)}, u32[]{:S(2)}, u32[]{:S(2)}) %collective-permute-start) | collective-permute-done | bytes 69664 | tf_op jit(solution)/shard_map/ppermute | solution.py:593
  44.9 0.0 copy-done.1
  44.9 5.7 %surface_lookup.1 = (f32[256,128]{1,0:T(8,128)}, f32[512,128]{1,0:T(8,128)S(1)}, f32[256,128]{1,0:T(8,128)S(1)}) custom-call(f32[136,128]{1,0:T(8,128)S(1)} %gather_sum.1.mine_ref, f32[136,128]{1,0:T(8,128)S(1)} %collective-permute-done.other_ref, f32[656,128]{1,0:T(8,128)S(1)} %get-tuple-element.14.rows_mine, ...), custom_call_target="tpu_custom_call" | custom-call | tf_op jit(solution)/shard_map/surface_lookup/pallas_call | solution.py:463
  50.5 7.0 %all-to-all-start.1 = ((f32[64,512,1]{1,2,0:T(1,128)}), f32[64,512,1]{1,2,0:T(1,128)S(1)}, u32[]{:S(2)}, u32[]{:S(2)}) async-start(f32[64,512,1]{1,2,0:T(1,128)} %bitcast.9), calls=%async_computation.1 | async-start | bytes 262144 | tf_op jit(solution)/shard_map/all_to_all | solution.py:596
  57.6 0.0 copy-start
  57.6 7.4 %add_sources.1.y_ref = f32[64,16384]{1,0:T(8,128)} custom-call(f32[64,16384]{1,0:T(8,128)} %get-tuple-element.17.y_ref, f32[64,128]{1,0:T(8,128)S(1)} %get-tuple-element.18.coef_ref, f32[4,128,128]{2,1,0:T(8,128)S(1)} %bitcast.20), custom_call_target="tpu_custom_call" | custom-call | tf_op jit(solution)/shard_map/add_sources/pallas_call | solution.py:503
  65.0 1.2 %all-to-all-done.1 = f32[64,512,1]{1,2,0:T(1,128)S(1)} async-done(((f32[64,512,1]{1,2,0:T(1,128)}), f32[64,512,1]{1,2,0:T(1,128)S(1)}, u32[]{:S(2)}, u32[]{:S(2)}) %all-to-all-start.1) | async-done | bytes 131104 | tf_op jit(solution)/shard_map/all_to_all | solution.py:596
  66.2 0.0 copy-done
  66.2 8.3 %face_finish.1 = (f32[64,16384]{1,0:T(8,128)}, f32[1,16384]{1,0:T(1,128)S(1)}, f32[2,16384]{1,0:T(2,128)S(1)}) custom-call(s32[1]{0:T(128)S(6)} %copy.13.live_ref, f32[256,128]{1,0:T(8,128)S(1)} %bitcast.19, s32[1,16384]{1,0:T(1,128)S(1)} %copy-done, f32[64,16384]{1,0:T(8,128)} %add_sources.1.y_ref, f32[64,128]{1,0:T(8,128)S(1)} %get-tuple-element.18.coef_ref, ...), custom_call_target="tpu_custom_call" | custom-call | tf_op jit(solution)/shard_map/face_finish/pallas_call | solution.py:558
  74.5 1.6 %collective-permute-start.2 = (f32[1,16384]{1,0:T(1,128)S(1)}, f32[1,16384]{1,0:T(1,128)S(1)}, u32[]{:S(2)}, u32[]{:S(2)}) collective-permute-start(f32[1,16384]{1,0:T(1,128)S(1)} %get-tuple-element.22), channel_id=1, source_target_pairs={{0,64},{1,65},{2,66},{3,67},{4,68},{5,69},{6,70},{7,71},{8,72},{9,... | collective-permute-start | bytes 196616 | tf_op jit(solution)/shard_map/ppermute | solution.py:593
  76.1 0.9 %collective-permute-done.2 = f32[1,16384]{1,0:T(1,128)S(1)} collective-permute-done((f32[1,16384]{1,0:T(1,128)S(1)}, f32[1,16384]{1,0:T(1,128)S(1)}, u32[]{:S(2)}, u32[]{:S(2)}) %collective-permute-start.2) | collective-permute-done | bytes 65568 | tf_op jit(solution)/shard_map/ppermute | solution.py:593
  77.0 0.8 %select_bitcast_fusion = f32[1,2,16384]{2,1,0:T(2,128)} fusion(f32[2,16384]{1,0:T(2,128)S(1)} %get-tuple-element.23, pred[2]{0:T(512)(128)(4,1)S(1)} %compare_and_fusion, f32[16384]{0:T(1024)S(1)} %bitcast.33), kind=kLoop, calls=%fused_computation | loop fusion | flops 32768 | bytes 327682 | tf_op jit(solution)/shard_map/broadcast_in_dim | solution.py:612
  (2 shorter events, 0.0 us)
Async XLA Ops:
  1.3 24.0 %copy-start.2 = (f32[1,64,64]{2,1,0:T(8,128)S(1)}, f32[1,64,64]{2,1,0:T(8,128)}, u32[]{:S(2)}) copy-start(f32[1,64,64]{2,1,0:T(8,128)} %param.10) | copy-start | bytes 49156
  1.3 24.0 %copy-start.3 = (f32[2,64]{1,0:T(2,128)S(1)}, f32[2,64]{1,0:T(2,128)}, u32[]{:S(2)}) copy-start(f32[2,64]{1,0:T(2,128)} %weight_ref.3) | copy-start | bytes 1540
  13.2 31.7 %copy-start.1 = (f32[16384]{0:T(1024)S(1)}, f32[16384]{0:T(1024)}, u32[]{:S(2)}) copy-start(f32[16384]{0:T(1024)} %param.17) | copy-start | bytes 196612
  13.2 22.4 %all-to-all-start = ((f32[64,1408,1]{1,2,0:T(1,128)}), f32[64,1408,1]{1,2,0:T(1,128)S(1)}, u32[]{:S(2)}, u32[]{:S(2)}) async-start(f32[64,1408,1]{1,2,0:T(1,128)} %bitcast.28), calls=%async_computation | async-start | bytes 720896 | tf_op jit(solution)/shard_map/all_to_all | solution.py:596
  33.3 10.6 %collective-permute-start.1 = (f32[656,128]{1,0:T(8,128)S(1)}, f32[656,128]{1,0:T(8,128)S(1)}, u32[]{:S(2)}, u32[]{:S(2)}) collective-permute-start(f32[656,128]{1,0:T(8,128)S(1)} %get-tuple-element.14.rows_mine), channel_id=1, source_target_pairs={{0,64},{1,65},{2,66},{3,67},{4,68},{5,69},{6,70},{7,71},{8,72},{9,... | collective-permute-start | bytes 1007624 | tf_op jit(solution)/shard_map/ppermute | solution.py:593
  41.8 3.1 %collective-permute-start = (f32[136,128]{1,0:T(8,128)S(1)}, f32[136,128]{1,0:T(8,128)S(1)}, u32[]{:S(2)}, u32[]{:S(2)}) collective-permute-start(f32[136,128]{1,0:T(8,128)S(1)} %gather_sum.1.mine_ref), channel_id=1, source_target_pairs={{0,64},{1,65},{2,66},{3,67},{4,68},{5,69},{6,70},{7,71},{8,72},{9,... | collective-permute-start | bytes 208904 | tf_op jit(solution)/shard_map/ppermute | solution.py:593
  50.5 15.7 %all-to-all-start.1 = ((f32[64,512,1]{1,2,0:T(1,128)}), f32[64,512,1]{1,2,0:T(1,128)S(1)}, u32[]{:S(2)}, u32[]{:S(2)}) async-start(f32[64,512,1]{1,2,0:T(1,128)} %bitcast.9), calls=%async_computation.1 | async-start | bytes 262144 | tf_op jit(solution)/shard_map/all_to_all | solution.py:596
  57.6 8.6 %copy-start = (s32[1,16384]{1,0:T(1,128)S(1)}, s32[1,16384]{1,0:T(1,128)}, u32[]{:S(2)}) copy-start(s32[1,16384]{1,0:T(1,128)} %get-tuple-element.16.slot_ref) | copy-start | bytes 196612
  74.5 2.5 %collective-permute-start.2 = (f32[1,16384]{1,0:T(1,128)S(1)}, f32[1,16384]{1,0:T(1,128)S(1)}, u32[]{:S(2)}, u32[]{:S(2)}) collective-permute-start(f32[1,16384]{1,0:T(1,128)S(1)} %get-tuple-element.22), channel_id=1, source_target_pairs={{0,64},{1,65},{2,66},{3,67},{4,68},{5,69},{6,70},{7,71},{8,72},{9,... | collective-permute-start | bytes 196616 | tf_op jit(solution)/shard_map/ppermute | solution.py:593

commit v5 on v4

--- a/solution.py
+++ b/solution.py
@@ -11,7 +11,7 @@
 PARAMS = pltpu.CompilerParams(vmem_limit_bytes=24 << 20)
 MIDDLE = pltpu.CompilerParams(vmem_limit_bytes=52 << 20)
 LARGE = pltpu.CompilerParams(vmem_limit_bytes=60 << 20)
-ROWS = 11
+ROWS = 9
 FACE_CHUNK = 2048
 PIECE = 256
 SLOT_STEP = 8
@@ -101,6 +101,7 @@
         before_ref,
         after_ref,
         weight_ref,
+        op_ref,
         out_ref,
         slot_ref,
         carry,
@@ -110,6 +111,7 @@
         weight,
         first_face,
         first_side,
+        leads,
     ):
         i = pl.program_id(0)
         gas = lax.axis_index("grp") == 0
@@ -125,20 +127,25 @@
             first_face[0:1, :] = patch[:, :L]
             first_face[1:2, :] = point[:, :L]
             first_side[...] = side[:, :L]
+            lead = jnp.where(iota((8, nl), 0) == 0, 1.0, 0.0) * jnp.where(iota((8, nl), 1) == 0, 1.0, 0.0)
+            leads[0:1, :] = lead[0:1]
+            for n in range(1, ITERS):
+                lead = dot(lead, op_ref[...], precision=HIGHEST)
+                leads[n : n + 1, :] = lead[0:1]
+            leads[ITERS:, :] = lead[ITERS:]
 
         named = iota((blocks, c), 0) == patch
         hot = onehot(hits(patch.astype(f32), blocks))
-        wide = (sub, sub + L)
-        upto = jnp.where((iota(wide, 0) <= iota(wide, 1)) | (iota(wide, 1) >= sub), 1.0, 0.0).astype(bf16)
+        upto = jnp.where(iota((sub, sub), 0) <= iota((sub, sub), 1), 1.0, 0.0).astype(bf16)
         cuts = [slice(j * sub, (j + 1) * sub) for j in range(c // sub)]
         counts = dot(jnp.concatenate([hot[:, cut] for cut in cuts], axis=0), upto)
         before = carry[...]
         ranks = []
         for j, cut in enumerate(cuts):
             count = counts[j * blocks : (j + 1) * blocks]
-            total = count[:, :sub] + jnp.concatenate([before] * (sub // L), axis=1)
+            total = count + jnp.concatenate([before] * (sub // L), axis=1)
             ranks.append(jnp.sum(jnp.where(named[:, cut], total, 0.0), axis=0, keepdims=True))
-            before = before + count[:, sub:]
+            before = before + jnp.broadcast_to(count[:, sub - 1 :], (blocks, L))
         carry[...] = before
         rank = jnp.concatenate(ranks, axis=1).astype(i32) - 1
         slot = patch * capacity + rank
@@ -186,19 +193,16 @@
                 info = jnp.where(spot == at, jnp.where((to == name) & alive, target.astype(f32), -1.0), info)
                 name, target = edge_of(name, target, width)
                 info = jnp.where(spot == at + 2, jnp.where((to == name) & alive, target.astype(f32), -1.0), info)
+            block = lax.axis_index("blk")
+            for near, columns, base in ((block - 1, first_side[...], 0), (block + 1, side[:, c - L :], L - HALO)):
+                led = dot(leads[...], columns, precision=HIGHEST)
+                for n in range(ITERS):
+                    at = 16 + HALO * n
+                    here = (spot >= at) & (spot < at + HALO) & (to == near)
+                    info = jnp.where(here, pltpu.roll(led[n : n + 1], (at - base) % L, 1), info)
             out_ref[pl.ds(2 * per, blocks, stride=ROWS), :] = info
-            block = lax.axis_index("blk")
-            half = spot[:1] < L // 2
-            left, right = transposed(first_side[...]), transposed(side[:, c - L :])
-            for r in range(2):
-                rows = []
-                for ends, base in ((left, 0), (right, L - HALO)):
-                    j = base + 2 * r
-                    rows.append(jnp.where(half, ends[j : j + 1], pltpu.roll(ends[j + 1 : j + 2], L // 2, 1)))
-                sent = jnp.where(to == block - 1, rows[0], jnp.where(to == block + 1, rows[1], 0.0))
-                out_ref[pl.ds(2 * per + 1 + r, blocks, stride=ROWS), :] = sent
-
-    def call(live_count, patch, point, impinged, load, side, weights):
+
+    def call(live_count, patch, point, impinged, load, side, weights, op):
         nl = side.shape[0]
         row = pl.BlockSpec((1, c), lambda i: (0, i))
         return pl.pallas_call(
@@ -214,6 +218,7 @@
                 pl.BlockSpec((8, L), lambda i: (0, jnp.maximum(i * (c // L) - 1, 0))),
                 pl.BlockSpec((8, L), lambda i: (0, jnp.minimum((i + 1) * (c // L), width // L - 1))),
                 pl.BlockSpec(weights.shape, lambda i: (0, 0)),
+                pl.BlockSpec(op.shape, lambda i: (0, 0)),
             ],
             out_specs=[pl.BlockSpec((blocks * ROWS, L), lambda i: (0, 0)), row],
             out_shape=[
@@ -228,10 +233,11 @@
                 pltpu.VMEM((nl, L), f32),
                 pltpu.VMEM((8, L), i32),
                 pltpu.VMEM((nl, L), f32),
+                pltpu.VMEM((8, nl), f32),
             ],
             compiler_params=LARGE,
             name="route",
-        )(live_count, patch, point, impinged, load, side, side, side, weights)
+        )(live_count, patch, point, impinged, load, side, side, side, weights, op)
 
     return call
 
@@ -350,10 +356,8 @@
         block, source = lax.axis_index("blk"), iota((blocks, L), 0)
         rows = [edge]
         for near in (block - 1, block + 1):
-            for r in range(2):
-                columns = x_ref[pl.ds(2 * per + 1 + r, blocks, stride=ROWS), :]
-                rows.append(jnp.sum(jnp.where(source == near, columns, 0.0), axis=0, keepdims=True))
-        out_ref[pl.ds(tall, 8), :] = jnp.concatenate(rows + [jnp.zeros((3, L), f32)], axis=0)
+            rows.append(jnp.sum(jnp.where(source == near, info, 0.0), axis=0, keepdims=True))
+        out_ref[pl.ds(tall, 8), :] = jnp.concatenate(rows + [jnp.zeros((5, L), f32)], axis=0)
 
     def call(x):
         return pl.pallas_call(
@@ -406,20 +410,11 @@
 
         lead = rows(tail + 8, 8)
         near = jnp.where(gas, other[tall:], mine[tall:])
-        half = lane[:1] < L // 2
-
-        def columns(a):
-            for x in (near[a : a + 1], near[a + 1 : a + 2]):
-                yield jnp.where(half, x, 0.0)
-                yield jnp.where(half, pltpu.roll(x, L // 2, 1), 0.0)
-
-        gap = jnp.zeros((L - 2 * HALO, L), f32)
-        halo = jnp.concatenate([*columns(3), gap, *columns(1)], axis=0)
-        halo = dot(rows(tail, 8), halo, NT, precision=HIGHEST)
 
         def base(n):
-            edge = halo[n : n + 1]
-            return extend(rows(n * tall, tall), edge, edge)
+            at = 16 + HALO * n
+            edges = [pltpu.roll(near[k : k + 1], (to - at) % L, 1) for k, to in ((1, L - HALO), (2, 0))]
+            return extend(rows(n * tall, tall), *edges)
 
         sources = []
         row = base(0)
@@ -521,61 +516,65 @@
     c = FACE_CHUNK
     steps = width // c
     tall = width // L
-    part = c // L
     highs = blocks * capacity // L
 
-    def kernel(live_ref, reply_ref, slot_ref, y_ref, coef_ref, surface_ref, out_ref, found_ref, rows_ref, table):
-        i = pl.program_id(0)
+    def kernel(live_ref, reply_ref, slot_ref, y_hbm, coef_ref, surface_ref, out_hbm, found_ref, rows_ref, buffer, arrive, leave):
         gas = lax.axis_index("grp") == 0
 
-        @pl.when(i == 0)
-        def _():
-            high, low = split(reply_ref[...].T)
-            table[...] = jnp.concatenate([high, low], axis=0).astype(bf16)
-
+        def incoming(i):
+            return pltpu.make_async_copy(y_hbm.at[:, pl.ds(i * c, c)], buffer.at[i], arrive.at[i])
+
+        def outgoing(i):
+            return pltpu.make_async_copy(buffer.at[i], out_hbm.at[:, pl.ds(i * c, c)], leave.at[i])
+
+        for i in range(steps):
+            incoming(i).start()
+        high, low = split(reply_ref[...].T)
+        table = jnp.concatenate([high, low], axis=0).astype(bf16)
         coupling = jnp.broadcast_to(jnp.where(gas, coef_ref[:, 0:1], 0.0), (nl, L))
-        for j in range(c // PIECE):
-            piece = slice(j * PIECE, (j + 1) * PIECE)
-            slot = slot_ref[:, piece]
-            hot = onehot(hits((slot >> 7).astype(f32), highs))
-            found = dot(table[...], hot)
-            found = found[:L] + found[L:]
-            low = iota((L, PIECE), 0) == (slot & (L - 1))
-            live = (iota((1, PIECE), 1) + (i * c + j * PIECE)) < live_ref[0]
-            picked = jnp.where(live, jnp.sum(jnp.where(low, found, 0.0), axis=0, keepdims=True), 0.0)
-            found_ref[:, piece] = picked
-            for k in range(PIECE // L):
-                m = j * (PIECE // L) + k
-                cut = slice(m * L, (m + 1) * L)
-                one = picked[:, k * L : (k + 1) * L]
-                out_ref[:, cut] = y_ref[:, cut] + coupling * one
-                rows_ref[0:1, cut] = jnp.where(gas, one, surface_ref[0, m : m + 1])
-                rows_ref[1:2, cut] = surface_ref[1, m : m + 1]
-
-    def call(live_count, reply, slot, y, coef, surface):
-        row = pl.BlockSpec((1, c), lambda i: (0, i))
-        wide = pl.BlockSpec((nl, c), lambda i: (0, i))
+        for i in range(steps):
+            incoming(i).wait()
+            for j in range(c // PIECE):
+                start = i * c + j * PIECE
+                piece = slice(start, start + PIECE)
+                slot = slot_ref[:, piece]
+                found = dot(table, onehot(hits((slot >> 7).astype(f32), highs)))
+                low = iota((L, PIECE), 0) == (slot & (L - 1))
+                live = (iota((1, PIECE), 1) + start) < live_ref[0]
+                picked = jnp.sum(jnp.where(low, found[:L] + found[L:], 0.0), axis=0, keepdims=True)
+                picked = jnp.where(live, picked, 0.0)
+                found_ref[:, piece] = picked
+                for k in range(PIECE // L):
+                    m = start // L + k
+                    cut = slice(m * L, (m + 1) * L)
+                    here = slice(j * PIECE + k * L, j * PIECE + (k + 1) * L)
+                    one = picked[:, k * L : (k + 1) * L]
+                    buffer[i, :, here] = buffer[i, :, here] + coupling * one
+                    rows_ref[0:1, cut] = jnp.where(gas, one, surface_ref[m : m + 1])
+                    rows_ref[1:2, cut] = surface_ref[tall + m : tall + m + 1]
+            outgoing(i).start()
+        for i in range(steps):
+            outgoing(i).wait()
+
+    def call(*args):
+        vmem, anywhere = pl.BlockSpec(memory_space=pltpu.VMEM), pl.BlockSpec(memory_space=pl.ANY)
         return pl.pallas_call(
             kernel,
-            grid=(steps,),
-            in_specs=[
-                pl.BlockSpec(memory_space=pltpu.SMEM),
-                pl.BlockSpec((highs, L), lambda i: (0, 0)),
-                row,
-                wide,
-                pl.BlockSpec((nl, L), lambda i: (0, 0)),
-                pl.BlockSpec((2, part, L), lambda i: (0, i, 0)),
-            ],
-            out_specs=[wide, row, pl.BlockSpec((2, c), lambda i: (0, i))],
+            in_specs=[pl.BlockSpec(memory_space=pltpu.SMEM), vmem, vmem, anywhere, vmem, vmem],
+            out_specs=[anywhere, vmem, vmem],
             out_shape=[
                 jax.ShapeDtypeStruct((nl, width), f32),
                 jax.ShapeDtypeStruct((1, width), f32),
                 jax.ShapeDtypeStruct((2, width), f32),
             ],
-            scratch_shapes=[pltpu.VMEM((2 * L, highs), bf16)],
+            scratch_shapes=[
+                pltpu.VMEM((steps, nl, c), f32),
+                pltpu.SemaphoreType.DMA((steps,)),
+                pltpu.SemaphoreType.DMA((steps,)),
+            ],
             compiler_params=MIDDLE,
             name="face_finish",
-        )(live_count, reply, slot, y, coef, surface.reshape(2, tall, L))
+        )(*args)
 
     return call
 
@@ -596,7 +595,7 @@
         return lax.all_to_all(x.reshape(-1), "blk", split_axis=0, concat_axis=0, tiled=True).reshape(x.shape)
 
     faces = [x.reshape(1, width) for x in (face_patch, face_point, impinged, crystal_load)]
-    message, slot = route(width, blocks, capacity)(live_count, *faces, side, normal_weights)
+    message, slot = route(width, blocks, capacity)(live_count, *faces, side, normal_weights, matrix)
     arrived = exchange(message)
     y, rows, coef = matrices(nl, width)(matrix, normal_weights, side)
     rows_other = across(rows)

time: 78.5 us -> 76.9 us (0.980)
  Pallas kernels: 47.5 us -> 45.9 us
  starting transfers between devices: 23.8 us -> 24.7 us
  waiting for transfers between devices: 4.28 us -> 3.49 us
    pallas_call x2 -> x1, Pallas kernels: 20.1 us -> 13 us  [call(): pl.pallas_call(kernel, grid=(steps,), in_specs=[pl.BlockSpec(memory_space...]
    pallas_call x0 -> x1, Pallas kernels: none -> 5.88 us  [call(): pl.pallas_call(kernel, in_specs=[pl.BlockSpec(memory_space=pltpu.SMEM), v...]
    all_to_all x2, waiting for transfers between devices: 2.48 us -> 1.69 us  [exchange(): lax.all_to_all(x.reshape(-1), 'blk', split_axis=0, concat_axis=0, tiled=T...]
where the time goes in v5:
time: 76.9 us; the launch traced here: 76.3 us
  Pallas kernels  45.9 us (60%)
  starting transfers between devices  24.7 us (32%)
  waiting for transfers between devices  3.49 us (5%)
  between operations  1.37 us (2%)
  other arithmetic  0.79 us (1%)
    all_to_all x2, starting transfers between devices, exchange(): lax.all_to_all(x.reshape(-1), 'blk', split_axis=0, concat_axis=0, tiled=T...  19.8 us
    pallas_call x1, Pallas kernels, call(): pl.pallas_call(kernel, grid=(steps,), in_specs=[pl.BlockSpec(memory_space...  13 us
    pallas_call x1, Pallas kernels, call(): pl.pallas_call(kernel, grid=(steps,), in_specs=[pl.BlockSpec((nl, nl), la...  8.01 us
    pallas_call x1, Pallas kernels, call(): pl.pallas_call(kernel, grid=(width // c,), in_specs=[wide, pl.BlockSpec((...  7.43 us
    pallas_call x1, Pallas kernels, call(): pl.pallas_call(kernel, out_shape=jax.ShapeDtypeStruct((tall + 8, L), f32)...  6.2 us
    pallas_call x1, Pallas kernels, call(): pl.pallas_call(kernel, in_specs=[pl.BlockSpec(memory_space=pltpu.SMEM), v...  5.88 us
    pallas_call x1, Pallas kernels, call(): pl.pallas_call(kernel, in_specs=[vmem] * 6, out_shape=[jax.ShapeDtypeStru...  5.45 us
    ppermute x3, starting transfers between devices, across(): return lax.ppermute(x, ('grp', 'blk'), swap)  4.9 us
  transfers between devices with their start and end apart: 5, of which 4 were waited for; matrix products, arithmetic and copies ran while one was open for 0% of the time, Pallas kernels for 28%

profile of v5, /device:TPU:1, one launch (start us, length us, event | category | flops | bytes accessed | tf_op | source)
XLA Modules:
  0.0 76.3 jit_solution(4402235292489005020)
XLA Ops:
  1.3 0.0 copy-start
  1.3 0.0 copy-start.3
  1.3 13.0 %route.1 = (f32[576,128]{1,0:T(8,128)}, s32[1,16384]{1,0:T(1,128)}) custom-call(s32[1]{0:T(128)S(6)} %copy.13.live_ref, s32[1,16384]{1,0:T(1,128)} %bitcast.28, s32[1,16384]{1,0:T(1,128)} %bitcast.29, s32[1,16384]{1,0:T(1,128)} %bitcast.30, f32[1,16384]{1,0:T(1,128)} %bitcast.31, f32[64,16384]{1,0:T(8,128)} %bitcast.23, f32[64,16384]{1,0:T(8,128)} %bitcast.24, ...), custom_call_target="tpu_custom_call" | custom-call | tf_op jit(solution)/shard_map/route/pallas_call | solution.py:208
  14.3 0.0 copy-start.2
  14.3 12.1 %all-to-all-start = ((f32[64,1152,1]{1,2,0:T(1,128)}), f32[64,1152,1]{1,2,0:T(1,128)S(1)}, u32[]{:S(2)}, u32[]{:S(2)}) async-start(f32[64,1152,1]{1,2,0:T(1,128)} %bitcast.27), calls=%async_computation | async-start | bytes 589824 | tf_op jit(solution)/shard_map/all_to_all | solution.py:595
  26.4 0.0 copy-done
  26.4 0.0 copy-done.3
  26.4 8.0 %matrices.1 = (f32[64,16384]{1,0:T(8,128)}, f32[656,128]{1,0:T(8,128)S(1)}, f32[64,128]{1,0:T(8,128)S(1)}) custom-call(f32[64,64]{1,0:T(8,128)S(1)} %bitcast.21, f32[2,64]{1,0:T(2,128)S(1)} %copy-done.3, f32[64,16384]{1,0:T(8,128)} %bitcast.26), custom_call_target="tpu_custom_call" | custom-call | tf_op jit(solution)/shard_map/matrices/pallas_call | solution.py:286
  34.4 1.0 %collective-permute-start.1 = (f32[656,128]{1,0:T(8,128)S(1)}, f32[656,128]{1,0:T(8,128)S(1)}, u32[]{:S(2)}, u32[]{:S(2)}) collective-permute-start(f32[656,128]{1,0:T(8,128)S(1)} %get-tuple-element.14.rows_mine), channel_id=1, source_target_pairs={{0,64},{1,65},{2,66},{3,67},{4,68},{5,69},{6,70},{7,71},{8,72},{9,... | collective-permute-start | bytes 1007624 | tf_op jit(solution)/shard_map/ppermute | solution.py:592
  35.4 0.5 all-to-all-done
  35.8 6.2 %gather_sum.1.mine_ref = f32[136,128]{1,0:T(8,128)S(1)} custom-call(f32[576,128]{1,0:T(8,128)S(1)} %bitcast.16), custom_call_target="tpu_custom_call" | custom-call | tf_op jit(solution)/shard_map/gather_sum/pallas_call | solution.py:363
  42.0 2.3 %collective-permute-start = (f32[136,128]{1,0:T(8,128)S(1)}, f32[136,128]{1,0:T(8,128)S(1)}, u32[]{:S(2)}, u32[]{:S(2)}) collective-permute-start(f32[136,128]{1,0:T(8,128)S(1)} %gather_sum.1.mine_ref), channel_id=1, source_target_pairs={{0,64},{1,65},{2,66},{3,67},{4,68},{5,69},{6,70},{7,71},{8,72},{9,... | collective-permute-start | bytes 208904 | tf_op jit(solution)/shard_map/ppermute | solution.py:592
  44.3 0.0 collective-permute-done.1.rows_other
  44.3 0.9 %collective-permute-done.other_ref = f32[136,128]{1,0:T(8,128)S(1)} collective-permute-done((f32[136,128]{1,0:T(8,128)S(1)}, f32[136,128]{1,0:T(8,128)S(1)}, u32[]{:S(2)}, u32[]{:S(2)}) %collective-permute-start) | collective-permute-done | bytes 69664 | tf_op jit(solution)/shard_map/ppermute | solution.py:592
  45.3 0.0 copy-done.2
  45.3 5.5 %surface_lookup.1 = (f32[256,128]{1,0:T(8,128)}, f32[512,128]{1,0:T(8,128)S(1)}, f32[256,128]{1,0:T(8,128)S(1)}) custom-call(f32[136,128]{1,0:T(8,128)S(1)} %gather_sum.1.mine_ref, f32[136,128]{1,0:T(8,128)S(1)} %collective-permute-done.other_ref, f32[656,128]{1,0:T(8,128)S(1)} %get-tuple-element.14.rows_mine, ...), custom_call_target="tpu_custom_call" | custom-call | tf_op jit(solution)/shard_map/surface_lookup/pallas_call | solution.py:458
  50.7 7.7 %all-to-all-start.1 = ((f32[64,512,1]{1,2,0:T(1,128)}), f32[64,512,1]{1,2,0:T(1,128)S(1)}, u32[]{:S(2)}, u32[]{:S(2)}) async-start(f32[64,512,1]{1,2,0:T(1,128)} %bitcast.9), calls=%async_computation.1 | async-start | bytes 262144 | tf_op jit(solution)/shard_map/all_to_all | solution.py:595
  58.4 7.4 %add_sources.1.y_hbm = f32[64,16384]{1,0:T(8,128)} custom-call(f32[64,16384]{1,0:T(8,128)} %get-tuple-element.17.y_ref, f32[64,128]{1,0:T(8,128)S(1)} %get-tuple-element.18.coef_ref, f32[4,128,128]{2,1,0:T(8,128)S(1)} %bitcast.19), custom_call_target="tpu_custom_call" | custom-call | tf_op jit(solution)/shard_map/add_sources/pallas_call | solution.py:498
  65.9 1.2 %all-to-all-done.1 = f32[64,512,1]{1,2,0:T(1,128)S(1)} async-done(((f32[64,512,1]{1,2,0:T(1,128)}), f32[64,512,1]{1,2,0:T(1,128)S(1)}, u32[]{:S(2)}, u32[]{:S(2)}) %all-to-all-start.1) | async-done | bytes 131104 | tf_op jit(solution)/shard_map/all_to_all | solution.py:595
  67.1 0.0 copy-done.1
  67.1 5.9 %face_finish.1 = (f32[64,16384]{1,0:T(8,128)}, f32[1,16384]{1,0:T(1,128)S(1)}, f32[2,16384]{1,0:T(2,128)S(1)}) custom-call(s32[1]{0:T(128)S(6)} %copy.13.live_ref, f32[256,128]{1,0:T(8,128)S(1)} %bitcast.18, s32[1,16384]{1,0:T(1,128)S(1)} %copy-done.1, f32[64,16384]{1,0:T(8,128)} %add_sources.1.y_hbm, f32[64,128]{1,0:T(8,128)S(1)} %get-tuple-element.18.coef_ref, ...), custom_call_target="tpu_custom_call" | custom-call | tf_op jit(solution)/shard_map/face_finish/pallas_call | solution.py:561
  73.0 1.7 %collective-permute-start.2 = (f32[1,16384]{1,0:T(1,128)S(1)}, f32[1,16384]{1,0:T(1,128)S(1)}, u32[]{:S(2)}, u32[]{:S(2)}) collective-permute-start(f32[1,16384]{1,0:T(1,128)S(1)} %get-tuple-element.22), channel_id=1, source_target_pairs={{0,64},{1,65},{2,66},{3,67},{4,68},{5,69},{6,70},{7,71},{8,72},{9,... | collective-permute-start | bytes 196616 | tf_op jit(solution)/shard_map/ppermute | solution.py:592
  74.6 0.9 %collective-permute-done.2 = f32[1,16384]{1,0:T(1,128)S(1)} collective-permute-done((f32[1,16384]{1,0:T(1,128)S(1)}, f32[1,16384]{1,0:T(1,128)S(1)}, u32[]{:S(2)}, u32[]{:S(2)}) %collective-permute-start.2) | collective-permute-done | bytes 65568 | tf_op jit(solution)/shard_map/ppermute | solution.py:592
  75.5 0.8 %select_bitcast_fusion = f32[1,2,16384]{2,1,0:T(2,128)} fusion(f32[2,16384]{1,0:T(2,128)S(1)} %get-tuple-element.23, pred[2]{0:T(512)(128)(4,1)S(1)} %compare_and_fusion, f32[16384]{0:T(1024)S(1)} %bitcast.32), kind=kLoop, calls=%fused_computation | loop fusion | flops 32768 | bytes 327682 | tf_op jit(solution)/shard_map/broadcast_in_dim | solution.py:611
  (2 shorter events, 0.0 us)
Async XLA Ops:
  1.3 25.1 %copy-start = (f32[1,64,64]{2,1,0:T(8,128)S(1)}, f32[1,64,64]{2,1,0:T(8,128)}, u32[]{:S(2)}) copy-start(f32[1,64,64]{2,1,0:T(8,128)} %param.10) | copy-start | bytes 49156
  1.3 25.1 %copy-start.3 = (f32[2,64]{1,0:T(2,128)S(1)}, f32[2,64]{1,0:T(2,128)}, u32[]{:S(2)}) copy-start(f32[2,64]{1,0:T(2,128)} %weight_ref.3) | copy-start | bytes 1540
  14.3 31.0 %copy-start.2 = (f32[16384]{0:T(1024)S(1)}, f32[16384]{0:T(1024)}, u32[]{:S(2)}) copy-start(f32[16384]{0:T(1024)} %param.17) | copy-start | bytes 196612
  14.3 21.6 %all-to-all-start = ((f32[64,1152,1]{1,2,0:T(1,128)}), f32[64,1152,1]{1,2,0:T(1,128)S(1)}, u32[]{:S(2)}, u32[]{:S(2)}) async-start(f32[64,1152,1]{1,2,0:T(1,128)} %bitcast.27), calls=%async_computation | async-start | bytes 589824 | tf_op jit(solution)/shard_map/all_to_all | solution.py:595
  34.4 9.9 %collective-permute-start.1 = (f32[656,128]{1,0:T(8,128)S(1)}, f32[656,128]{1,0:T(8,128)S(1)}, u32[]{:S(2)}, u32[]{:S(2)}) collective-permute-start(f32[656,128]{1,0:T(8,128)S(1)} %get-tuple-element.14.rows_mine), channel_id=1, source_target_pairs={{0,64},{1,65},{2,66},{3,67},{4,68},{5,69},{6,70},{7,71},{8,72},{9,... | collective-permute-start | bytes 1007624 | tf_op jit(solution)/shard_map/ppermute | solution.py:592
  42.0 3.2 %collective-permute-start = (f32[136,128]{1,0:T(8,128)S(1)}, f32[136,128]{1,0:T(8,128)S(1)}, u32[]{:S(2)}, u32[]{:S(2)}) collective-permute-start(f32[136,128]{1,0:T(8,128)S(1)} %gather_sum.1.mine_ref), channel_id=1, source_target_pairs={{0,64},{1,65},{2,66},{3,67},{4,68},{5,69},{6,70},{7,71},{8,72},{9,... | collective-permute-start | bytes 208904 | tf_op jit(solution)/shard_map/ppermute | solution.py:592
  50.7 16.4 %all-to-all-start.1 = ((f32[64,512,1]{1,2,0:T(1,128)}), f32[64,512,1]{1,2,0:T(1,128)S(1)}, u32[]{:S(2)}, u32[]{:S(2)}) async-start(f32[64,512,1]{1,2,0:T(1,128)} %bitcast.9), calls=%async_computation.1 | async-start | bytes 262144 | tf_op jit(solution)/shard_map/all_to_all | solution.py:595
  58.4 8.6 %copy-start.1 = (s32[1,16384]{1,0:T(1,128)S(1)}, s32[1,16384]{1,0:T(1,128)}, u32[]{:S(2)}) copy-start(s32[1,16384]{1,0:T(1,128)} %get-tuple-element.16.slot_ref) | copy-start | bytes 196612
  73.0 2.6 %collective-permute-start.2 = (f32[1,16384]{1,0:T(1,128)S(1)}, f32[1,16384]{1,0:T(1,128)S(1)}, u32[]{:S(2)}, u32[]{:S(2)}) collective-permute-start(f32[1,16384]{1,0:T(1,128)S(1)} %get-tuple-element.22), channel_id=1, source_target_pairs={{0,64},{1,65},{2,66},{3,67},{4,68},{5,69},{6,70},{7,71},{8,72},{9,... | collective-permute-start | bytes 196616 | tf_op jit(solution)/shard_map/ppermute | solution.py:592

commit v6 on v5

--- a/solution.py
+++ b/solution.py
@@ -97,147 +97,130 @@
         point_ref,
         impinged_ref,
         load_ref,
-        side_ref,
-        before_ref,
-        after_ref,
+        side_hbm,
         weight_ref,
         op_ref,
         out_ref,
         slot_ref,
-        carry,
         acc,
         spots,
-        eacc,
-        weight,
-        first_face,
-        first_side,
-        leads,
+        buffer,
+        arrive,
     ):
-        i = pl.program_id(0)
         gas = lax.axis_index("grp") == 0
-        patch, point, side = patch_ref[...], point_ref[...], side_ref[...]
-
-        @pl.when(i == 0)
-        def _():
-            carry[...] = jnp.zeros_like(carry)
-            acc[...] = jnp.zeros_like(acc)
-            eacc[...] = jnp.zeros_like(eacc)
-            nl = side.shape[0]
-            weight[...] = transposed(weight_ref[...])[:nl]
-            first_face[0:1, :] = patch[:, :L]
-            first_face[1:2, :] = point[:, :L]
-            first_side[...] = side[:, :L]
-            lead = jnp.where(iota((8, nl), 0) == 0, 1.0, 0.0) * jnp.where(iota((8, nl), 1) == 0, 1.0, 0.0)
-            leads[0:1, :] = lead[0:1]
-            for n in range(1, ITERS):
-                lead = dot(lead, op_ref[...], precision=HIGHEST)
-                leads[n : n + 1, :] = lead[0:1]
-            leads[ITERS:, :] = lead[ITERS:]
-
-        named = iota((blocks, c), 0) == patch
-        hot = onehot(hits(patch.astype(f32), blocks))
-        upto = jnp.where(iota((sub, sub), 0) <= iota((sub, sub), 1), 1.0, 0.0).astype(bf16)
-        cuts = [slice(j * sub, (j + 1) * sub) for j in range(c // sub)]
-        counts = dot(jnp.concatenate([hot[:, cut] for cut in cuts], axis=0), upto)
-        before = carry[...]
-        ranks = []
-        for j, cut in enumerate(cuts):
-            count = counts[j * blocks : (j + 1) * blocks]
-            total = count + jnp.concatenate([before] * (sub // L), axis=1)
-            ranks.append(jnp.sum(jnp.where(named[:, cut], total, 0.0), axis=0, keepdims=True))
-            before = before + jnp.broadcast_to(count[:, sub - 1 :], (blocks, L))
-        carry[...] = before
-        rank = jnp.concatenate(ranks, axis=1).astype(i32) - 1
-        slot = patch * capacity + rank
-        slot_ref[...] = slot
-
-        lane = iota((1, c), 1)
-        live = (lane + i * c) < live_ref[0]
-        row = side[0:1]
-        ahead = jnp.where(lane == c - 1, jnp.where(i == steps - 1, 0.0, after_ref[0:1, 0:1]), pltpu.roll(row, c - 1, 1))
-        behind = jnp.where(lane == 0, jnp.where(i == 0, 0.0, before_ref[0:1, L - 1 : L]), pltpu.roll(row, 1, 1))
-        flux = jnp.sum(weight[:, 0:1] * side, axis=0, keepdims=True) + 0.25 * (behind + ahead - 2.0 * row)
-        crystal = impinged_ref[...].astype(f32) * load_ref[...]
-        value = jnp.where(live, jnp.where(gas, flux, crystal), 0.0)
-        v_high, v_low = split(value)
-        t_high, t_low = ((point >> 7).astype(f32), (point & (L - 1)).astype(f32))
-        high = onehot(hits((slot >> 7).astype(f32), highs))
-        low = hits((slot & (L - 1)).astype(f32), L)
-        laid = jnp.concatenate([masked(low, x) for x in (*halves(value), spread(t_high), spread(t_low))], axis=0)
-        placed = dot(laid, high, NT)
-        for q in range(4):
-            acc[pl.ds(q * L, L), :] += placed[q * L : (q + 1) * L]
-
-        edge_patch, edge_point = edge_of(patch, point, width)
-        edge_hot = onehot(hits(edge_patch.astype(f32), blocks))
-        edge_low = iota((8, c), 0) == edge_point
-        edges = jnp.concatenate([jnp.where(edge_low, x, 0.0) for x in (v_high, v_low)], axis=0).astype(bf16)
-        eacc[...] += dot(edges, edge_hot, NT)
-
-        @pl.when(i == steps - 1)
-        def _():
-            spots[pl.ds(0, highs), :] = (acc[:L] + acc[L : 2 * L]).T
-            spots[pl.ds(highs, highs), :] = (acc[2 * L : 3 * L] * float(L) + acc[3 * L :]).T
-            for r in range(per):
-                for q in range(2):
-                    out_ref[pl.ds(q * per + r, blocks, stride=ROWS), :] = spots[pl.ds(q * highs + r, blocks, stride=per), :]
-            spot, to = iota((blocks, L), 1), iota((blocks, L), 0)
-            info = transposed(eacc[0:8] + eacc[8:16])[:blocks]
-            info = jnp.where((spot == 8) & gas, first_side[0:1, 0:1], info)
-            info = jnp.where((spot == 9) & gas, row[:, c - 1 :], info)
-            ends = (
-                (10, first_face[0:1, 0:1], first_face[1:2, 0:1], live_ref[0] > 0),
-                (11, patch[:, c - 1 :], point[:, c - 1 :], live_ref[0] >= width),
-            )
-            for at, name, target, alive in ends:
-                info = jnp.where(spot == at, jnp.where((to == name) & alive, target.astype(f32), -1.0), info)
-                name, target = edge_of(name, target, width)
-                info = jnp.where(spot == at + 2, jnp.where((to == name) & alive, target.astype(f32), -1.0), info)
-            block = lax.axis_index("blk")
-            for near, columns, base in ((block - 1, first_side[...], 0), (block + 1, side[:, c - L :], L - HALO)):
-                led = dot(leads[...], columns, precision=HIGHEST)
-                for n in range(ITERS):
-                    at = 16 + HALO * n
-                    here = (spot >= at) & (spot < at + HALO) & (to == near)
-                    info = jnp.where(here, pltpu.roll(led[n : n + 1], (at - base) % L, 1), info)
-            out_ref[pl.ds(2 * per, blocks, stride=ROWS), :] = info
-
-    def call(live_count, patch, point, impinged, load, side, weights, op):
-        nl = side.shape[0]
-        row = pl.BlockSpec((1, c), lambda i: (0, i))
+        nl = op_ref.shape[0]
+
+        def incoming(i):
+            return pltpu.make_async_copy(side_hbm.at[:, pl.ds(i * c, c)], buffer.at[i], arrive.at[i])
+
+        for i in range(steps):
+            incoming(i).start()
+
+        wide = (sub, sub + L)
+        upto = jnp.where((iota(wide, 0) <= iota(wide, 1)) | (iota(wide, 1) >= sub), 1.0, 0.0).astype(bf16)
+        before = jnp.zeros((blocks, L), f32)
+        for i in range(steps):
+            patch = patch_ref[:, i * c : (i + 1) * c]
+            named = iota((blocks, c), 0) == patch
+            hot = onehot(hits(patch.astype(f32), blocks))
+            cuts = [slice(j * sub, (j + 1) * sub) for j in range(c // sub)]
+            counts = dot(jnp.concatenate([hot[:, cut] for cut in cuts], axis=0), upto)
+            ranks = []
+            for j, cut in enumerate(cuts):
+                count = counts[j * blocks : (j + 1) * blocks]
+                total = count[:, :sub] + jnp.concatenate([before] * (sub // L), axis=1)
+                ranks.append(jnp.sum(jnp.where(named[:, cut], total, 0.0), axis=0, keepdims=True))
+                before = before + count[:, sub:]
+            slot_ref[:, i * c : (i + 1) * c] = patch * capacity + jnp.concatenate(ranks, axis=1).astype(i32) - 1
+
+        weight = transposed(weight_ref[...])[:nl, 0:1]
+        lead = op_ref[0:8, :]
+        leads = [jnp.where(iota((1, nl), 1) == 0, 1.0, 0.0), lead[0:1]]
+        for _ in range(2, ITERS):
+            lead = dot(lead, op_ref[...], precision=HIGHEST)
+            leads.append(lead[0:1])
+        leads = jnp.concatenate(leads + [jnp.zeros((8 - ITERS, nl), f32)], axis=0)
+        for i in range(steps):
+            incoming(i).wait()
+
+        eacc = jnp.zeros((16, blocks), f32)
+        for i in range(steps):
+            part = slice(i * c, (i + 1) * c)
+            slot, point, side = slot_ref[:, part], point_ref[:, part], buffer[i]
+            lane = iota((1, c), 1)
+            live = (lane + i * c) < live_ref[0]
+            row = side[0:1]
+            after = buffer[i + 1, 0:1, 0:1] if i + 1 < steps else 0.0
+            prior = buffer[i - 1, 0:1, c - L :][:, L - 1 :] if i else 0.0
+            ahead = jnp.where(lane == c - 1, after, pltpu.roll(row, c - 1, 1))
+            behind = jnp.where(lane == 0, prior, pltpu.roll(row, 1, 1))
+            flux = jnp.sum(weight * side, axis=0, keepdims=True) + 0.25 * (behind + ahead - 2.0 * row)
+            crystal = impinged_ref[:, part].astype(f32) * load_ref[:, part]
+            value = jnp.where(live, jnp.where(gas, flux, crystal), 0.0)
+            t_high, t_low = ((point >> 7).astype(f32), (point & (L - 1)).astype(f32))
+            high = onehot(hits((slot >> 7).astype(f32), highs))
+            low = hits((slot & (L - 1)).astype(f32), L)
+            laid = jnp.concatenate([masked(low, x) for x in (*halves(value), spread(t_high), spread(t_low))], axis=0)
+            placed = dot(laid, high, NT)
+            for q in range(4):
+                rows = placed[q * L : (q + 1) * L]
+                acc[pl.ds(q * L, L), :] = rows if i == 0 else acc[pl.ds(q * L, L), :] + rows
+
+            v_high, v_low = split(value)
+            edge_patch, edge_point = edge_of(patch_ref[:, part], point, width)
+            edge_hot = onehot(hits(edge_patch.astype(f32), blocks))
+            edge_low = iota((8, c), 0) == edge_point
+            edges = jnp.concatenate([jnp.where(edge_low, x, 0.0) for x in (v_high, v_low)], axis=0).astype(bf16)
+            eacc = eacc + dot(edges, edge_hot, NT)
+
+        spots[pl.ds(0, highs), :] = (acc[:L] + acc[L : 2 * L]).T
+        spots[pl.ds(highs, highs), :] = (acc[2 * L : 3 * L] * float(L) + acc[3 * L :]).T
+        for r in range(per):
+            for q in range(2):
+                out_ref[pl.ds(q * per + r, blocks, stride=ROWS), :] = spots[pl.ds(q * highs + r, blocks, stride=per), :]
+        spot, to = iota((blocks, L), 1), iota((blocks, L), 0)
+        info = transposed(eacc[0:8] + eacc[8:16])[:blocks]
+        first, last = buffer[0, :, :L], buffer[steps - 1, :, c - L :]
+        info = jnp.where((spot == 8) & gas, first[0:1, 0:1], info)
+        info = jnp.where((spot == 9) & gas, last[0:1, L - 1 :], info)
+        patches, points = (patch_ref[:, :L], patch_ref[:, width - L :]), (point_ref[:, :L], point_ref[:, width - L :])
+        ends = (
+            (10, patches[0][:, 0:1], points[0][:, 0:1], live_ref[0] > 0),
+            (11, patches[1][:, L - 1 :], points[1][:, L - 1 :], live_ref[0] >= width),
+        )
+        for at, name, target, alive in ends:
+            info = jnp.where(spot == at, jnp.where((to == name) & alive, target.astype(f32), -1.0), info)
+            name, target = edge_of(name, target, width)
+            info = jnp.where(spot == at + 2, jnp.where((to == name) & alive, target.astype(f32), -1.0), info)
+        block = lax.axis_index("blk")
+        for near, columns, base in ((block - 1, first, 0), (block + 1, last, L - HALO)):
+            led = dot(leads, columns, precision=HIGHEST)
+            for n in range(ITERS):
+                at = 16 + HALO * n
+                here = (spot >= at) & (spot < at + HALO) & (to == near)
+                info = jnp.where(here, pltpu.roll(led[n : n + 1], (at - base) % L, 1), info)
+        out_ref[pl.ds(2 * per, blocks, stride=ROWS), :] = info
+
+    def call(*args):
+        nl = args[5].shape[0]
+        vmem, anywhere = pl.BlockSpec(memory_space=pltpu.VMEM), pl.BlockSpec(memory_space=pl.ANY)
         return pl.pallas_call(
             kernel,
-            grid=(steps,),
-            in_specs=[
-                pl.BlockSpec(memory_space=pltpu.SMEM),
-                row,
-                row,
-                row,
-                row,
-                pl.BlockSpec((nl, c), lambda i: (0, i)),
-                pl.BlockSpec((8, L), lambda i: (0, jnp.maximum(i * (c // L) - 1, 0))),
-                pl.BlockSpec((8, L), lambda i: (0, jnp.minimum((i + 1) * (c // L), width // L - 1))),
-                pl.BlockSpec(weights.shape, lambda i: (0, 0)),
-                pl.BlockSpec(op.shape, lambda i: (0, 0)),
-            ],
-            out_specs=[pl.BlockSpec((blocks * ROWS, L), lambda i: (0, 0)), row],
+            in_specs=[pl.BlockSpec(memory_space=pltpu.SMEM), vmem, vmem, vmem, vmem, anywhere, vmem, vmem],
+            out_specs=[vmem, vmem],
             out_shape=[
                 jax.ShapeDtypeStruct((blocks * ROWS, L), f32),
                 jax.ShapeDtypeStruct((1, width), i32),
             ],
             scratch_shapes=[
-                pltpu.VMEM((blocks, L), f32),
                 pltpu.VMEM((4 * L, highs), f32),
                 pltpu.VMEM((2 * highs, L), f32),
-                pltpu.VMEM((16, blocks), f32),
-                pltpu.VMEM((nl, L), f32),
-                pltpu.VMEM((8, L), i32),
-                pltpu.VMEM((nl, L), f32),
-                pltpu.VMEM((8, nl), f32),
+                pltpu.VMEM((steps, nl, c), f32),
+                pltpu.SemaphoreType.DMA((steps,)),
             ],
             compiler_params=LARGE,
             name="route",
-        )(live_count, patch, point, impinged, load, side, side, side, weights, op)
+        )(*args)
 
     return call
 

time: 76.9 us -> 74.5 us (0.969)
  Pallas kernels: 45.9 us -> 43.6 us
    pallas_call x1 -> x0, Pallas kernels: 13 us -> none  [call(): pl.pallas_call(kernel, grid=(steps,), in_specs=[pl.BlockSpec(memory_space...]
    pallas_call x1 -> x2, Pallas kernels: 5.88 us -> 16.5 us  [call(): pl.pallas_call(kernel, in_specs=[pl.BlockSpec(memory_space=pltpu.SMEM), v...]
  transfers between devices with their start and end apart: 5 -> 5, of which waited for: 4 -> 4; matrix products, arithmetic and copies ran while one was open for 0% -> 0% of each run, Pallas kernels for 28% -> 29%
where the time goes in v6:
time: 74.5 us; the launch traced here: 73.9 us
  Pallas kernels  43.6 us (59%)
  starting transfers between devices  24.7 us (33%)
  waiting for transfers between devices  3.33 us (4%)
  between operations  1.39 us (2%)
  other arithmetic  0.79 us (1%)
    all_to_all x2, starting transfers between devices, exchange(): lax.all_to_all(x.reshape(-1), 'blk', split_axis=0, concat_axis=0, tiled=T...  19.9 us
    pallas_call x2, Pallas kernels, call(): pl.pallas_call(kernel, in_specs=[pl.BlockSpec(memory_space=pltpu.SMEM), v...  16.5 us
    pallas_call x1, Pallas kernels, call(): pl.pallas_call(kernel, grid=(steps,), in_specs=[pl.BlockSpec((nl, nl), la...  8.02 us
    pallas_call x1, Pallas kernels, call(): pl.pallas_call(kernel, grid=(width // c,), in_specs=[wide, pl.BlockSpec((...  7.43 us
    pallas_call x1, Pallas kernels, call(): pl.pallas_call(kernel, out_shape=jax.ShapeDtypeStruct((tall + 8, L), f32)...  6.2 us
    pallas_call x1, Pallas kernels, call(): pl.pallas_call(kernel, in_specs=[vmem] * 6, out_shape=[jax.ShapeDtypeStru...  5.45 us
    ppermute x3, starting transfers between devices, across(): return lax.ppermute(x, ('grp', 'blk'), swap)  4.88 us
    ppermute x3, waiting for transfers between devices, across(): return lax.ppermute(x, ('grp', 'blk'), swap)  1.8 us
  transfers between devices with their start and end apart: 5, of which 4 were waited for; matrix products, arithmetic and copies ran while one was open for 0% of the time, Pallas kernels for 29%

profile of v6, /device:TPU:1, one launch (start us, length us, event | category | flops | bytes accessed | tf_op | source)
XLA Modules:
  0.0 73.9 jit_solution(15108207257637109528)
XLA Ops:
  0.6 0.0 copy-start.3
  0.6 0.0 copy-start
  1.3 0.0 copy-start.2
  1.3 10.6 %route.1 = (f32[576,128]{1,0:T(8,128)}, s32[1,16384]{1,0:T(1,128)}) custom-call(s32[1]{0:T(128)S(6)} %copy.13.live_ref, s32[1,16384]{1,0:T(1,128)} %bitcast.27, s32[1,16384]{1,0:T(1,128)} %bitcast.28, s32[1,16384]{1,0:T(1,128)} %bitcast.29, f32[1,16384]{1,0:T(1,128)} %bitcast.30, f32[64,16384]{1,0:T(8,128)} %bitcast.23, f32[2,64]{1,0:T(2,128)} %weight_ref.3, ...), custom_call_target="tpu_custom_call" | custom-call | tf_op jit(solution)/shard_map/route/pallas_call | solution.py:207
  12.0 12.0 %all-to-all-start = ((f32[64,1152,1]{1,2,0:T(1,128)}), f32[64,1152,1]{1,2,0:T(1,128)S(1)}, u32[]{:S(2)}, u32[]{:S(2)}) async-start(f32[64,1152,1]{1,2,0:T(1,128)} %bitcast.25), calls=%async_computation | async-start | bytes 589824 | tf_op jit(solution)/shard_map/all_to_all | solution.py:578
  23.9 0.0 copy-done.3
  23.9 0.0 copy-done
  24.0 8.0 %matrices.1 = (f32[64,16384]{1,0:T(8,128)}, f32[656,128]{1,0:T(8,128)S(1)}, f32[64,128]{1,0:T(8,128)S(1)}) custom-call(f32[64,64]{1,0:T(8,128)S(1)} %bitcast.21, f32[2,64]{1,0:T(2,128)S(1)} %copy-done.3, f32[64,16384]{1,0:T(8,128)} %bitcast.24), custom_call_target="tpu_custom_call" | custom-call | tf_op jit(solution)/shard_map/matrices/pallas_call | solution.py:269
  32.0 0.9 %collective-permute-start.1 = (f32[656,128]{1,0:T(8,128)S(1)}, f32[656,128]{1,0:T(8,128)S(1)}, u32[]{:S(2)}, u32[]{:S(2)}) collective-permute-start(f32[656,128]{1,0:T(8,128)S(1)} %get-tuple-element.14.rows_mine), channel_id=1, source_target_pairs={{0,64},{1,65},{2,66},{3,67},{4,68},{5,69},{6,70},{7,71},{8,72},{9,... | collective-permute-start | bytes 1007624 | tf_op jit(solution)/shard_map/ppermute | solution.py:575
  32.9 0.5 all-to-all-done
  33.4 6.2 %gather_sum.1.mine_ref = f32[136,128]{1,0:T(8,128)S(1)} custom-call(f32[576,128]{1,0:T(8,128)S(1)} %bitcast.16), custom_call_target="tpu_custom_call" | custom-call | tf_op jit(solution)/shard_map/gather_sum/pallas_call | solution.py:346
  39.6 2.3 %collective-permute-start = (f32[136,128]{1,0:T(8,128)S(1)}, f32[136,128]{1,0:T(8,128)S(1)}, u32[]{:S(2)}, u32[]{:S(2)}) collective-permute-start(f32[136,128]{1,0:T(8,128)S(1)} %gather_sum.1.mine_ref), channel_id=1, source_target_pairs={{0,64},{1,65},{2,66},{3,67},{4,68},{5,69},{6,70},{7,71},{8,72},{9,... | collective-permute-start | bytes 208904 | tf_op jit(solution)/shard_map/ppermute | solution.py:575
  41.9 0.0 collective-permute-done.1.rows_other
  41.9 0.9 %collective-permute-done.other_ref = f32[136,128]{1,0:T(8,128)S(1)} collective-permute-done((f32[136,128]{1,0:T(8,128)S(1)}, f32[136,128]{1,0:T(8,128)S(1)}, u32[]{:S(2)}, u32[]{:S(2)}) %collective-permute-start) | collective-permute-done | bytes 69664 | tf_op jit(solution)/shard_map/ppermute | solution.py:575
  42.8 0.0 copy-done.2
  42.8 5.5 %surface_lookup.1 = (f32[256,128]{1,0:T(8,128)}, f32[512,128]{1,0:T(8,128)S(1)}, f32[256,128]{1,0:T(8,128)S(1)}) custom-call(f32[136,128]{1,0:T(8,128)S(1)} %gather_sum.1.mine_ref, f32[136,128]{1,0:T(8,128)S(1)} %collective-permute-done.other_ref, f32[656,128]{1,0:T(8,128)S(1)} %get-tuple-element.14.rows_mine, ...), custom_call_target="tpu_custom_call" | custom-call | tf_op jit(solution)/shard_map/surface_lookup/pallas_call | solution.py:441
  48.3 7.9 %all-to-all-start.1 = ((f32[64,512,1]{1,2,0:T(1,128)}), f32[64,512,1]{1,2,0:T(1,128)S(1)}, u32[]{:S(2)}, u32[]{:S(2)}) async-start(f32[64,512,1]{1,2,0:T(1,128)} %bitcast.9), calls=%async_computation.1 | async-start | bytes 262144 | tf_op jit(solution)/shard_map/all_to_all | solution.py:578
  56.2 0.0 copy-start.1
  56.2 7.4 %add_sources.1.y_hbm = f32[64,16384]{1,0:T(8,128)} custom-call(f32[64,16384]{1,0:T(8,128)} %get-tuple-element.17.y_ref, f32[64,128]{1,0:T(8,128)S(1)} %get-tuple-element.18.coef_ref, f32[4,128,128]{2,1,0:T(8,128)S(1)} %bitcast.19), custom_call_target="tpu_custom_call" | custom-call | tf_op jit(solution)/shard_map/add_sources/pallas_call | solution.py:481
  63.6 1.0 %all-to-all-done.1 = f32[64,512,1]{1,2,0:T(1,128)S(1)} async-done(((f32[64,512,1]{1,2,0:T(1,128)}), f32[64,512,1]{1,2,0:T(1,128)S(1)}, u32[]{:S(2)}, u32[]{:S(2)}) %all-to-all-start.1) | async-done | bytes 131104 | tf_op jit(solution)/shard_map/all_to_all | solution.py:578
  64.6 5.9 %face_finish.1 = (f32[64,16384]{1,0:T(8,128)}, f32[1,16384]{1,0:T(1,128)S(1)}, f32[2,16384]{1,0:T(2,128)S(1)}) custom-call(s32[1]{0:T(128)S(6)} %copy.13.live_ref, f32[256,128]{1,0:T(8,128)S(1)} %bitcast.18, s32[1,16384]{1,0:T(1,128)S(1)} %copy-done.1, f32[64,16384]{1,0:T(8,128)} %add_sources.1.y_hbm, f32[64,128]{1,0:T(8,128)S(1)} %get-tuple-element.18.coef_ref, ...), custom_call_target="tpu_custom_call" | custom-call | tf_op jit(solution)/shard_map/face_finish/pallas_call | solution.py:544
  70.5 1.7 %collective-permute-start.2 = (f32[1,16384]{1,0:T(1,128)S(1)}, f32[1,16384]{1,0:T(1,128)S(1)}, u32[]{:S(2)}, u32[]{:S(2)}) collective-permute-start(f32[1,16384]{1,0:T(1,128)S(1)} %get-tuple-element.22), channel_id=1, source_target_pairs={{0,64},{1,65},{2,66},{3,67},{4,68},{5,69},{6,70},{7,71},{8,72},{9,... | collective-permute-start | bytes 196616 | tf_op jit(solution)/shard_map/ppermute | solution.py:575
  72.2 0.9 %collective-permute-done.2 = f32[1,16384]{1,0:T(1,128)S(1)} collective-permute-done((f32[1,16384]{1,0:T(1,128)S(1)}, f32[1,16384]{1,0:T(1,128)S(1)}, u32[]{:S(2)}, u32[]{:S(2)}) %collective-permute-start.2) | collective-permute-done | bytes 65568 | tf_op jit(solution)/shard_map/ppermute | solution.py:575
  73.1 0.8 %select_bitcast_fusion = f32[1,2,16384]{2,1,0:T(2,128)} fusion(f32[2,16384]{1,0:T(2,128)S(1)} %get-tuple-element.23, pred[2]{0:T(512)(128)(4,1)S(1)} %compare_and_fusion, f32[16384]{0:T(1024)S(1)} %bitcast.26), kind=kLoop, calls=%fused_computation | loop fusion | flops 32768 | bytes 327682 | tf_op jit(solution)/shard_map/broadcast_in_dim | solution.py:594
  (2 shorter events, 0.0 us)
Async XLA Ops:
  0.6 23.3 %copy-start.3 = (f32[2,64]{1,0:T(2,128)S(1)}, f32[2,64]{1,0:T(2,128)}, u32[]{:S(2)}) copy-start(f32[2,64]{1,0:T(2,128)} %weight_ref.3) | copy-start | bytes 1540
  0.6 23.3 %copy-start = (f32[1,64,64]{2,1,0:T(8,128)S(1)}, f32[1,64,64]{2,1,0:T(8,128)}, u32[]{:S(2)}) copy-start(f32[1,64,64]{2,1,0:T(8,128)} %param.10) | copy-start | bytes 49156
  1.3 41.5 %copy-start.2 = (f32[16384]{0:T(1024)S(1)}, f32[16384]{0:T(1024)}, u32[]{:S(2)}) copy-start(f32[16384]{0:T(1024)} %param.17) | copy-start | bytes 196612
  12.0 21.5 %all-to-all-start = ((f32[64,1152,1]{1,2,0:T(1,128)}), f32[64,1152,1]{1,2,0:T(1,128)S(1)}, u32[]{:S(2)}, u32[]{:S(2)}) async-start(f32[64,1152,1]{1,2,0:T(1,128)} %bitcast.25), calls=%async_computation | async-start | bytes 589824 | tf_op jit(solution)/shard_map/all_to_all | solution.py:578
  32.0 9.9 %collective-permute-start.1 = (f32[656,128]{1,0:T(8,128)S(1)}, f32[656,128]{1,0:T(8,128)S(1)}, u32[]{:S(2)}, u32[]{:S(2)}) collective-permute-start(f32[656,128]{1,0:T(8,128)S(1)} %get-tuple-element.14.rows_mine), channel_id=1, source_target_pairs={{0,64},{1,65},{2,66},{3,67},{4,68},{5,69},{6,70},{7,71},{8,72},{9,... | collective-permute-start | bytes 1007624 | tf_op jit(solution)/shard_map/ppermute | solution.py:575
  39.6 3.2 %collective-permute-start = (f32[136,128]{1,0:T(8,128)S(1)}, f32[136,128]{1,0:T(8,128)S(1)}, u32[]{:S(2)}, u32[]{:S(2)}) collective-permute-start(f32[136,128]{1,0:T(8,128)S(1)} %gather_sum.1.mine_ref), channel_id=1, source_target_pairs={{0,64},{1,65},{2,66},{3,67},{4,68},{5,69},{6,70},{7,71},{8,72},{9,... | collective-permute-start | bytes 208904 | tf_op jit(solution)/shard_map/ppermute | solution.py:575
  48.3 16.4 %all-to-all-start.1 = ((f32[64,512,1]{1,2,0:T(1,128)}), f32[64,512,1]{1,2,0:T(1,128)S(1)}, u32[]{:S(2)}, u32[]{:S(2)}) async-start(f32[64,512,1]{1,2,0:T(1,128)} %bitcast.9), calls=%async_computation.1 | async-start | bytes 262144 | tf_op jit(solution)/shard_map/all_to_all | solution.py:578
  56.2 8.5 %copy-start.1 = (s32[1,16384]{1,0:T(1,128)S(1)}, s32[1,16384]{1,0:T(1,128)}, u32[]{:S(2)}) copy-start(s32[1,16384]{1,0:T(1,128)} %get-tuple-element.16.slot_ref) | copy-start | bytes 196612
  70.5 2.6 %collective-permute-start.2 = (f32[1,16384]{1,0:T(1,128)S(1)}, f32[1,16384]{1,0:T(1,128)S(1)}, u32[]{:S(2)}, u32[]{:S(2)}) collective-permute-start(f32[1,16384]{1,0:T(1,128)S(1)} %get-tuple-element.22), channel_id=1, source_target_pairs={{0,64},{1,65},{2,66},{3,67},{4,68},{5,69},{6,70},{7,71},{8,72},{9,... | collective-permute-start | bytes 196616 | tf_op jit(solution)/shard_map/ppermute | solution.py:575

commit v7 on v6

--- a/solution.py
+++ b/solution.py
@@ -14,7 +14,7 @@
 ROWS = 9
 FACE_CHUNK = 2048
 PIECE = 256
-SLOT_STEP = 8
+SLOT_STEP = 32
 
 f32 = jnp.float32
 bf16 = jnp.bfloat16

time: 74.5 us -> 73.1 us (0.981)
  Pallas kernels: 43.6 us -> 42 us
    pallas_call x1, Pallas kernels: 6.2 us -> 5.17 us  [call(): pl.pallas_call(kernel, out_shape=jax.ShapeDtypeStruct((tall + 8, L), f32)...]
  transfers between devices with their start and end apart: 5 -> 5, of which waited for: 4 -> 4; matrix products, arithmetic and copies ran while one was open for 0% -> 0% of each run, Pallas kernels for 29% -> 28%
where the time goes in v7:
time: 73.1 us; the launch traced here: 72.4 us
  Pallas kernels  42 us (57%)
  starting transfers between devices  24.7 us (34%)
  waiting for transfers between devices  3.51 us (5%)
  between operations  1.39 us (2%)
  other arithmetic  0.79 us (1%)
    all_to_all x2, starting transfers between devices, exchange(): lax.all_to_all(x.reshape(-1), 'blk', split_axis=0, concat_axis=0, tiled=T...  19.7 us
    pallas_call x2, Pallas kernels, call(): pl.pallas_call(kernel, in_specs=[pl.BlockSpec(memory_space=pltpu.SMEM), v...  16.5 us
    pallas_call x1, Pallas kernels, call(): pl.pallas_call(kernel, grid=(steps,), in_specs=[pl.BlockSpec((nl, nl), la...  8.02 us
    pallas_call x1, Pallas kernels, call(): pl.pallas_call(kernel, grid=(width // c,), in_specs=[wide, pl.BlockSpec((...  7.43 us
    pallas_call x1, Pallas kernels, call(): pl.pallas_call(kernel, out_shape=jax.ShapeDtypeStruct((tall + 8, L), f32)...  5.17 us
    ppermute x3, starting transfers between devices, across(): return lax.ppermute(x, ('grp', 'blk'), swap)  5.06 us
    pallas_call x1, Pallas kernels, call(): pl.pallas_call(kernel, in_specs=[vmem] * 6, out_shape=[jax.ShapeDtypeStru...  4.84 us
    ppermute x3, waiting for transfers between devices, across(): return lax.ppermute(x, ('grp', 'blk'), swap)  1.8 us
  transfers between devices with their start and end apart: 5, of which 4 were waited for; matrix products, arithmetic and copies ran while one was open for 0% of the time, Pallas kernels for 28%

profile of v7, /device:TPU:1, one launch (start us, length us, event | category | flops | bytes accessed | tf_op | source)
XLA Modules:
  0.0 72.4 jit_solution(15048099278596728695)
XLA Ops:
  0.6 0.0 copy-start.3
  0.6 0.0 copy-start
  1.3 0.0 copy-start.2
  1.3 10.6 %route.1 = (f32[576,128]{1,0:T(8,128)}, s32[1,16384]{1,0:T(1,128)}) custom-call(s32[1]{0:T(128)S(6)} %copy.13.live_ref, s32[1,16384]{1,0:T(1,128)} %bitcast.27, s32[1,16384]{1,0:T(1,128)} %bitcast.28, s32[1,16384]{1,0:T(1,128)} %bitcast.29, f32[1,16384]{1,0:T(1,128)} %bitcast.30, f32[64,16384]{1,0:T(8,128)} %bitcast.23, f32[2,64]{1,0:T(2,128)} %weight_ref.3, ...), custom_call_target="tpu_custom_call" | custom-call | tf_op jit(solution)/shard_map/route/pallas_call | solution.py:207
  12.0 12.0 %all-to-all-start = ((f32[64,1152,1]{1,2,0:T(1,128)}), f32[64,1152,1]{1,2,0:T(1,128)S(1)}, u32[]{:S(2)}, u32[]{:S(2)}) async-start(f32[64,1152,1]{1,2,0:T(1,128)} %bitcast.25), calls=%async_computation | async-start | bytes 589824 | tf_op jit(solution)/shard_map/all_to_all | solution.py:578
  23.9 0.0 copy-done.3
  23.9 0.0 copy-done
  24.0 8.0 %matrices.1 = (f32[64,16384]{1,0:T(8,128)}, f32[656,128]{1,0:T(8,128)S(1)}, f32[64,128]{1,0:T(8,128)S(1)}) custom-call(f32[64,64]{1,0:T(8,128)S(1)} %bitcast.21, f32[2,64]{1,0:T(2,128)S(1)} %copy-done.3, f32[64,16384]{1,0:T(8,128)} %bitcast.24), custom_call_target="tpu_custom_call" | custom-call | tf_op jit(solution)/shard_map/matrices/pallas_call | solution.py:269
  32.0 0.9 %collective-permute-start.1 = (f32[656,128]{1,0:T(8,128)S(1)}, f32[656,128]{1,0:T(8,128)S(1)}, u32[]{:S(2)}, u32[]{:S(2)}) collective-permute-start(f32[656,128]{1,0:T(8,128)S(1)} %get-tuple-element.14.rows_mine), channel_id=1, source_target_pairs={{0,64},{1,65},{2,66},{3,67},{4,68},{5,69},{6,70},{7,71},{8,72},{9,... | collective-permute-start | bytes 1007624 | tf_op jit(solution)/shard_map/ppermute | solution.py:575
  32.9 0.5 all-to-all-done
  33.4 5.2 %gather_sum.1.mine_ref = f32[136,128]{1,0:T(8,128)S(1)} custom-call(f32[576,128]{1,0:T(8,128)S(1)} %bitcast.16), custom_call_target="tpu_custom_call" | custom-call | tf_op jit(solution)/shard_map/gather_sum/pallas_call | solution.py:346
  38.6 2.5 %collective-permute-start = (f32[136,128]{1,0:T(8,128)S(1)}, f32[136,128]{1,0:T(8,128)S(1)}, u32[]{:S(2)}, u32[]{:S(2)}) collective-permute-start(f32[136,128]{1,0:T(8,128)S(1)} %gather_sum.1.mine_ref), channel_id=1, source_target_pairs={{0,64},{1,65},{2,66},{3,67},{4,68},{5,69},{6,70},{7,71},{8,72},{9,... | collective-permute-start | bytes 208904 | tf_op jit(solution)/shard_map/ppermute | solution.py:575
  41.1 0.0 collective-permute-done.1.rows_other
  41.1 0.9 %collective-permute-done.other_ref = f32[136,128]{1,0:T(8,128)S(1)} collective-permute-done((f32[136,128]{1,0:T(8,128)S(1)}, f32[136,128]{1,0:T(8,128)S(1)}, u32[]{:S(2)}, u32[]{:S(2)}) %collective-permute-start) | collective-permute-done | bytes 69664 | tf_op jit(solution)/shard_map/ppermute | solution.py:575
  42.0 0.0 copy-done.2
  42.0 4.8 %surface_lookup.1 = (f32[256,128]{1,0:T(8,128)}, f32[512,128]{1,0:T(8,128)S(1)}, f32[256,128]{1,0:T(8,128)S(1)}) custom-call(f32[136,128]{1,0:T(8,128)S(1)} %gather_sum.1.mine_ref, f32[136,128]{1,0:T(8,128)S(1)} %collective-permute-done.other_ref, f32[656,128]{1,0:T(8,128)S(1)} %get-tuple-element.14.rows_mine, ...), custom_call_target="tpu_custom_call" | custom-call | tf_op jit(solution)/shard_map/surface_lookup/pallas_call | solution.py:441
  46.8 7.7 %all-to-all-start.1 = ((f32[64,512,1]{1,2,0:T(1,128)}), f32[64,512,1]{1,2,0:T(1,128)S(1)}, u32[]{:S(2)}, u32[]{:S(2)}) async-start(f32[64,512,1]{1,2,0:T(1,128)} %bitcast.9), calls=%async_computation.1 | async-start | bytes 262144 | tf_op jit(solution)/shard_map/all_to_all | solution.py:578
  54.6 0.0 copy-start.1
  54.6 7.4 %add_sources.1.y_hbm = f32[64,16384]{1,0:T(8,128)} custom-call(f32[64,16384]{1,0:T(8,128)} %get-tuple-element.17.y_ref, f32[64,128]{1,0:T(8,128)S(1)} %get-tuple-element.18.coef_ref, f32[4,128,128]{2,1,0:T(8,128)S(1)} %bitcast.19), custom_call_target="tpu_custom_call" | custom-call | tf_op jit(solution)/shard_map/add_sources/pallas_call | solution.py:481
  62.0 1.2 %all-to-all-done.1 = f32[64,512,1]{1,2,0:T(1,128)S(1)} async-done(((f32[64,512,1]{1,2,0:T(1,128)}), f32[64,512,1]{1,2,0:T(1,128)S(1)}, u32[]{:S(2)}, u32[]{:S(2)}) %all-to-all-start.1) | async-done | bytes 131104 | tf_op jit(solution)/shard_map/all_to_all | solution.py:578
  63.2 5.9 %face_finish.1 = (f32[64,16384]{1,0:T(8,128)}, f32[1,16384]{1,0:T(1,128)S(1)}, f32[2,16384]{1,0:T(2,128)S(1)}) custom-call(s32[1]{0:T(128)S(6)} %copy.13.live_ref, f32[256,128]{1,0:T(8,128)S(1)} %bitcast.18, s32[1,16384]{1,0:T(1,128)S(1)} %copy-done.1, f32[64,16384]{1,0:T(8,128)} %add_sources.1.y_hbm, f32[64,128]{1,0:T(8,128)S(1)} %get-tuple-element.18.coef_ref, ...), custom_call_target="tpu_custom_call" | custom-call | tf_op jit(solution)/shard_map/face_finish/pallas_call | solution.py:544
  69.1 1.7 %collective-permute-start.2 = (f32[1,16384]{1,0:T(1,128)S(1)}, f32[1,16384]{1,0:T(1,128)S(1)}, u32[]{:S(2)}, u32[]{:S(2)}) collective-permute-start(f32[1,16384]{1,0:T(1,128)S(1)} %get-tuple-element.22), channel_id=1, source_target_pairs={{0,64},{1,65},{2,66},{3,67},{4,68},{5,69},{6,70},{7,71},{8,72},{9,... | collective-permute-start | bytes 196616 | tf_op jit(solution)/shard_map/ppermute | solution.py:575
  70.7 0.9 %collective-permute-done.2 = f32[1,16384]{1,0:T(1,128)S(1)} collective-permute-done((f32[1,16384]{1,0:T(1,128)S(1)}, f32[1,16384]{1,0:T(1,128)S(1)}, u32[]{:S(2)}, u32[]{:S(2)}) %collective-permute-start.2) | collective-permute-done | bytes 65568 | tf_op jit(solution)/shard_map/ppermute | solution.py:575
  71.6 0.8 %select_bitcast_fusion = f32[1,2,16384]{2,1,0:T(2,128)} fusion(f32[2,16384]{1,0:T(2,128)S(1)} %get-tuple-element.23, pred[2]{0:T(512)(128)(4,1)S(1)} %compare_and_fusion, f32[16384]{0:T(1024)S(1)} %bitcast.26), kind=kLoop, calls=%fused_computation | loop fusion | flops 32768 | bytes 327682 | tf_op jit(solution)/shard_map/broadcast_in_dim | solution.py:594
  (2 shorter events, 0.0 us)
Async XLA Ops:
  0.6 23.3 %copy-start.3 = (f32[2,64]{1,0:T(2,128)S(1)}, f32[2,64]{1,0:T(2,128)}, u32[]{:S(2)}) copy-start(f32[2,64]{1,0:T(2,128)} %weight_ref.3) | copy-start | bytes 1540
  0.6 23.3 %copy-start = (f32[1,64,64]{2,1,0:T(8,128)S(1)}, f32[1,64,64]{2,1,0:T(8,128)}, u32[]{:S(2)}) copy-start(f32[1,64,64]{2,1,0:T(8,128)} %param.10) | copy-start | bytes 49156
  1.3 40.7 %copy-start.2 = (f32[16384]{0:T(1024)S(1)}, f32[16384]{0:T(1024)}, u32[]{:S(2)}) copy-start(f32[16384]{0:T(1024)} %param.17) | copy-start | bytes 196612
  12.0 21.5 %all-to-all-start = ((f32[64,1152,1]{1,2,0:T(1,128)}), f32[64,1152,1]{1,2,0:T(1,128)S(1)}, u32[]{:S(2)}, u32[]{:S(2)}) async-start(f32[64,1152,1]{1,2,0:T(1,128)} %bitcast.25), calls=%async_computation | async-start | bytes 589824 | tf_op jit(solution)/shard_map/all_to_all | solution.py:578
  32.0 9.1 %collective-permute-start.1 = (f32[656,128]{1,0:T(8,128)S(1)}, f32[656,128]{1,0:T(8,128)S(1)}, u32[]{:S(2)}, u32[]{:S(2)}) collective-permute-start(f32[656,128]{1,0:T(8,128)S(1)} %get-tuple-element.14.rows_mine), channel_id=1, source_target_pairs={{0,64},{1,65},{2,66},{3,67},{4,68},{5,69},{6,70},{7,71},{8,72},{9,... | collective-permute-start | bytes 1007624 | tf_op jit(solution)/shard_map/ppermute | solution.py:575
  38.6 3.4 %collective-permute-start = (f32[136,128]{1,0:T(8,128)S(1)}, f32[136,128]{1,0:T(8,128)S(1)}, u32[]{:S(2)}, u32[]{:S(2)}) collective-permute-start(f32[136,128]{1,0:T(8,128)S(1)} %gather_sum.1.mine_ref), channel_id=1, source_target_pairs={{0,64},{1,65},{2,66},{3,67},{4,68},{5,69},{6,70},{7,71},{8,72},{9,... | collective-permute-start | bytes 208904 | tf_op jit(solution)/shard_map/ppermute | solution.py:575
  46.8 16.4 %all-to-all-start.1 = ((f32[64,512,1]{1,2,0:T(1,128)}), f32[64,512,1]{1,2,0:T(1,128)S(1)}, u32[]{:S(2)}, u32[]{:S(2)}) async-start(f32[64,512,1]{1,2,0:T(1,128)} %bitcast.9), calls=%async_computation.1 | async-start | bytes 262144 | tf_op jit(solution)/shard_map/all_to_all | solution.py:578
  54.6 8.6 %copy-start.1 = (s32[1,16384]{1,0:T(1,128)S(1)}, s32[1,16384]{1,0:T(1,128)}, u32[]{:S(2)}) copy-start(s32[1,16384]{1,0:T(1,128)} %get-tuple-element.16.slot_ref) | copy-start | bytes 196612
  69.1 2.6 %collective-permute-start.2 = (f32[1,16384]{1,0:T(1,128)S(1)}, f32[1,16384]{1,0:T(1,128)S(1)}, u32[]{:S(2)}, u32[]{:S(2)}) collective-permute-start(f32[1,16384]{1,0:T(1,128)S(1)} %get-tuple-element.22), channel_id=1, source_target_pairs={{0,64},{1,65},{2,66},{3,67},{4,68},{5,69},{6,70},{7,71},{8,72},{9,... | collective-permute-start | bytes 196616 | tf_op jit(solution)/shard_map/ppermute | solution.py:575
